TPU v7x, 32 devices: a whole 2x2x4 slice. The times are simulated.
32 devices in a mesh: dp: 16 (over z, x, core), tensor: 2 (over y).
Axes of the slice: x: 2, y: 2, z: 4, core: 2. Of those that a mesh axis runs over, the one named last changes fastest.
Arguments:
- tokens: bfloat16 [32768, 768], P(('dp', 'tensor')), may hold values from -6 to 6
- timesteps: int32 [32], replicated, may hold values from 0 to 999
- norm_gains: bfloat16 [2, 768], P(None, ('dp', 'tensor')), may hold values from 0.5 to 1.5
- biases: bfloat16 [5, 768], P(None, ('dp', 'tensor')), may hold values from -2 to 2
- second_shift: bfloat16 [768], P(('dp', 'tensor')), may hold values from -2 to 2
- hidden_bias: bfloat16 [3072], P(('dp', 'tensor')), may hold values from -3 to 3
- step_table: bfloat16 [1000, 768], P(None, ('dp', 'tensor')), may hold values from -3 to 3
- qkv_weight: bfloat16 [3, 768, 768], P(None, 'dp', 'tensor'), may hold values from -0.21875 to 0.21875
- out_weight: bfloat16 [768, 768], P('tensor', 'dp'), may hold values from -2 to 2
- up_weight: bfloat16 [768, 3072], P('dp', 'tensor'), may hold values from -0.21875 to 0.21875
- down_weight: bfloat16 [3072, 768], P('tensor', 'dp'), may hold values from -0.109375 to 0.109375
- cotangent: bfloat16 [32768, 768], P(('dp', 'tensor')), may hold values from -6 to 6
Outputs:
- layer_out: bfloat16 [32768, 768], P(('dp', 'tensor'))
- grad_tokens: float32 [32768, 768], P(('dp', 'tensor'))
- grad_gains: float32 [2, 768], P(None, ('dp', 'tensor'))
- grad_biases: float32 [5, 768], P(None, ('dp', 'tensor'))
- grad_second_shift: float32 [768], P(('dp', 'tensor'))
- grad_hidden: float32 [3072], P(('dp', 'tensor'))
- grad_table: float32 [1000, 768], P(None, ('dp', 'tensor'))
- grad_qkv: float32 [3, 768, 768], P(None, 'dp', 'tensor')
- grad_out: float32 [768, 768], P('tensor', 'dp')
- grad_up: float32 [768, 3072], P('dp', 'tensor')
- grad_down: float32 [3072, 768], P('tensor', 'dp')
All inputs are finite; a program needn't handle non-finite values.
Results may differ from a plain program's by a relative error of at most 0.014.
Values may be sent and summed in bfloat16 or wider, within the bound.
A program may use at most 192 MiB of HBM per device.

v0:
```python
import jax
import jax.numpy as jnp
from jax import lax
from jax.sharding import PartitionSpec as P

HEAD_DIM = 64
TSTEPS = 1000
LEN = 1024
BLOCK = 256
QBLK = 512


EPS = 1e-05
NEGATIVE = -1e30
HIGH = lax.Precision.HIGHEST


def layer_norm(hidden, gain, shift):
    average = jnp.mean(hidden, axis=-1, keepdims=True)
    centered = hidden - average
    variance = jnp.mean(centered * centered, axis=-1, keepdims=True)
    return centered * lax.rsqrt(variance + EPS) * gain + shift


def gather_rows(values):
    return lax.all_gather(values, "tensor", axis=0, tiled=True)


def sum_rows(values):
    return lax.psum_scatter(
        values.astype(jnp.bfloat16), "tensor", scatter_dimension=0, tiled=True
    ).astype(jnp.float32)


def fetch_attn(qkv_weight, out_weight):
    return (
        lax.all_gather(qkv_weight, "dp", axis=1, tiled=True),
        lax.all_gather(out_weight, "dp", axis=1, tiled=True),
    )


def fetch_mlp(up_weight, down_weight):
    return (
        lax.all_gather(up_weight, "dp", axis=0, tiled=True),
        lax.all_gather(down_weight, "dp", axis=1, tiled=True),
    )


def place_part(part, whole_len, offset):
    return lax.dynamic_update_slice_in_dim(jnp.zeros((whole_len,), jnp.float32), part, offset, 0)


def contract_rows(left, right):
    return lax.dot_general(
        left, right, (((0,), (0,)), ((), ())), preferred_element_type=jnp.float32
    )


def contract_cols(left, right):
    return lax.dot_general(
        left, right, (((1,), (1,)), ((), ())), preferred_element_type=jnp.float32
    )


def block_mask(start):
    query_pos = start + jnp.arange(QBLK)
    key_pos = jnp.arange(LEN)
    return query_pos[:, None] // BLOCK >= key_pos[None, :] // BLOCK


def split_heads(values):
    return values.reshape(values.shape[0], values.shape[1] // HEAD_DIM, HEAD_DIM)


def masked_scores(query_heads, key_heads, start, scale):
    scores = (
        jnp.einsum("qhd,khd->hqk", query_heads, key_heads, preferred_element_type=jnp.float32)
        * scale
    )
    return jnp.where(block_mask(start)[None], scores, NEGATIVE)


def block_slices(queries, keys_all, values_all, index):
    per_seq = LEN // QBLK
    seq_start = index // per_seq * LEN
    start = index % per_seq * QBLK
    query_blk = lax.dynamic_slice_in_dim(queries, seq_start + start, QBLK, 0)
    key_seq = lax.dynamic_slice_in_dim(keys_all, seq_start, LEN, 0)
    value_seq = lax.dynamic_slice_in_dim(values_all, seq_start, LEN, 0)
    return (seq_start, start, query_blk, key_seq, value_seq)


def run_attention(queries, keys_all, values_all, scale):
    total_rows = queries.shape[0]

    def run_advance(carry, index):
        seq_start, start, query_blk, key_seq, value_seq = block_slices(
            queries, keys_all, values_all, index
        )
        scores = masked_scores(split_heads(query_blk), split_heads(key_seq), start, scale)
        largest = jnp.max(scores, axis=-1, keepdims=True)
        expo = jnp.exp(scores - largest)
        totals = jnp.sum(expo, axis=-1, keepdims=True)
        chances = (expo / totals).astype(jnp.bfloat16)
        log_total = (largest + jnp.log(totals))[..., 0]
        mixed = jnp.einsum(
            "hqk,khd->qhd", chances, split_heads(value_seq), preferred_element_type=jnp.float32
        )
        return (carry, (mixed.reshape(QBLK, -1).astype(jnp.bfloat16), log_total))

    unused, (mixed, log_total) = lax.scan(run_advance, 0, jnp.arange(total_rows // QBLK))
    return (mixed.reshape(total_rows, -1), log_total)


def attention_back(queries, keys_all, values_all, grad_mixed, log_total, scale):
    total_rows = queries.shape[0]
    zeros = jnp.zeros(queries.shape, jnp.float32)

    def attention_advance(carry, inputs):
        grad_keys, grad_values = carry
        index, log_blk = inputs
        seq_start, start, query_blk, key_seq, value_seq = block_slices(
            queries, keys_all, values_all, index
        )
        grad_blk = lax.dynamic_slice_in_dim(grad_mixed, seq_start + start, QBLK, 0)
        query_heads = split_heads(query_blk)
        key_heads = split_heads(key_seq)
        grad_heads = split_heads(grad_blk)
        scores = masked_scores(query_heads, key_heads, start, scale)
        chances = jnp.exp(scores - log_blk[..., None])
        grad_probs = jnp.einsum(
            "qhd,khd->hqk", grad_heads, split_heads(value_seq), preferred_element_type=jnp.float32
        )
        inner = jnp.sum(chances * grad_probs, axis=-1, keepdims=True)
        grad_scores = (chances * (grad_probs - inner)).astype(jnp.bfloat16)
        grad_query = (
            jnp.einsum("hqk,khd->qhd", grad_scores, key_heads, preferred_element_type=jnp.float32)
            * scale
        )
        grad_key = (
            jnp.einsum("hqk,qhd->khd", grad_scores, query_heads, preferred_element_type=jnp.float32)
            * scale
        )
        grad_value = jnp.einsum(
            "hqk,qhd->khd",
            chances.astype(jnp.bfloat16),
            grad_heads,
            preferred_element_type=jnp.float32,
        )
        old_keys = lax.dynamic_slice_in_dim(grad_keys, seq_start, LEN, 0)
        old_values = lax.dynamic_slice_in_dim(grad_values, seq_start, LEN, 0)
        grad_keys = lax.dynamic_update_slice_in_dim(
            grad_keys, old_keys + grad_key.reshape(LEN, -1), seq_start, 0
        )
        grad_values = lax.dynamic_update_slice_in_dim(
            grad_values, old_values + grad_value.reshape(LEN, -1), seq_start, 0
        )
        return ((grad_keys, grad_values), grad_query.reshape(QBLK, -1))

    (grad_keys, grad_values), grad_queries = lax.scan(
        attention_advance, (zeros, zeros), (jnp.arange(total_rows // QBLK), log_total)
    )
    return (grad_queries.reshape(total_rows, -1), grad_keys, grad_values)


def shards(
    tokens,
    timesteps,
    norm_gains,
    biases,
    second_shift,
    hidden_bias,
    step_table,
    qkv_weight,
    out_weight,
    up_weight,
    down_weight,
    cotangent,
):
    width = tokens.shape[1]
    half_width = qkv_weight.shape[2]
    half_hidden = up_weight.shape[1]
    slot = lax.axis_index("tensor")
    device = lax.axis_index(("dp", "tensor"))
    scale = HEAD_DIM ** (-0.5)
    gains_all, biases_all, second_all, hidden_all, table_all = (
        lax.all_gather(norm_gains, ("dp", "tensor"), axis=1, tiled=True),
        lax.all_gather(biases, ("dp", "tensor"), axis=1, tiled=True),
        lax.all_gather(second_shift, ("dp", "tensor"), axis=0, tiled=True),
        lax.all_gather(hidden_bias, ("dp", "tensor"), axis=0, tiled=True),
        lax.all_gather(step_table, ("dp", "tensor"), axis=1, tiled=True),
    )
    gains_all = gains_all.astype(jnp.float32)
    biases_all = biases_all.astype(jnp.float32)
    second_all = second_all.astype(jnp.float32)
    hidden_local = lax.dynamic_slice_in_dim(
        hidden_all.astype(jnp.float32), slot * half_hidden, half_hidden, 0
    )
    query_bias = lax.dynamic_slice_in_dim(biases_all[1], slot * half_width, half_width, 0)
    value_bias = lax.dynamic_slice_in_dim(biases_all[2], slot * half_width, half_width, 0)
    step_id = lax.dynamic_slice_in_dim(timesteps, device, 1, 0)
    picker = (step_id[:, None] == jnp.arange(TSTEPS)[None, :]).astype(jnp.bfloat16)
    embed = jnp.dot(picker, table_all, preferred_element_type=jnp.float32)
    start_h = tokens.astype(jnp.float32) + embed
    qkv_full, out_full = fetch_attn(qkv_weight, out_weight)
    up_full, down_full = fetch_mlp(up_weight, down_weight)
    normed = gather_rows(layer_norm(start_h, gains_all[0], biases_all[0]).astype(jnp.bfloat16))
    projected = jnp.einsum("rd,jde->jre", normed, qkv_full, preferred_element_type=jnp.float32)
    queries = (projected[0] + query_bias).astype(jnp.bfloat16)
    keys_all = projected[1].astype(jnp.bfloat16)
    values_all = (projected[2] + value_bias).astype(jnp.bfloat16)
    mixed, log_total = run_attention(queries, keys_all, values_all, scale)
    attn_out = (
        sum_rows(jnp.dot(mixed, out_full, preferred_element_type=jnp.float32)) + biases_all[3]
    )
    middle = start_h + attn_out
    second = gather_rows(layer_norm(middle, gains_all[1], second_all).astype(jnp.bfloat16))
    pre_act = jnp.dot(second, up_full, preferred_element_type=jnp.float32) + hidden_local
    activated = jax.nn.gelu(pre_act).astype(jnp.bfloat16)
    mlp_out = (
        sum_rows(jnp.dot(activated, down_full, preferred_element_type=jnp.float32)) + biases_all[4]
    )
    layer_out = (middle + mlp_out).astype(jnp.bfloat16)
    grad_top = cotangent.astype(jnp.float32)
    up_full, down_full = fetch_mlp(up_weight, down_weight)
    grad_mlp_all = gather_rows(cotangent)
    grad_downw = contract_rows(activated, grad_mlp_all)
    grad_act = contract_cols(grad_mlp_all, down_full)
    unused, gelu_back = jax.vjp(jax.nn.gelu, pre_act)
    grad_pre = gelu_back(grad_act)[0].astype(jnp.bfloat16)
    grad_upw = contract_rows(second, grad_pre)
    grad_hidden_local = jnp.sum(grad_pre.astype(jnp.float32), axis=0)
    grad_second = sum_rows(contract_cols(grad_pre, up_full))
    unused, second_back = jax.vjp(layer_norm, middle, gains_all[1], second_all)
    grad_mid_part, grad_gain_two, grad_shift_two = second_back(grad_second)
    grad_middle = grad_top + grad_mid_part
    grad_up, grad_down = (
        lax.psum_scatter(grad_upw, "dp", scatter_dimension=0, tiled=True),
        lax.psum_scatter(grad_downw, "dp", scatter_dimension=1, tiled=True),
    )
    qkv_full, out_full = fetch_attn(qkv_weight, out_weight)
    grad_attn = grad_middle.astype(jnp.bfloat16)
    grad_attn_all = gather_rows(grad_attn)
    grad_outw = contract_rows(mixed, grad_attn_all)
    grad_mixed = contract_cols(grad_attn_all, out_full).astype(jnp.bfloat16)
    grad_queries, grad_keys, grad_values = attention_back(
        queries, keys_all, values_all, grad_mixed, log_total, scale
    )
    grad_rows = jnp.stack([grad_queries, grad_keys, grad_values]).astype(jnp.bfloat16)
    grad_qkvw = jnp.einsum("rd,jre->jde", normed, grad_rows, preferred_element_type=jnp.float32)
    grad_normed = sum_rows(
        jnp.einsum("jre,jde->rd", grad_rows, qkv_full, preferred_element_type=jnp.float32)
    )
    unused, first_back = jax.vjp(layer_norm, start_h, gains_all[0], biases_all[0])
    grad_start_part, grad_gain_one, grad_shift_one = first_back(grad_normed)
    grad_tokens = grad_middle + grad_start_part
    grad_qkv, grad_out = (
        lax.psum_scatter(grad_qkvw, "dp", scatter_dimension=1, tiled=True),
        lax.psum_scatter(grad_outw, "dp", scatter_dimension=1, tiled=True),
    )
    row_sums = jnp.sum(grad_rows.astype(jnp.float32), axis=1)
    gain_terms = jnp.stack([grad_gain_one, grad_gain_two])
    bias_terms = jnp.stack(
        [
            grad_shift_one,
            place_part(row_sums[0], width, slot * half_width),
            place_part(row_sums[2], width, slot * half_width),
            jnp.sum(grad_attn.astype(jnp.float32), axis=0),
            jnp.sum(grad_top, axis=0),
        ]
    )
    hidden_terms = place_part(
        grad_hidden_local,
        hidden_bias.shape[0] * lax.axis_size(("dp", "tensor")),
        slot * half_hidden,
    )
    seq_grad = jnp.sum(grad_tokens, axis=0, keepdims=True)
    table_terms = lax.dot_general(
        picker.astype(jnp.float32),
        seq_grad,
        (((0,), (0,)), ((), ())),
        precision=HIGH,
        preferred_element_type=jnp.float32,
    )
    grad_gains, grad_biases, grad_shift, grad_hidden, grad_table = (
        lax.psum_scatter(gain_terms, ("dp", "tensor"), scatter_dimension=1, tiled=True),
        lax.psum_scatter(bias_terms, ("dp", "tensor"), scatter_dimension=1, tiled=True),
        lax.psum_scatter(grad_shift_two, ("dp", "tensor"), scatter_dimension=0, tiled=True),
        lax.psum_scatter(hidden_terms, ("dp", "tensor"), scatter_dimension=0, tiled=True),
        lax.psum_scatter(table_terms, ("dp", "tensor"), scatter_dimension=1, tiled=True),
    )
    return (
        layer_out,
        grad_tokens,
        grad_gains,
        grad_biases,
        grad_shift,
        grad_hidden,
        grad_table,
        grad_qkv,
        grad_out,
        grad_up,
        grad_down,
    )


def solution(mesh):
    in_specs = (
        P(("dp", "tensor"), None),
        P(),
        P(None, ("dp", "tensor")),
        P(None, ("dp", "tensor")),
        P(("dp", "tensor")),
        P(("dp", "tensor")),
        P(None, ("dp", "tensor")),
        P(None, "dp", "tensor"),
        P("tensor", "dp"),
        P("dp", "tensor"),
        P("tensor", "dp"),
        P(("dp", "tensor"), None),
    )
    out_specs = (
        P(("dp", "tensor"), None),
        P(("dp", "tensor"), None),
        P(None, ("dp", "tensor")),
        P(None, ("dp", "tensor")),
        P(("dp", "tensor")),
        P(("dp", "tensor")),
        P(None, ("dp", "tensor")),
        P(None, "dp", "tensor"),
        P("tensor", "dp"),
        P("dp", "tensor"),
        P("tensor", "dp"),
    )
    return jax.shard_map(shards, mesh=mesh, in_specs=in_specs, out_specs=out_specs, check_vma=False)
```

profile of v0, /device:TPU:0, one launch (start us, length us, event | category | flops | bytes accessed | tf_op | source)
XLA Modules:
  0.0 1429.5 jit_solution(11528582043966617550)
XLA Ops:
  10.6 69.5 %all-gather = bf16[32,24,2]{1,2,0:T(2,128)(2,1)S(1)} all-gather(bf16[1,24,2]{1,2,0:T(2,128)(2,1)} %bitcast.184), channel_id=1, replica_groups=mesh['dp'=16,'tensor'=2] {'dp','tensor'}, dimensions={0}, use_global_device_ids=true | all-gather | bytes 3168 | tf_op jit(solution)/shard_map/all_gather | solution.py:187
  80.4 64.1 %all-gather.1 = bf16[32,24,5]{1,2,0:T(8,128)(2,1)S(1)} all-gather(bf16[1,24,5]{1,2,0:T(8,128)(2,1)} %bitcast.183), channel_id=1, replica_groups=mesh['dp'=16,'tensor'=2] {'dp','tensor'}, dimensions={0}, use_global_device_ids=true | all-gather | bytes 7920 | tf_op jit(solution)/shard_map/all_gather | solution.py:188
  152.2 20.4 %all_gather.48 = bf16[384,768]{0,1:T(8,128)(2,1)} all-gather(bf16[384,48]{0,1:T(8,128)(2,1)S(1)} %copy-done.40), channel_id=1, replica_groups=mesh['dp'=16,'tensor'=2] {'dp'}, dimensions={1}, use_global_device_ids=true | all-gather | bytes 626688 | tf_op jit(solution)/shard_map/all_gather | solution.py:38
  172.6 22.6 %all-gather.13.cloned.1.call-done = bf16[2048,768]{1,0:T(8,128)(2,1)} async-done(((bf16[1024,768]{1,0:T(8,128)(2,1)}), bf16[2048,768]{1,0:T(8,128)(2,1)}) %all-gather.13.cloned.1.call-update) | async-done | bytes 3145744 | tf_op jit(solution)/shard_map/all_gather | solution.py:26
  214.3 67.5 %while.32 = (s32[]{:T(128)}, bf16[4,512,384]{2,1,0:T(8,128)(2,1)S(1)}, f32[4,6,512]{2,1,0:T(8,128)S(1)}, s32[4]{0:T(128)S(1)}, bf16[2048,384]{0,1:T(8,128)(2,1)}...) while((s32[]{:T(128)}, ...), condition=%wide.region_5.6_spmd, body=%wide.region_2.5_spmd.sunk | while | flops 843789312 | bytes 47833552 | solution.py:111
  286.5 39.9 %all-reduce.8 = (bf16[768]{0:T(1024)(128)(2,1)S(1)}, bf16[3072]{0:T(1024)(128)(2,1)S(1)}) all-reduce(bf16[768]{0:T(1024)(128)(2,1)S(1)} %dynamic-update-slice, bf16[3072]{0:T(1024)(128)(2,1)S(1)} %dynamic-update-slice.1), channel_id=1, replica_groups=mesh['dp'=16,'tensor'=2] {'dp','tensor'}, use_global_device_ids=true, to_apply=%add | all-reduce | flops 3840 | bytes 15360
  337.1 37.5 %all-gather.19.cloned.1.call-done = bf16[768,1536]{1,0:T(8,128)(2,1)} async-done(((bf16[48,1536]{1,0:T(8,128)(2,1)}), bf16[768,1536]{1,0:T(8,128)(2,1)}) %all-gather.19.cloned.1.call-update) | async-done | bytes 2359312 | tf_op jit(solution)/shard_map/all_gather | solution.py:44
  374.6 45.8 %all-gather.17.cloned.1.call-done = bf16[2048,768]{1,0:T(8,128)(2,1)} async-done(((bf16[1024,768]{1,0:T(8,128)(2,1)}), bf16[2048,768]{1,0:T(8,128)(2,1)}) %all-gather.17.cloned.1.call-update) | async-done | bytes 3145744 | tf_op jit(solution)/shard_map/all_gather | solution.py:26
  420.4 14.1 multiply_convert_fusion.1
  434.5 32.5 %all-gather.23.cloned.1.call-done = bf16[2048,768]{1,0:T(8,128)(2,1)} async-done(((bf16[1024,768]{1,0:T(8,128)(2,1)}), bf16[2048,768]{1,0:T(8,128)(2,1)}) %all-gather.23.cloned.1.call-update) | async-done | bytes 3145744 | tf_op jit(solution)/shard_map/all_gather | solution.py:26
  467.0 44.9 %all-gather.21.cloned.1.call-done = bf16[1536,768]{0,1:T(8,128)(2,1)} async-done(((bf16[1536,48]{0,1:T(8,128)(2,1)}), bf16[1536,768]{0,1:T(8,128)(2,1)}) %all-gather.21.cloned.1.call-update) | async-done | bytes 2359312 | tf_op jit(solution)/shard_map/all_gather | solution.py:45
  511.9 17.3 %convert_reduce_fusion = (f32[1536]{0:T(1024)}, bf16[2048,1536]{1,0:T(8,128)(2,1)S(1)}) fusion(f32[2048,1536]{1,0:T(8,128)} %get-tuple-element.493, f32[1536]{0:T(1024)S(1)} %dynamic-slice_convert_fusion, bf16[2048,768]{1,0:T(8,128)(2,1)} %all-gather.23.cloned.1.call-done, bf16[1536,768]{0,1:T(8,128)(2,1)} %all-gather.21.cloned.1.call-done), kind=kOutput, calls=%fused_computation.79 | convolution fusion | flops 4904188416 | bytes 24391680 | tf_op jit(solution)/shard_map/dot_general | solution.py:60
  538.5 9.2 convolution_convert_fusion.2
  547.8 32.9 %reduce-scatter.15.cloned.1.call-done = bf16[1024,768]{1,0:T(8,128)(2,1)} async-done(((bf16[2048,768]{1,0:T(8,128)(2,1)}), bf16[1024,768]{1,0:T(8,128)(2,1)}) %reduce-scatter.15.cloned.1.call-update) | async-done | bytes 1572880 | tf_op jit(solution)/shard_map/reduce_scatter | solution.py:30
  584.5 41.7 %reduce-scatter.13.cloned.1.call-done = bf16[1024,768]{1,0:T(8,128)(2,1)} async-done(((bf16[2048,768]{1,0:T(8,128)(2,1)}), bf16[1024,768]{1,0:T(8,128)(2,1)}) %reduce-scatter.13.cloned.1.call-update) | async-done | bytes 1572880 | tf_op jit(solution)/shard_map/reduce_scatter | solution.py:30
  633.1 45.0 %all-gather.25.cloned.1.call-done = bf16[2048,768]{1,0:T(8,128)(2,1)} async-done(((bf16[1024,768]{1,0:T(8,128)(2,1)}), bf16[2048,768]{1,0:T(8,128)(2,1)}) %all-gather.25.cloned.1.call-update) | async-done | bytes 3145744 | tf_op jit(solution)/shard_map/all_gather | solution.py:26
  686.6 232.3 %while.33 = (s32[]{:T(128)}, f32[2048,384]{1,0:T(8,128)}, f32[2048,384]{1,0:T(8,128)}, bf16[4,512,384]{1,2,0:T(8,128)(2,1)}, s32[4]{0:T(128)S(1)}, /*index=5*/bf...) while((s32[]{:T(128)}, f32[2048,384]{1,0:T(8,128)}, ...), condition=%wide.region_15.16_spmd, body=%wide.region_13.15_spmd.sunk | while | flops 2062562304 | bytes 266044048 | solution.py:160
  712.7 11.6 multiply_reduce_fusion.4
  725.6 6.9 multiply_convert_fusion.3
  770.7 11.6 multiply_reduce_fusion.4
  783.6 6.9 multiply_convert_fusion.3
  828.7 11.6 multiply_reduce_fusion.4
  886.7 11.6 multiply_reduce_fusion.4
  932.7 8.1 fusion.49
  948.9 9.7 fusion.65
  960.4 9.5 fusion.66
  991.4 104.0 %all-reduce.11.cloned.1.call-done = f32[3,768,384]{2,0,1:T(4,128)} async-done(((f32[3,768,384]{2,0,1:T(4,128)}), f32[3,768,384]{2,0,1:T(4,128)}) %all-reduce.11.cloned.1.call-update) | async-done | bytes 3538960
  1097.3 40.8 %all-reduce.7 = (f32[2,768]{1,0:T(2,128)S(1)}, f32[5,768]{1,0:T(8,128)S(1)}, f32[768]{0:T(1024)S(1)}, f32[3072]{0:T(1024)S(1)}) all-reduce(f32[2,768]{1,0:T(2,128)S(1)} %pad_maximum_fusion.1, f32[5,768]{1,0:T(8,128)S(1)} %stack.38, f32[768]{0:T(1024)S(1)} %copy-done.41, ...), channel_id=6, replica_groups=mesh['dp'=16,'tensor'=2] {'dp','tensor'}, use_global_device_ids=true, to_apply=%region_21.22.clone | all-reduce | flops 9216 | bytes 73728
  1140.6 35.2 %reduce-scatter.23.cloned.1.call-done = f32[48,1536]{1,0:T(8,128)} async-done(((f32[768,1536]{1,0:T(8,128)}), f32[48,1536]{1,0:T(8,128)}) %reduce-scatter.23.cloned.1.call-update) | async-done | bytes 294928 | tf_op jit(solution)/shard_map/reduce_scatter | solution.py:238
  1175.8 79.4 %reduce-scatter.25.cloned.1.call-done = f32[1536,48]{0,1:T(8,128)} async-done(((f32[1536,768]{0,1:T(8,128)}), f32[1536,48]{0,1:T(8,128)}) %reduce-scatter.25.cloned.1.call-update) | async-done | bytes 294928 | tf_op jit(solution)/shard_map/reduce_scatter | solution.py:239
  1255.2 61.2 %reduce-scatter.21.cloned.1.call-done = f32[384,48]{0,1:T(8,128)} async-done(((f32[384,768]{0,1:T(8,128)}), f32[384,48]{0,1:T(8,128)}) %reduce-scatter.21.cloned.1.call-update) | async-done | bytes 73744 | tf_op jit(solution)/shard_map/reduce_scatter | solution.py:259
  1316.4 106.3 %reduce-scatter.19.cloned.1.call-done = f32[1000,24]{0,1:T(8,128)} async-done(((f32[1000,768]{0,1:T(8,128)}), f32[1000,24]{0,1:T(8,128)}) %reduce-scatter.19.cloned.1.call-update) | async-done | bytes 96016 | tf_op jit(solution)/shard_map/reduce_scatter | solution.py:290
  (412 shorter events, 339.7 us)
Async XLA Ops:
  7.2 140.8 %copy-start.2 = (bf16[1024,768]{1,0:T(8,128)(2,1)S(1)}, bf16[1024,768]{1,0:T(8,128)(2,1)}, u32[]{:S(2)}) copy-start(bf16[1024,768]{1,0:T(8,128)(2,1)} %param.16) | copy-start | bytes 4718596
  7.2 138.8 %all-gather.11.cloned.1.call-start = ((), (), s32[]{:S(2)}) async-start(), calls=%async_computation.8 | async-start | bytes 1622016 | tf_op jit(solution)/shard_map/all_gather | solution.py:191
  7.9 164.7 %all-gather.15.cloned.1.call-start = ((), (), s32[]{:S(2)}) async-start(), calls=%async_computation.10 | async-start | bytes 1880064 | tf_op jit(solution)/shard_map/all_gather | solution.py:37
  8.7 186.5 %all-gather.13.cloned.1.call-start = ((), (), s32[]{:S(2)}) async-start(), calls=%async_computation.9 | async-start | bytes 4718592 | tf_op jit(solution)/shard_map/all_gather | solution.py:26
  145.4 6.7 copy-start.31
  152.1 178.0 %reduce-scatter.11.cloned.1.call-start = ((), (), s32[]{:S(2)}) async-start(), calls=%async_computation.11 | async-start | bytes 4718592 | tf_op jit(solution)/shard_map/reduce_scatter | solution.py:30
  214.3 67.5 %copy-start.26 = (bf16[384,768]{0,1:T(8,128)(2,1)S(1)}, bf16[384,768]{0,1:T(8,128)(2,1)}, u32[]{:S(2)}) copy-start(bf16[384,768]{0,1:T(8,128)(2,1)} %all_gather.48) | copy-start | bytes 1769476
  285.3 44.8 %copy-start.3 = (bf16[1024,768]{1,0:T(8,128)(2,1)S(1)}, bf16[1024,768]{1,0:T(8,128)(2,1)}, u32[]{:S(2)}) copy-start(bf16[1024,768]{1,0:T(8,128)(2,1)} %param.16) | copy-start | bytes 4718596
  285.3 44.8 %copy-start.24 = (f32[768]{0:T(1024)S(1)}, f32[768]{0:T(1024)}, u32[]{:S(2)}) copy-start(f32[768]{0:T(1024)} %copy-done.23) | copy-start | bytes 9220
  285.3 44.8 %copy-start.30 = (f32[768]{0:T(1024)S(1)}, f32[768]{0:T(1024)}, u32[]{:S(2)}) copy-start(f32[768]{0:T(1024)} %get-tuple-element.490) | copy-start | bytes 9220
  285.3 89.3 %all-gather.19.cloned.1.call-start = ((), (), s32[]{:S(2)}) async-start(), calls=%async_computation.13 | async-start | bytes 2506752 | tf_op jit(solution)/shard_map/all_gather | solution.py:44
  285.9 134.5 %all-gather.17.cloned.1.call-start = ((), (), s32[]{:S(2)}) async-start(), calls=%async_computation.12 | async-start | bytes 4718592 | tf_op jit(solution)/shard_map/all_gather | solution.py:26
  335.5 131.5 %all-gather.23.cloned.1.call-start = ((), (), s32[]{:S(2)}) async-start(), calls=%async_computation.16 | async-start | bytes 4718592 | tf_op jit(solution)/shard_map/all_gather | solution.py:26
  336.3 175.7 %all-gather.21.cloned.1.call-start = ((), (), s32[]{:S(2)}) async-start(), calls=%async_computation.14 | async-start | bytes 2506752 | tf_op jit(solution)/shard_map/all_gather | solution.py:45
  337.0 243.7 %reduce-scatter.15.cloned.1.call-start = ((), (), s32[]{:S(2)}) async-start(), calls=%async_computation.17 | async-start | bytes 4718592 | tf_op jit(solution)/shard_map/reduce_scatter | solution.py:30
  511.9 20.1 %copy-start.48 = (bf16[768,1536]{1,0:T(8,128)(2,1)S(1)}, bf16[768,1536]{1,0:T(8,128)(2,1)}, u32[]{:S(2)}) copy-start(bf16[768,1536]{1,0:T(8,128)(2,1)} %all-gather.19.cloned.1.call-done) | copy-start | bytes 7077892
  538.4 87.8 %reduce-scatter.13.cloned.1.call-start = ((), (), s32[]{:S(2)}) async-start(), calls=%async_computation.15 | async-start | bytes 4718592 | tf_op jit(solution)/shard_map/reduce_scatter | solution.py:30
  547.7 78.5 %copy-start.42 = (f32[768]{0:T(1024)S(1)}, f32[768]{0:T(1024)}, u32[]{:S(2)}) copy-start(f32[768]{0:T(1024)} %get-tuple-element.491) | copy-start | bytes 9220
  547.8 130.3 %all-gather.25.cloned.1.call-start = ((), (), s32[]{:S(2)}) async-start(), calls=%async_computation.18 | async-start | bytes 4718592 | tf_op jit(solution)/shard_map/all_gather | solution.py:26
  630.7 47.4 %copy-start.27 = (bf16[384,768]{0,1:T(8,128)(2,1)S(1)}, bf16[384,768]{0,1:T(8,128)(2,1)}, u32[]{:S(2)}) copy-start(bf16[384,768]{0,1:T(8,128)(2,1)} %all_gather.48) | copy-start | bytes 1769476
  633.0 343.5 %reduce-scatter.17.cloned.1.call-start = ((), (), s32[]{:S(2)}) async-start(), calls=%async_computation.19 | async-start | bytes 4718592 | tf_op jit(solution)/shard_map/reduce_scatter | solution.py:30
  712.7 12.9 copy-start.1
  770.7 12.9 copy-start.1
  828.7 12.9 copy-start.1
  886.7 12.9 copy-start.1
  931.3 164.2 %all-reduce.11.cloned.1.call-start = ((), (), s32[]{:S(2)}) async-start(), calls=%async_computation.24 | async-start | bytes 9437184
  947.0 228.8 %reduce-scatter.23.cloned.1.call-start = ((), (), s32[]{:S(2)}) async-start(), calls=%async_computation.22 | async-start | bytes 5013504 | tf_op jit(solution)/shard_map/reduce_scatter | solution.py:238
  958.6 296.6 %reduce-scatter.25.cloned.1.call-start = ((), (), s32[]{:S(2)}) async-start(), calls=%async_computation.23 | async-start | bytes 5013504 | tf_op jit(solution)/shard_map/reduce_scatter | solution.py:239
  970.0 346.4 %reduce-scatter.21.cloned.1.call-start = ((), (), s32[]{:S(2)}) async-start(), calls=%async_computation.21 | async-start | bytes 1253376 | tf_op jit(solution)/shard_map/reduce_scatter | solution.py:259
  976.4 6.1 copy-start.15
  976.4 446.4 %reduce-scatter.19.cloned.1.call-start = ((), (), s32[]{:S(2)}) async-start(), calls=%async_computation.20 | async-start | bytes 3244032 | tf_op jit(solution)/shard_map/reduce_scatter | solution.py:290
  987.8 109.4 %copy-start.41 = (f32[768]{0:T(1024)S(1)}, f32[768]{0:T(1024)}, u32[]{:S(2)}) copy-start(f32[768]{0:T(1024)} %get-tuple-element.421) | copy-start | bytes 9220
  (57 other events, 173.1 us)
Sparse Core Ops, SparseCore 0:
  10.9 57.7 all-gather.10
  71.1 39.3 all-gather.14
  152.2 42.9 all-gather.12
  285.4 44.6 reduce-scatter.10
  332.5 42.0 all-gather.18
  376.7 43.7 all-gather.16
  422.1 44.9 all-gather.22
  469.6 42.3 all-gather.20
  538.6 42.1 reduce-scatter.14
  582.8 43.3 reduce-scatter.12
  633.1 44.9 all-gather.24
  931.4 43.3 reduce-scatter.16
  978.4 117.0 all-reduce.10
  1099.7 75.9 reduce-scatter.22
  1180.6 74.5 reduce-scatter.24
  1259.2 57.1 reduce-scatter.20
  1322.3 100.4 reduce-scatter.18
where the time goes:
time: 1440 us; the launch traced here: 1430 us
  waiting for transfers between devices  696 us (48%)
  blocking collectives  235 us (16%)
  matrix products  210 us (15%)
  local copies, waits for them, and re-layouts  156 us (11%)
  other arithmetic  94.2 us (7%)
  loops' own time  22.2 us (2%)
  between operations  15.5 us (1%)
    all_gather x4, waiting for transfers between devices, gather_rows(): return lax.all_gather(values, 'tensor', axis=0, tiled=True)  146 us
    unnamed x18, waiting for transfers between devices  108 us
    reduce_scatter x1, waiting for transfers between devices, shards(): lax.psum_scatter(table_terms, ('dp', 'tensor'), scatter_dimension=1, tile...  106 us
    unnamed x2, blocking collectives  80.8 us
    reduce_scatter x1, waiting for transfers between devices, shards(): lax.psum_scatter(grad_downw, 'dp', scatter_dimension=1, tiled=True)  79.4 us
    reduce_scatter x4, waiting for transfers between devices, sum_rows(): lax.psum_scatter(values.astype(jnp.bfloat16), 'tensor', scatter_dimension...  78.4 us
    all_gather x1, blocking collectives, shards(): lax.all_gather(norm_gains, ('dp', 'tensor'), axis=1, tiled=True)  69.5 us
    all_gather x1, blocking collectives, shards(): lax.all_gather(biases, ('dp', 'tensor'), axis=1, tiled=True)  64.1 us
  transfers between devices with their start and end apart: 17, of which 14 were waited for; matrix products, arithmetic and copies ran while one was open for 7% of the time, Pallas kernels for 0%

commit v1 on v0

--- a/solution.py
+++ b/solution.py
@@ -1,6 +1,10 @@
+import functools
+
 import jax
 import jax.numpy as jnp
 from jax import lax
+from jax.experimental import pallas as pl
+from jax.experimental.pallas import tpu as pltpu
 from jax.sharding import PartitionSpec as P
 
 HEAD_DIM = 64
@@ -13,6 +17,7 @@
 EPS = 1e-05
 NEGATIVE = -1e30
 HIGH = lax.Precision.HIGHEST
+VMEM_LIMIT = 62 * 1024 * 1024
 
 
 def layer_norm(hidden, gain, shift):
@@ -304,6 +309,1028 @@
     )
 
 
+MESH_ID = pl.DeviceIdType.MESH
+F32, BF16 = jnp.float32, jnp.bfloat16
+NZ, NX, NC, NY = 4, 2, 2, 2
+QB = 256
+PACK_ROWS = 32
+GELU_A, GELU_B = 0.7978845608028654, 0.044715
+
+
+def nt(left, right):
+    return lax.dot_general(left, right, (((1,), (1,)), ((), ())), preferred_element_type=F32)
+
+
+def nn(left, right):
+    return lax.dot_general(left, right, (((1,), (0,)), ((), ())), preferred_element_type=F32)
+
+
+def tn(left, right):
+    return lax.dot_general(left, right, (((0,), (0,)), ((), ())), preferred_element_type=F32)
+
+
+def position():
+    dp = lax.axis_index("dp")
+    return (lax.axis_index("tensor"), dp // (NX * NC), lax.rem(dp // NC, NX), lax.rem(dp, NC))
+
+
+def device_at(y, z, x, c):
+    return (z * (NX * NC) + x * NC + c, y)
+
+
+def greet(pos):
+    y, z, x, c = pos
+    peers = [device_at(y, lax.rem(z + k, NZ), x, c) for k in range(1, NZ)]
+    peers += [device_at(y, z, 1 - x, c), device_at(1 - y, z, x, c), device_at(y, z, x, 1 - c)]
+    barrier = pltpu.get_barrier_semaphore()
+    for peer in peers:
+        pl.semaphore_signal(barrier, inc=1, device_id=peer, device_id_type=MESH_ID)
+    pl.semaphore_wait(barrier, len(peers))
+
+
+def remote(src, dst, send, recv, index, peer):
+    return pltpu.make_async_remote_copy(
+        src_ref=src,
+        dst_ref=dst,
+        send_sem=send.at[index],
+        recv_sem=recv.at[index],
+        device_id=peer,
+        device_id_type=MESH_ID,
+    )
+
+
+class Gather:
+    def __init__(self, buf, cols, send, recv, pos):
+        self.buf, self.cols, self.send, self.recv, self.pos = buf, cols, send, recv, pos
+
+    def view(self, y, z, x, c):
+        return self.buf.at[y, z, x, c, :, self.cols]
+
+    def steps(self, step):
+        y, z, x, c = self.pos
+        lo, hi, both = pl.ds(0, 2), pl.ds(2, 2), pl.ds(0, 2)
+        if step == 0:
+            return [
+                (k - 1, (y, z, x, c), (y, lax.rem(z + NZ - k, NZ), x, c), device_at(y, lax.rem(z + k, NZ), x, c))
+                for k in range(1, NZ)
+            ]
+        x_peer, y_peer = device_at(y, z, 1 - x, c), device_at(1 - y, z, x, c)
+        if step == 1:
+            return [(3, (y, lo, x, c), (y, lo, 1 - x, c), x_peer), (4, (y, hi, x, c), (1 - y, hi, x, c), y_peer)]
+        if step == 2:
+            return [
+                (5, (y, lo, both, c), (1 - y, lo, both, c), y_peer),
+                (6, (both, hi, x, c), (both, hi, 1 - x, c), x_peer),
+            ]
+        return [(7, (both, pl.ds(0, NZ), both, c), (both, pl.ds(0, NZ), both, 1 - c), device_at(y, z, x, 1 - c))]
+
+    def start(self, step):
+        for sem, src, _, peer in self.steps(step):
+            remote(self.view(*src), self.view(*src), self.send, self.recv, sem, peer).start()
+
+    def wait(self, step):
+        for sem, _, dst, peer in self.steps(step):
+            remote(self.view(*dst), self.view(*dst), self.send, self.recv, sem, peer).wait_recv()
+
+    def next(self, step):
+        self.wait(step)
+        self.start(step + 1)
+
+    def drain(self):
+        for step in range(4):
+            for sem, src, _, peer in self.steps(step):
+                remote(self.view(*src), self.view(*src), self.send, self.recv, sem, peer).wait_send()
+
+
+def gelu_parts(v):
+    square = v * v
+    half = 0.5 + 0.5 * jnp.tanh(v * (GELU_A + (GELU_A * GELU_B) * square))
+    act = v * half
+    slope = half + (2.0 * act) * (1.0 - half) * (GELU_A + (3 * GELU_A * GELU_B) * square)
+    return act, slope
+
+
+def moments(hidden):
+    average = jnp.mean(hidden, axis=-1, keepdims=True)
+    centered = hidden - average
+    variance = jnp.mean(centered * centered, axis=-1, keepdims=True)
+    scale = lax.rsqrt(variance + EPS)
+    return centered * scale, scale
+
+
+def norm_back(xhat, scale, grad):
+    return (grad - jnp.mean(grad, axis=-1, keepdims=True) - xhat * jnp.mean(grad * xhat, axis=-1, keepdims=True)) * scale
+
+
+def row_block(index, size):
+    return pl.ds(pl.multiple_of(index * size, size), size)
+
+
+def sum_rows_of(values):
+    return jnp.sum(values.astype(F32), axis=0, keepdims=True)
+
+
+def blocks():
+    for z in range(NZ):
+        for x in range(NX):
+            for c in range(NC):
+                for y in range(NY):
+                    yield (z * NX + x) * NC * NY + c * NY + y, (y, z, x, c)
+
+
+def forward_kernel(
+    dims,
+    tokens,
+    steps,
+    gains,
+    biases,
+    shift2,
+    hidden,
+    table,
+    qkv,
+    outw,
+    upw,
+    downw,
+    cot,
+    q_out,
+    k_out,
+    v_out,
+    mixed_out,
+    normed_out,
+    middle_out,
+    gsec_out,
+    small_out,
+    lse_out,
+    ghid_out,
+    csum_out,
+    layer_out,
+    weights_out,
+    grads_out,
+    full,
+    pack,
+    stage,
+    normed,
+    queries,
+    keys_all,
+    values_all,
+    mixed,
+    middle,
+    second,
+    second_t,
+    cot_t,
+    result,
+    gsec,
+    act,
+    gpre,
+    gtile,
+    hid,
+    send,
+    recv,
+    local,
+):
+    rows, width, per, half, ffh, ft = dims
+    pos = position()
+    y, z, x, c = pos
+    me = device_at(y, z, x, c)[0] * NY + y
+    share = width // (NZ * NX * NC * NY)
+    n_ff = ffh // ft
+    greet(pos)
+
+    names = ["pack", "q", "k", "v", "o"] + [f"m{i}" for i in range(n_ff)]
+    col = {"pack": pl.ds(0, 128)}
+    for i, name in enumerate(["q", "k", "v", "o"]):
+        col[name] = pl.ds(i * half, half)
+    for i in range(n_ff):
+        col[f"m{i}"] = pl.ds(4 * half + 2 * ft * i, 2 * ft)
+    flow = {
+        name: Gather(pack if name == "pack" else full, col[name], send.at[i], recv.at[i], pos) for i, name in enumerate(names)
+    }
+
+    for i, name in enumerate(["q", "k", "v"]):
+        full[y, z, x, c, :, col[name]] = qkv[i]
+        if name == "q":
+            flow["q"].start(0)
+    stage[...] = jnp.zeros_like(stage)
+    stage[0:2, 0:share] = gains[...].astype(F32)
+    stage[2:7, 0:share] = biases[...].astype(F32)
+    stage[7:8, 0:share] = shift2[...].astype(F32)
+    picked = (steps[...] == lax.broadcasted_iota(jnp.int32, (steps.shape[0], table.shape[0]), 1)).astype(BF16)
+    stage[32 : 32 + steps.shape[0], 0:share] = nn(picked, table[...])
+    turned = stage[...].T
+    pack[y, z, x, c, 0:share, :] = turned[0:share]
+    hshare = hidden.shape[1]
+    lane = lax.broadcasted_iota(jnp.int32, (hshare, NC * NY * hshare), 0) + hshare * (c * NY + y)
+    place = (lane == lax.broadcasted_iota(jnp.int32, (hshare, NC * NY * hshare), 1)).astype(BF16)
+    spread = nn(jnp.broadcast_to(hidden[...], (8, hshare)), place)
+    for j in range(spread.shape[1] // 128):
+        pack[y, z, x, c, share + j : share + j + 1, :] = spread[0:1, 128 * j : 128 * j + 128]
+    flow["pack"].start(0)
+    flow["k"].start(0)
+    flow["v"].start(0)
+    full[y, z, x, c, :, col["o"]] = outw[...].T
+    flow["o"].start(0)
+    for i in range(n_ff):
+        full[y, z, x, c, :, pl.ds(4 * half + 2 * ft * i, ft)] = upw[:, ft * i : ft * i + ft]
+        full[y, z, x, c, :, pl.ds(4 * half + 2 * ft * i + ft, ft)] = downw[ft * i : ft * i + ft, :].T
+        flow[f"m{i}"].start(0)
+
+    flow["pack"].next(0)
+    flow["q"].next(0)
+    flow["pack"].next(1)
+
+    def turn_cot(i, total):
+        rb = row_block(i, 256)
+        block = cot[rb, :]
+        cot_t[:, rb] = block.T
+        return total + sum_rows_of(block)
+
+    csum_out[...] = lax.fori_loop(0, rows // 256, turn_cot, jnp.zeros((1, width), F32))
+    flow["q"].next(1)
+    flow["pack"].next(2)
+    flow["k"].next(0)
+    flow["pack"].wait(3)
+
+    for d, (by, bz, bx, bc) in blocks():
+        middle[d * share : d * share + share, 0:128] = pack[by, bz, bx, bc, 0:share, :]
+    small_out[...] = middle[0:width, 0:128].T
+    for bz in range(NZ):
+        for bx in range(NX):
+            total = pack[0, bz, bx, 0, share : share + 8, :]
+            for bc, by in ((0, 1), (1, 0), (1, 1)):
+                total = total + pack[by, bz, bx, bc, share : share + 8, :]
+            for j in range(NC * NY * hshare // 128):
+                at = (bz * NX + bx) * NC * NY * hshare + 128 * j
+                hid[0:1, at : at + 128] = total[j : j + 1]
+    embed = small_out[pl.ds(32 + me, 1), :]
+
+    def first_norm(i, _):
+        rb = row_block(i, 128)
+        xhat, _ = moments(tokens[rb, :].astype(F32) + embed)
+        normed[rb, :] = (xhat * small_out[0:1, :] + small_out[2:3, :]).astype(BF16)
+        return 0
+
+    flow["q"].next(2)
+    lax.fori_loop(0, rows // 128, first_norm, 0)
+
+    def whole(cols):
+        return jnp.concatenate([full[by, :, :, :, :, cols].reshape(width, half) for by in range(NY)], axis=1)
+
+    def project(name, bias, factor, out):
+        def body(i, _):
+            rb = row_block(i, 512)
+            value = nn(normed[rb, :], whole(col[name]))
+            if bias is not None:
+                value = value + small_out[bias : bias + 1, :]
+            value = value.astype(BF16)
+            out[rb, :] = value * jnp.asarray(factor, BF16) if factor != 1 else value
+            return 0
+
+        lax.fori_loop(0, rows // 512, body, 0)
+
+    locals_ = []
+
+    def save(src, dst, index):
+        copy = pltpu.make_async_copy(src, dst, local.at[index])
+        copy.start()
+        locals_.append(copy)
+
+    flow["k"].next(1)
+    flow["v"].next(0)
+    flow["q"].wait(3)
+    project("q", 3, HEAD_DIM**-0.5, queries)
+    flow["k"].next(2)
+    flow["v"].next(1)
+    flow["o"].next(0)
+    flow["k"].wait(3)
+    project("k", None, 1, keys_all)
+    flow["v"].next(2)
+    flow["o"].next(1)
+    flow["m0"].next(0)
+    flow["v"].wait(3)
+    project("v", 4, 1, values_all)
+    save(normed, normed_out, 0)
+    save(queries, q_out, 1)
+    save(keys_all, k_out, 2)
+    save(values_all, v_out, 3)
+
+    def attend(p, _):
+        @pl.when(p == 0)
+        def _():
+            flow["o"].next(2)
+            flow["m0"].next(1)
+
+        @pl.when(p == 1)
+        def _():
+            flow["m1"].next(0)
+
+        @pl.when(p == 3)
+        def _():
+            flow["m0"].next(2)
+            flow["m2"].next(0)
+
+        @pl.when(p == 4)
+        def _():
+            flow["m1"].next(1)
+
+        cols = pl.ds(pl.multiple_of(p * 128, 128), 128)
+        low = lax.broadcasted_iota(jnp.int32, (QB, 128), 1) < HEAD_DIM
+        for i in range(rows // QB):
+            n = (i + 1) * QB
+            rb = slice(i * QB, n)
+            key, value, query = keys_all[0:n, cols], values_all[0:n, cols], queries[rb, cols]
+            outs = []
+            for h in range(2):
+                scores = nt(key, jnp.where(low == (h == 0), query, jnp.zeros_like(query)))
+                top = jnp.max(scores, axis=0, keepdims=True)
+                expo = jnp.exp(scores - top)
+                total = jnp.sum(expo, axis=0, keepdims=True)
+                lse_out[pl.ds(2 * p + h, 1), rb] = top + jnp.log(total)
+                outs.append(tn((expo * (1.0 / total)).astype(BF16), value))
+            mixed[rb, cols] = jnp.where(low, outs[0], outs[1]).astype(BF16)
+        return 0
+
+    lax.fori_loop(0, width // 128, attend, 0)
+    flow["o"].wait(3)
+    save(mixed, mixed_out, 4)
+    for by in range(NY):
+        save(full.at[by, :, :, :, :, pl.ds(0, 4 * half)], weights_out.at[by], 5 + by)
+
+    def second_norm(i, _):
+        rb = row_block(i, 256)
+        start_h = tokens[rb, :].astype(F32) + embed
+        value = start_h + (nt(mixed[rb, :], whole(col["o"])) + small_out[5:6, :])
+        middle[rb, :] = value
+        xhat, _ = moments(value)
+        block = (xhat * small_out[1:2, :] + small_out[7:8, :]).astype(BF16)
+        second[rb, :] = block
+        second_t[:, rb] = block.T
+        return 0
+
+    lax.fori_loop(0, rows // 256, second_norm, 0)
+    save(middle, middle_out, 7)
+    flow["m1"].next(2)
+    flow["m0"].wait(3)
+
+    def tile_copy(t, slot):
+        ty, tm = lax.rem(t, NY), t // NY
+        return pltpu.make_async_copy(
+            gtile.at[slot], grads_out.at[ty, :, pl.ds(pl.multiple_of(tm * 2 * ft, 128), 2 * ft)], local.at[8 + slot]
+        )
+
+    def tile(t, _):
+        ty, tm = lax.rem(t, NY), t // NY
+        slot = lax.rem(t, 2)
+
+        @pl.when(t == 1)
+        def _():
+            flow["m2"].next(1)
+
+        @pl.when(t == 2)
+        def _():
+            flow["m1"].wait(3)
+
+        @pl.when(t == 3)
+        def _():
+            flow["m2"].next(2)
+
+        @pl.when(t == 4)
+        def _():
+            flow["m2"].wait(3)
+
+        up_at = pl.ds(pl.multiple_of(4 * half + tm * 2 * ft, 128), ft)
+        down_at = pl.ds(pl.multiple_of(4 * half + tm * 2 * ft + ft, 128), ft)
+        hid_at = pl.ds(pl.multiple_of(ty * ffh + tm * ft, 128), ft)
+
+        def up():
+            return full[ty, :, :, :, :, up_at].reshape(width, ft)
+
+        def down():
+            return full[ty, :, :, :, :, down_at].reshape(width, ft)
+
+        pre = nn(second[...], up()) + hid[:, hid_at]
+        gact = nn(cot[...], down())
+        value, slope = gelu_parts(pre)
+        act[...] = value.astype(BF16)
+        grad = (gact * slope).astype(BF16)
+        gpre[...] = grad
+        ghid_out[:, hid_at] = sum_rows_of(grad)
+        more = nt(act[...], down())
+        gmore = nt(gpre[...], up())
+
+        @pl.when(t == 0)
+        def _():
+            result[...] = more
+            gsec[...] = gmore
+
+        @pl.when(t > 0)
+        def _():
+            result[...] += more
+            gsec[...] += gmore
+
+        @pl.when(t >= 2)
+        def _():
+            tile_copy(t - 2, slot).wait()
+
+        def weight_grad(i, _):
+            rb = row_block(i, 256)
+            gtile[slot, rb, 0:ft] = nn(second_t[rb, :], gpre[...]).astype(BF16)
+            gtile[slot, rb, ft : 2 * ft] = nn(cot_t[rb, :], act[...]).astype(BF16)
+            return 0
+
+        lax.fori_loop(0, width // 256, weight_grad, 0)
+        tile_copy(t, slot).start()
+        return 0
+
+    tiles = NY * n_ff
+    lax.fori_loop(0, tiles, tile, 0)
+    save(gsec, gsec_out, 10)
+
+    def finish(i, _):
+        rb = row_block(i, 256)
+        layer_out[rb, :] = (middle[rb, :] + (result[rb, :] + small_out[6:7, :])).astype(BF16)
+        return 0
+
+    lax.fori_loop(0, rows // 256, finish, 0)
+    tile_copy(tiles - 2, 0).wait()
+    tile_copy(tiles - 1, 1).wait()
+    for copy in locals_:
+        copy.wait()
+    for name in names:
+        flow[name].drain()
+
+
+class Scatter:
+    def __init__(self, source, own, bufs, send, recv, pos, loaded):
+        self.source, self.own, self.bufs = source, own, bufs
+        self.send, self.recv, self.pos, self.loaded = send, recv, pos, loaded
+
+    def copies(self, step):
+        y, z, x, c = self.pos
+        first, second_x, second_y, third_y, third_x, last = self.bufs
+        own = self.own
+        lo, hi, both = pl.ds(0, 2), pl.ds(2, 2), pl.ds(0, 2)
+        x_peer, y_peer = device_at(y, z, 1 - x, c), device_at(1 - y, z, x, c)
+        if step == 0:
+            return [(0, self.source.at[both, pl.ds(0, NZ), both, 1 - c], first, device_at(y, z, x, 1 - c))]
+        if step == 1:
+            return [(1, own.at[both, lo, 1 - x], second_x, x_peer), (2, own.at[1 - y, hi, both], second_y, y_peer)]
+        if step == 2:
+            return [(3, own.at[1 - y, lo, x], third_y, y_peer), (4, own.at[y, hi, 1 - x], third_x, x_peer)]
+        return [
+            (4 + k, own.at[y, lax.rem(z + k, NZ), x], last.at[k - 1], device_at(y, lax.rem(z + k, NZ), x, c))
+            for k in range(1, NZ)
+        ]
+
+    def start(self, step):
+        for sem, src, dst, peer in self.copies(step):
+            remote(src, dst, self.send, self.recv, sem, peer).start()
+
+    def wait(self, step):
+        for sem, src, dst, peer in self.copies(step):
+            remote(src, dst, self.send, self.recv, sem, peer).wait_recv()
+
+    def add(self, step):
+        y, z, x, c = self.pos
+        own, source = self.own, self.source
+        first, second_x, second_y, third_y, third_x, last = self.bufs
+        kind = own.dtype
+
+        def plus(left, right):
+            return (left.astype(F32) + right.astype(F32)).astype(kind)
+
+        def each(count, body):
+            def run(i, _):
+                body(i)
+                return 0
+
+            lax.fori_loop(0, count, run, 0)
+
+        if step == 0:
+
+            def body(i):
+                iy, iz, ix = i // (NZ * NX), lax.rem(i // NX, NZ), lax.rem(i, NX)
+                mine = own[iy, iz, ix] if self.loaded else source[iy, iz, ix, c]
+                own[iy, iz, ix] = plus(mine, first[iy, iz, ix])
+
+            each(NY * NZ * NX, body)
+        elif step == 1:
+
+            def body(i):
+                a, b = i // 2, lax.rem(i, 2)
+                own[a, b, x] = plus(own[a, b, x], second_x[a, b])
+                own[y, 2 + a, b] = plus(own[y, 2 + a, b], second_y[a, b])
+
+            each(4, body)
+        else:
+
+            def body(i):
+                own[y, i, x] = plus(own[y, i, x], third_y[i])
+                own[y, 2 + i, x] = plus(own[y, 2 + i, x], third_x[i])
+
+            each(2, body)
+
+    def next(self, step):
+        self.wait(step)
+        self.add(step)
+        self.start(step + 1)
+
+    def final(self):
+        y, z, x, c = self.pos
+        last = self.bufs[5]
+        self.wait(3)
+        total = self.own[y, z, x].astype(F32)
+        for k in range(NZ - 1):
+            total = total + last[k].astype(F32)
+        return total
+
+    def drain(self):
+        for step in range(4):
+            for sem, src, dst, peer in self.copies(step):
+                remote(src, dst, self.send, self.recv, sem, peer).wait_send()
+
+
+def scatter_scratch(per, width, kind):
+    return [
+        pltpu.VMEM((NY, NZ, NX, per, width), kind),
+        pltpu.VMEM((NY, NZ, NX, per, width), kind),
+        pltpu.VMEM((2, 2, per, width), kind),
+        pltpu.VMEM((2, 2, per, width), kind),
+        pltpu.VMEM((2, per, width), kind),
+        pltpu.VMEM((2, per, width), kind),
+        pltpu.VMEM((NZ - 1, per, width), kind),
+    ]
+
+
+def backward_kernel(
+    dims,
+    tokens,
+    cot,
+    small,
+    lse,
+    ghid,
+    csum,
+    q_in,
+    k_in,
+    v_in,
+    mixed_in,
+    normed_in,
+    middle_in,
+    gsec_in,
+    weights_in,
+    grads_in,
+    gup_out,
+    gdown_out,
+    gout_out,
+    gqkv_out,
+    gpack_out,
+    gtok_out,
+    queries,
+    keys_all,
+    values_all,
+    mixed,
+    normed,
+    normed_t,
+    middle,
+    gsec,
+    weights,
+    gattn,
+    gattn_t,
+    gval,
+    acc_k,
+    acc_v,
+    sums,
+    gpack,
+    gout,
+    gqkv,
+    *rest,
+):
+    rows, width, per, half, ffh, ft = dims
+    pos = position()
+    y, z, x, c = pos
+    me = device_at(y, z, x, c)[0] * NY + y
+    share = width // (NZ * NX * NC * NY)
+    n_ff = ffh // ft
+    n_groups = half // 128
+    names = [f"m{i}" for i in range(n_ff)] + ["o"] + [f"q{i}" for i in range(n_groups)] + ["pack"]
+    send, recv, local = rest[-3:]
+    flow = {}
+    for i, name in enumerate(names):
+        own, first, *others = rest[7 * i : 7 * i + 7]
+        if name[0] == "m":
+            source = grads_in.at[:, :, :, :, :, pl.ds(2 * ft * i, 2 * ft)]
+        else:
+            source = {"o": gout, "p": gpack}.get(name[0], None)
+            if source is None:
+                source = gqkv.at[int(name[1:])]
+        flow[name] = Scatter(source, own, [first] + others, send.at[i], recv.at[i], pos, name[0] == "m")
+
+    copies = {}
+
+    def load(name, src, dst, index):
+        copies[name] = pltpu.make_async_copy(src, dst, local.at[index])
+        copies[name].start()
+
+    load("middle", middle_in, middle, 0)
+    load("gsec", gsec_in, gsec, 1)
+    for i in range(n_ff):
+        name = f"m{i}"
+        load(name, flow[name].source.at[:, :, :, c], flow[name].own, 2 + i)
+    at = 2 + n_ff
+    load("w", weights_in, weights, at)
+    load("mixed", mixed_in, mixed, at + 1)
+    load("normed", normed_in, normed, at + 2)
+    load("q", q_in, queries, at + 3)
+    load("k", k_in, keys_all, at + 4)
+    load("v", v_in, values_all, at + 5)
+    greet(pos)
+    for i in range(n_ff):
+        flow[f"m{i}"].start(0)
+    copies["middle"].wait()
+    copies["gsec"].wait()
+
+    def second_back(i, totals):
+        rb = row_block(i, 128)
+        xhat, scale = moments(middle[rb, :])
+        grad = gsec[rb, :]
+        result = cot[rb, :].astype(F32) + norm_back(xhat, scale, grad * small[1:2, :])
+        gsec[rb, :] = result
+        low = result.astype(BF16)
+        gattn[rb, :] = low
+        gattn_t[:, rb] = low.T
+        return (
+            totals[0] + sum_rows_of(grad * xhat),
+            totals[1] + sum_rows_of(grad),
+            totals[2] + sum_rows_of(low),
+        )
+
+    zero = jnp.zeros((1, width), F32)
+    ggain2, gshift2, gattn_sum = lax.fori_loop(0, rows // 128, second_back, (zero, zero, zero))
+    sums[...] = jnp.zeros_like(sums)
+    sums[1:2, :] = ggain2
+    sums[5:6, :] = gattn_sum
+    sums[6:7, :] = csum[...]
+    sums[7:8, :] = gshift2
+    copies["m0"].wait()
+    flow["m0"].next(0)
+    copies["w"].wait()
+    copies["mixed"].wait()
+
+    def whole(index):
+        cols = pl.ds(index * half, half)
+        return jnp.concatenate([weights[by, :, cols] for by in range(NY)], axis=1)
+
+    for by in range(NY):
+        def out_grad(i, _):
+            rb = row_block(i, 384)
+            part = nn(gattn_t[rb, :], mixed[:, by * half : by * half + half]).astype(BF16)
+            gout[by, pl.ds(i * 2, 2)] = part.reshape(2, NX, NC, per, half)
+            return 0
+
+        lax.fori_loop(0, width // 384, out_grad, 0)
+    flow["o"].start(0)
+
+    def mixed_grad(i, _):
+        rb = row_block(i, 512)
+        mixed[rb, :] = nn(gattn[rb, :], whole(3)).astype(BF16)
+        return 0
+
+    lax.fori_loop(0, rows // 512, mixed_grad, 0)
+    copies["m1"].wait()
+    flow["m1"].next(0)
+    copies["normed"].wait()
+
+    def turn_normed(i, _):
+        rb = row_block(i, 256)
+        normed_t[:, rb] = normed[rb, :].T
+        return 0
+
+    lax.fori_loop(0, rows // 256, turn_normed, 0)
+    copies["q"].wait()
+    copies["k"].wait()
+    copies["v"].wait()
+    gq, gk, gv = gattn, normed, gval
+
+    def attend_back(s, _):
+        group, by = s // NY, lax.rem(s, NY)
+        p = by * n_groups + group
+
+        @pl.when(s == 1)
+        def _():
+            copies["m2"].wait()
+            flow["m2"].next(0)
+            flow["m0"].next(1)
+
+        @pl.when(s == 2)
+        def _():
+            flow["o"].next(0)
+
+        @pl.when(s == 3)
+        def _():
+            flow["m1"].next(1)
+            flow["m0"].next(2)
+            flow["q0"].next(0)
+
+        @pl.when(s == 4)
+        def _():
+            flow["m2"].next(1)
+            flow["o"].next(1)
+
+        @pl.when(s == 5)
+        def _():
+            flow["q1"].next(0)
+            flow["m1"].next(2)
+            flow["q0"].next(1)
+
+        cols = pl.ds(pl.multiple_of(p * 128, 128), 128)
+        low = lax.broadcasted_iota(jnp.int32, (QB, 128), 1) < HEAD_DIM
+        for i in range(rows // QB):
+            n = (i + 1) * QB
+            rb = slice(i * QB, n)
+            key, value = keys_all[0:n, cols], values_all[0:n, cols]
+            query, grad = queries[rb, cols], mixed[rb, cols]
+            parts, dv, dk = [], None, None
+            for h in range(2):
+                sel = low == (h == 0)
+                query_h = jnp.where(sel, query, jnp.zeros_like(query))
+                grad_h = jnp.where(sel, grad, jnp.zeros_like(grad))
+                probs = jnp.exp(nt(key, query_h) - lse[pl.ds(2 * p + h, 1), rb])
+                gprobs = nt(value, grad_h)
+                inner = jnp.sum(probs * gprobs, axis=0, keepdims=True)
+                gscores = (probs * (gprobs - inner)).astype(BF16)
+                pv, pk = nn(probs.astype(BF16), grad_h), nn(gscores, query_h)
+                dv = pv if dv is None else dv + pv
+                dk = pk if dk is None else dk + pk
+                parts.append(tn(gscores, key))
+            last = n - QB
+            if last:
+                acc_k[0:last] += dk[:last]
+                acc_v[0:last] += dv[:last]
+            acc_k[last:n] = dk[last:]
+            acc_v[last:n] = dv[last:]
+            gq[rb, cols] = (jnp.where(low, parts[0], parts[1]) * HEAD_DIM**-0.5).astype(BF16)
+        gk[:, cols] = acc_k[...].astype(BF16)
+        gv[:, cols] = acc_v[...].astype(BF16)
+
+        @pl.when(by == NY - 1)
+        def _():
+            for piece, source in enumerate((gq, gk, gv)):
+                pick = jnp.concatenate(
+                    [source[:, pl.ds(pl.multiple_of((b * n_groups + group) * 128, 128), 128)] for b in range(NY)], axis=1
+                )
+                part = nn(normed_t[...], pick).astype(BF16)
+                for b in range(NY):
+                    gqkv[group, b, :, :, :, :, piece * 128 : piece * 128 + 128] = part[:, b * 128 : b * 128 + 128].reshape(
+                        NZ, NX, NC, per, 128
+                    )
+            for g in range(n_groups):
+                @pl.when(group == g)
+                def _():
+                    flow[f"q{g}"].start(0)
+
+        return 0
+
+    lax.fori_loop(0, NY * n_groups, attend_back, 0)
+    flow["q0"].next(2)
+    flow["m2"].next(2)
+    flow["o"].next(2)
+    flow["q1"].next(1)
+    flow["q2"].next(0)
+    embed = small[pl.ds(32 + me, 1), :]
+
+    def first_back(i, totals):
+        rb = row_block(i, 256)
+        xhat, scale = moments(tokens[rb, :].astype(F32) + embed)
+        q_rows, k_rows, v_rows = gq[rb, :], gk[rb, :], gv[rb, :]
+        grad = nt(q_rows, whole(0)) + nt(k_rows, whole(1)) + nt(v_rows, whole(2))
+        result = gsec[rb, :] + norm_back(xhat, scale, grad * small[0:1, :])
+        middle[rb, :] = result
+
+        @pl.when(i == 1)
+        def _():
+            flow["q1"].next(2)
+            flow["q2"].next(1)
+
+        return (
+            totals[0] + sum_rows_of(grad * xhat),
+            totals[1] + sum_rows_of(grad),
+            totals[2] + sum_rows_of(q_rows),
+            totals[3] + sum_rows_of(v_rows),
+            totals[4] + sum_rows_of(result),
+        )
+
+    ggain1, gshift1, q_sum, v_sum, seq_sum = lax.fori_loop(0, rows // 256, first_back, (zero,) * 5)
+    sums[0:1, :] = ggain1
+    sums[2:3, :] = gshift1
+    sums[3:4, :] = q_sum
+    sums[4:5, :] = v_sum
+    sums[pl.ds(32 + me, 1), :] = seq_sum
+    gtok = pltpu.make_async_copy(middle, gtok_out, local.at[at + 6])
+    gtok.start()
+    turned = sums[...].T
+    hgroup = ghid.shape[1] // (NZ * NX)
+    for d, (by, bz, bx, bc) in blocks():
+        gpack[by, bz, bx, bc, 0:share, :] = turned[d * share : d * share + share]
+        for j in range(hgroup // 128):
+            start = (bz * NX + bx) * hgroup + 128 * j
+            gpack[by, bz, bx, bc, share + j : share + j + 1, :] = ghid[:, start : start + 128]
+        gpack[by, bz, bx, bc, share + hgroup // 128 :, :] = jnp.zeros((PACK_ROWS - share - hgroup // 128, 128), F32)
+    flow["pack"].start(0)
+    for i in range(n_ff):
+        total = flow[f"m{i}"].final()
+        gup_out[:, ft * i : ft * i + ft] = total[:, 0:ft]
+        gdown_out[:, ft * i : ft * i + ft] = total[:, ft:]
+    flow["pack"].next(0)
+    flow["q2"].next(2)
+    flow["pack"].next(1)
+    gout_out[...] = flow["o"].final()
+    for g in range(n_groups - 1):
+        total = flow[f"q{g}"].final()
+        for piece in range(3):
+            gqkv_out[piece, :, 128 * g : 128 * g + 128] = total[:, 128 * piece : 128 * piece + 128]
+    flow["pack"].next(2)
+    g = n_groups - 1
+    total = flow[f"q{g}"].final()
+    for piece in range(3):
+        gqkv_out[piece, :, 128 * g : 128 * g + 128] = total[:, 128 * piece : 128 * piece + 128]
+    gpack_out[...] = flow["pack"].final()
+    gtok.wait()
+    for name in names:
+        flow[name].drain()
+
+
+def fast_shards(
+    tokens,
+    timesteps,
+    norm_gains,
+    biases,
+    second_shift,
+    hidden_bias,
+    step_table,
+    qkv_weight,
+    out_weight,
+    up_weight,
+    down_weight,
+    cotangent,
+):
+    rows, width = tokens.shape
+    _, per, half = qkv_weight.shape
+    ffh = up_weight.shape[1]
+    ft = 512
+    dims = (rows, width, per, half, ffh, ft)
+    n_ff, n_groups = ffh // ft, half // 128
+    total = 4 * half + 2 * ffh
+    vmem, anywhere = pl.BlockSpec(memory_space=pltpu.VMEM), pl.BlockSpec(memory_space=pl.ANY)
+    shape = jax.ShapeDtypeStruct
+    low, wide = shape((rows, width), BF16), shape((rows, width), F32)
+    vm = pltpu.VMEM
+    hshare = hidden_bias.shape[0]
+    n_chunks = 5 + n_ff
+    outs = pl.pallas_call(
+        functools.partial(forward_kernel, dims),
+        in_specs=[vmem] * 12,
+        out_specs=[anywhere] * 7 + [vmem] * 5 + [anywhere] * 2,
+        out_shape=[
+            low,
+            low,
+            low,
+            low,
+            low,
+            wide,
+            wide,
+            shape((128, width), F32),
+            shape((16, rows), F32),
+            shape((1, NY * ffh), F32),
+            shape((1, width), F32),
+            low,
+            shape((NY, NZ, NX, NC, per, 4 * half), BF16),
+            shape((NY, width, 2 * ffh), BF16),
+        ],
+        scratch_shapes=[
+            vm((NY, NZ, NX, NC, per, total), BF16),
+            vm((NY, NZ, NX, NC, PACK_ROWS, 128), F32),
+            vm((128, 128), F32),
+            vm((rows, width), BF16),
+            vm((rows, width), BF16),
+            vm((rows, width), BF16),
+            vm((rows, width), BF16),
+            vm((rows, width), BF16),
+            vm((rows, width), F32),
+            vm((rows, width), BF16),
+            vm((width, rows), BF16),
+            vm((width, rows), BF16),
+            vm((rows, width), F32),
+            vm((rows, width), F32),
+            vm((rows, ft), BF16),
+            vm((rows, ft), BF16),
+            vm((2, width, 2 * ft), BF16),
+            vm((1, NY * ffh), F32),
+            pltpu.SemaphoreType.DMA((n_chunks, 8)),
+            pltpu.SemaphoreType.DMA((n_chunks, 8)),
+            pltpu.SemaphoreType.DMA((11,)),
+        ],
+        compiler_params=pltpu.CompilerParams(collective_id=0, has_side_effects=True, vmem_limit_bytes=VMEM_LIMIT),
+        name="layer_forward",
+    )(
+        tokens,
+        timesteps.reshape(-1, 1),
+        norm_gains,
+        biases,
+        second_shift.reshape(1, -1),
+        hidden_bias.reshape(1, -1),
+        step_table,
+        qkv_weight,
+        out_weight,
+        up_weight,
+        down_weight,
+        cotangent,
+    )
+    q, k, v, mixed, normed, middle, gsec, small, lse, ghid, csum, layer_out, weights, grads = outs
+    chunks = [2 * ft] * n_ff + [half] * (1 + n_groups)
+    scratch = []
+    for cols in chunks:
+        scratch += scatter_scratch(per, cols, BF16)
+    scratch += scatter_scratch(PACK_ROWS, 128, F32)
+    n_local = 2 + n_ff + 7
+    gup, gdown, gout, gqkv, gpack, gtok = pl.pallas_call(
+        functools.partial(backward_kernel, dims),
+        in_specs=[vmem] * 6 + [anywhere] * 9,
+        out_specs=[vmem] * 5 + [anywhere],
+        out_shape=[
+            shape((per, ffh), F32),
+            shape((per, ffh), F32),
+            shape((per, half), F32),
+            shape((3, per, half), F32),
+            shape((PACK_ROWS, 128), F32),
+            wide,
+        ],
+        scratch_shapes=[
+            vm((rows, width), BF16),
+            vm((rows, width), BF16),
+            vm((rows, width), BF16),
+            vm((rows, width), BF16),
+            vm((rows, width), BF16),
+            vm((width, rows), BF16),
+            vm((rows, width), F32),
+            vm((rows, width), F32),
+            vm((NY, width, 4 * half), BF16),
+            vm((rows, width), BF16),
+            vm((width, rows), BF16),
+            vm((rows, width), BF16),
+            vm((rows, 128), F32),
+            vm((rows, 128), F32),
+            vm((128, width), F32),
+            vm((NY, NZ, NX, NC, PACK_ROWS, 128), F32),
+            vm((NY, NZ, NX, NC, per, half), BF16),
+            vm((n_groups, NY, NZ, NX, NC, per, 3 * 128), BF16),
+            *scratch,
+            pltpu.SemaphoreType.DMA((len(chunks) + 1, 8)),
+            pltpu.SemaphoreType.DMA((len(chunks) + 1, 8)),
+            pltpu.SemaphoreType.DMA((n_local,)),
+        ],
+        compiler_params=pltpu.CompilerParams(collective_id=1, has_side_effects=True, vmem_limit_bytes=VMEM_LIMIT),
+        name="layer_backward",
+    )(
+        tokens,
+        cotangent,
+        small,
+        lse,
+        ghid,
+        csum,
+        q,
+        k,
+        v,
+        mixed,
+        normed,
+        middle,
+        gsec,
+        weights.reshape(NY, width, 4 * half),
+        grads.reshape(NY, NZ, NX, NC, per, 2 * ffh),
+    )
+    share = norm_gains.shape[1]
+    rows_small = gpack[:share, :8].T
+    hid_rows = gpack[share : share + NC * NY * hshare // 128].reshape(-1)
+    slot = lax.rem(lax.axis_index("dp"), NC) * NY + lax.axis_index("tensor")
+    grad_hidden = lax.dynamic_slice_in_dim(hid_rows, slot * hshare, hshare, 0)
+    n_seq = timesteps.shape[0]
+    picker = (jnp.arange(step_table.shape[0])[:, None] == timesteps[None, :]).astype(F32)
+    grad_table = lax.dot_general(
+        picker, gpack[:share, 32 : 32 + n_seq], (((1,), (1,)), ((), ())), precision=HIGH, preferred_element_type=F32
+    )
+    return (
+        layer_out,
+        gtok,
+        rows_small[0:2],
+        rows_small[2:7],
+        rows_small[7],
+        grad_hidden,
+        grad_table,
+        gqkv,
+        gout.T,
+        gup,
+        gdown.T,
+    )
+
+
 def solution(mesh):
     in_specs = (
         P(("dp", "tensor"), None),
@@ -332,4 +1359,5 @@
         P("dp", "tensor"),
         P("tensor", "dp"),
     )
-    return jax.shard_map(shards, mesh=mesh, in_specs=in_specs, out_specs=out_specs, check_vma=False)
+    fast = mesh.shape["dp"] == NZ * NX * NC and mesh.shape["tensor"] == NY
+    return jax.shard_map(fast_shards if fast else shards, mesh=mesh, in_specs=in_specs, out_specs=out_specs, check_vma=False)

time: 1440 us -> 229 us (0.16)
  waiting for transfers between devices: 696 us -> 0 us
  blocking collectives: 235 us -> 0 us
  Pallas kernels: 0 us -> 209 us
  matrix products: 210 us -> 1.77 us
  local copies, waits for them, and re-layouts: 156 us -> 17.3 us
  other arithmetic: 94.2 us -> 0 us
  loops' own time: 22.2 us -> 0 us
  between operations: 15.5 us -> 0.69 us
    reduce_scatter x8 -> x0, waiting for transfers between devices: 361 us -> none  [the longest x1 106 us: shards(): lax.psum_scatter(table_terms, ('dp', 'tensor'), scatter_dimension=1, tile...]
    all_gather x8 -> x0, waiting for transfers between devices: 228 us -> none  [the longest x4 146 us: gather_rows(): return lax.all_gather(values, 'tensor', axis=0, tiled=True)]
    pallas_call x0 -> x2, Pallas kernels: none -> 209 us  [the longest x1 116 us: fast_shards(): pl.pallas_call(functools.partial(forward_kernel, dims), in_specs=[vmem] *...]
    dot_general x41 -> x1, matrix products: 210 us -> 1.77 us  [fast_shards(): lax.dot_general(picker, gpack[:share, 32:32 + n_seq], (((1,), (1,)), ((),...]
    all_gather x3 -> x0, blocking collectives: 154 us -> none  [the longest x1 69.5 us: shards(): lax.all_gather(norm_gains, ('dp', 'tensor'), axis=1, tiled=True)]
    unnamed x18 -> x0, waiting for transfers between devices: 108 us -> none
    unnamed x2 -> x0, blocking collectives: 80.8 us -> none
    dynamic_slice x54 -> x1, local copies, waits for them, and re-layouts: 66.9 us -> 0.58 us  [fast_shards(): grad_hidden = lax.dynamic_slice_in_dim(hid_rows, slot * hshare, hshare, 0)]
  transfers between devices with their start and end apart: 17 -> 0, of which waited for: 14 -> 0; matrix products, arithmetic and copies ran while one was open for 7% -> 0% of each run, Pallas kernels for 0% -> 0%
where the time goes in v1:
time: 229 us; the launch traced here: 228 us
  Pallas kernels  209 us (91%)
  local copies, waits for them, and re-layouts  17.3 us (8%)
    pallas_call x1, Pallas kernels, fast_shards(): pl.pallas_call(functools.partial(forward_kernel, dims), in_specs=[vmem] *...  116 us
    pallas_call x1, Pallas kernels, fast_shards(): pl.pallas_call(functools.partial(backward_kernel, dims), in_specs=[vmem]...  92.9 us
    unnamed x25, local copies, waits for them, and re-layouts  13.2 us

profile of v1, /device:TPU:0, one launch (start us, length us, event | category | flops | bytes accessed | tf_op | source)
XLA Modules:
  0.0 228.3 jit_solution(533815073858897185)
XLA Ops:
  0.6 1.3 copy.29.steps
  2.0 1.7 copy.30.table
  3.6 1.5 copy.31.outw
  5.2 1.8 copy.32.downw
  7.0 115.7 %layer_forward.1 = (bf16[1024,768]{1,0:T(8,128)(2,1)}, bf16[1024,768]{1,0:T(8,128)(2,1)}, bf16[1024,768]{1,0:T(8,128)(2,1)}, bf16[1024,768]{1,0:T(8,128)(2,1)}, ...) custom-call(bf16[1024,768]{1,0:T(8,128)(2,1)} %tokens.3, ...), custom_call_target="tpu_custom_call" | custom-call | tf_op jit(solution)/shard_map/layer_forward/pallas_call | solution.py:1188
  122.7 0.0 copy-start.6
  122.7 0.0 copy-start.1
  122.7 92.9 %layer_backward.1 = (f32[48,1536]{1,0:T(8,128)}, f32[48,1536]{1,0:T(8,128)}, f32[48,384]{1,0:T(8,128)}, f32[3,48,384]{2,1,0:T(8,128)}, f32[32,128]{1,0:T(8,128)}, /*index=5*/f32[1024,768]{1,0:T(8,128)}) custom-call(bf16[1024,768]{1,0:T(8,128)(2,1)} %tokens.3, bf16[1024,768]{1,0:T(8,128)(2,1)} %cot.3, f32[128,768]{1,0:T(8,128)} %get-tuple-element.32.small, ...), custom_call_target="tpu_custom_call" | custom-call | tf_op jit(solution)/shard_map/layer_backward/pallas_call | solution.py:1254
  215.5 0.7 slice_bitcast_fusion
  216.2 0.6 copy.33
  216.9 0.1 slice.25
  217.0 0.7 copy.34
  217.6 0.7 slice_reduce_fusion
  218.3 0.7 slice_bitcast_fusion.1
  219.0 0.6 dynamic_slice.3
  219.6 0.0 copy-done.6
  219.6 1.8 fusion
  221.4 0.0 copy-done.1
  221.4 0.0 copy-start
  221.4 1.1 copy.41
  222.5 1.3 copy-done
  223.8 0.0 copy-start.4
  223.8 0.0 copy-start.5
  223.8 1.7 copy.42
  225.5 0.0 copy-done.4
  225.5 0.7 copy.43
  226.2 0.0 copy-done.5
  226.2 0.6 copy.44
  226.8 0.0 copy-done.3
  226.8 0.7 copy.45
  227.5 0.0 copy-done.2
  227.5 0.7 copy.46
  (2 shorter events, 0.0 us)
Async XLA Ops:
  122.7 96.9 %copy-start.6 = (s32[32]{0:T(128)S(1)}, s32[32]{0:T(128)}, u32[]{:S(2)}) copy-start(s32[32]{0:T(128)} %param.13) | copy-start | bytes 388
  122.7 98.7 %copy-start.1 = (bf16[1024,768]{1,0:T(8,128)(2,1)S(1)}, bf16[1024,768]{1,0:T(8,128)(2,1)}, u32[]{:S(2)}) copy-start(bf16[1024,768]{1,0:T(8,128)(2,1)} %get-tuple-element.84) | copy-start | bytes 4718596
  221.4 2.5 %copy-start = (f32[1024,768]{1,0:T(8,128)S(1)}, f32[1024,768]{1,0:T(8,128)}, u32[]{:S(2)}) copy-start(f32[1024,768]{1,0:T(8,128)} %get-tuple-element.85) | copy-start | bytes 9437188
  223.8 1.7 copy-start.4
  223.8 2.4 %copy-start.5 = (f32[48,384]{1,0:T(8,128)S(1)}, f32[48,384]{1,0:T(8,128)}, u32[]{:S(2)}) copy-start(f32[48,384]{1,0:T(8,128)} %get-tuple-element.48) | copy-start | bytes 221188
  223.8 3.0 %copy-start.3 = (f32[48,1536]{1,0:T(8,128)S(1)}, f32[48,1536]{1,0:T(8,128)}, u32[]{:S(2)}) copy-start(f32[48,1536]{1,0:T(8,128)} %get-tuple-element.93) | copy-start | bytes 884740
  223.8 3.7 %copy-start.2 = (f32[48,1536]{1,0:T(8,128)S(1)}, f32[48,1536]{1,0:T(8,128)}, u32[]{:S(2)}) copy-start(f32[48,1536]{1,0:T(8,128)} %get-tuple-element.50) | copy-start | bytes 884740

commit v2 on v1

--- a/solution.py
+++ b/solution.py
@@ -313,7 +313,7 @@
 F32, BF16 = jnp.float32, jnp.bfloat16
 NZ, NX, NC, NY = 4, 2, 2, 2
 QB = 256
-PACK_ROWS = 32
+LINE = 40
 GELU_A, GELU_B = 0.7978845608028654, 0.044715
 
 
@@ -338,14 +338,30 @@
     return (z * (NX * NC) + x * NC + c, y)
 
 
+def plane_peers(pos):
+    y, z, x, c = pos
+    for flip in range(1, NY * NX * NC):
+        to = (1 - y if flip & 4 else y, z, 1 - x if flip & 2 else x, 1 - c if flip & 1 else c)
+        yield flip - 1, to
+
+
 def greet(pos):
     y, z, x, c = pos
     peers = [device_at(y, lax.rem(z + k, NZ), x, c) for k in range(1, NZ)]
-    peers += [device_at(y, z, 1 - x, c), device_at(1 - y, z, x, c), device_at(y, z, x, 1 - c)]
+    peers += [device_at(*to) for _, to in plane_peers(pos)]
     barrier = pltpu.get_barrier_semaphore()
     for peer in peers:
         pl.semaphore_signal(barrier, inc=1, device_id=peer, device_id_type=MESH_ID)
-    pl.semaphore_wait(barrier, len(peers))
+    return lambda: pl.semaphore_wait(barrier, len(peers))
+
+
+def at_step(index, events):
+    for step, names in events.items():
+
+        @pl.when(index == step)
+        def _():
+            for name in names:
+                name()
 
 
 def remote(src, dst, send, recv, index, peer):
@@ -396,10 +412,103 @@
         self.wait(step)
         self.start(step + 1)
 
-    def drain(self):
-        for step in range(4):
+    def drain(self, count):
+        for step in range(count):
             for sem, src, _, peer in self.steps(step):
                 remote(self.view(*src), self.view(*src), self.send, self.recv, sem, peer).wait_send()
+
+
+class SmallGather(Gather):
+    def __init__(self, buf, send, recv, pos):
+        super().__init__(buf, None, send, recv, pos)
+
+    def view(self, y, z, x, c):
+        return self.buf.at[y, z, x, c]
+
+    def steps(self, step):
+        y, z, x, c = self.pos
+        if step == 0:
+            return super().steps(0)
+        every = pl.ds(0, NZ)
+        return [
+            (3 + flip, (y, every, x, c), (to[0], every, to[2], to[3]), device_at(*to)) for flip, to in plane_peers(self.pos)
+        ]
+
+
+class SmallScatter:
+    def __init__(self, source, acc, first, last, send, recv, pos):
+        self.source, self.acc, self.first, self.last = source, acc, first, last
+        self.send, self.recv, self.pos = send, recv, pos
+
+    def copies(self, step):
+        y, z, x, c = self.pos
+        every = pl.ds(0, NZ)
+        if step == 0:
+            return [
+                remote(
+                    self.source.at[to[0], every, to[2], to[3]],
+                    self.first.at[flip],
+                    self.send,
+                    self.recv,
+                    3 + flip,
+                    device_at(*to),
+                )
+                for flip, to in plane_peers(self.pos)
+            ]
+        return [
+            remote(
+                self.acc.at[lax.rem(z + k, NZ)],
+                self.last.at[k - 1],
+                self.send,
+                self.recv,
+                k - 1,
+                device_at(y, lax.rem(z + k, NZ), x, c),
+            )
+            for k in range(1, NZ)
+        ]
+
+    def start(self, step):
+        for copy in self.copies(step):
+            copy.start()
+
+    def next(self):
+        y, z, x, c = self.pos
+        total = self.source[y, :, x, c]
+        for flip, copy in enumerate(self.copies(0)):
+            copy.wait_recv()
+            total = total + self.first[flip]
+        self.acc[...] = total
+        self.start(1)
+
+    def final(self):
+        total = self.acc[self.pos[1]]
+        for k, copy in enumerate(self.copies(1)):
+            copy.wait_recv()
+            total = total + self.last[k]
+        return total
+
+    def drain(self, _):
+        for step in range(2):
+            for copy in self.copies(step):
+                copy.wait_send()
+
+
+def small_scratch():
+    tile = (8, 128)
+    return [
+        pltpu.VMEM((NY, NZ, NX, NC, *tile), F32),
+        pltpu.VMEM((NZ, *tile), F32),
+        pltpu.VMEM((NY * NX * NC - 1, NZ, *tile), F32),
+        pltpu.VMEM((NZ - 1, *tile), F32),
+    ]
+
+
+def fold(values):
+    return values[0:8] + pltpu.roll(values[8:16], LINE, 1) + pltpu.roll(values[16:24], 2 * LINE, 1)
+
+
+def unfold(tile):
+    return jnp.concatenate([tile, pltpu.roll(tile, 128 - LINE, 1), pltpu.roll(tile, 128 - 2 * LINE, 1)], axis=0)
 
 
 def gelu_parts(v):
@@ -440,18 +549,18 @@
 
 def forward_kernel(
     dims,
-    tokens,
     steps,
     gains,
     biases,
     shift2,
     hidden,
-    table,
-    qkv,
-    outw,
-    upw,
-    downw,
-    cot,
+    table_t,
+    tokens_in,
+    qkv_in,
+    outw_t,
+    upw_in,
+    downw_t,
+    cot_in,
     q_out,
     k_out,
     v_out,
@@ -466,9 +575,13 @@
     layer_out,
     weights_out,
     grads_out,
+    part_out,
     full,
     pack,
+    lines,
     stage,
+    tokens,
+    cot,
     normed,
     queries,
     keys_all,
@@ -484,9 +597,7 @@
     gpre,
     gtile,
     hid,
-    send,
-    recv,
-    local,
+    *rest,
 ):
     rows, width, per, half, ffh, ft = dims
     pos = position()
@@ -494,49 +605,71 @@
     me = device_at(y, z, x, c)[0] * NY + y
     share = width // (NZ * NX * NC * NY)
     n_ff = ffh // ft
-    greet(pos)
-
-    names = ["pack", "q", "k", "v", "o"] + [f"m{i}" for i in range(n_ff)]
-    col = {"pack": pl.ds(0, 128)}
-    for i, name in enumerate(["q", "k", "v", "o"]):
-        col[name] = pl.ds(i * half, half)
+    scatter_bufs, (send, recv, local) = rest[:-3], rest[-3:]
+
+    n_groups = half // 128
+    groups = [f"g{i}" for i in range(n_groups)]
+    names = ["pack", "hid", *groups, "o"] + [f"m{i}" for i in range(n_ff)]
+    col = {"o": pl.ds(3 * half, half)}
+    for i in range(n_groups):
+        col[f"g{i}"] = pl.ds(i * 384, 384)
     for i in range(n_ff):
         col[f"m{i}"] = pl.ds(4 * half + 2 * ft * i, 2 * ft)
-    flow = {
-        name: Gather(pack if name == "pack" else full, col[name], send.at[i], recv.at[i], pos) for i, name in enumerate(names)
-    }
-
-    for i, name in enumerate(["q", "k", "v"]):
-        full[y, z, x, c, :, col[name]] = qkv[i]
-        if name == "q":
-            flow["q"].start(0)
+    flow = {}
+    for i, name in enumerate(names):
+        if name in col:
+            flow[name] = Gather(full, col[name], send.at[i], recv.at[i], pos)
+        else:
+            flow[name] = SmallGather({"pack": pack, "hid": lines}[name], send.at[i], recv.at[i], pos)
+    ready = greet(pos)
+    copies = {}
+
+    def copy(name, src, dst):
+        copies[name] = pltpu.make_async_copy(src, dst, local.at[len(copies)])
+        copies[name].start()
+
+    def own(start, size):
+        return full.at[y, z, x, c, :, pl.ds(start, size)]
+
+    parts = {"pack": [], "hid": []}
+    for g in range(n_groups):
+        parts[f"g{g}"] = [f"g{g}{i}" for i in range(3)]
+        for i in range(3):
+            copy(f"g{g}{i}", qkv_in.at[i, :, pl.ds(128 * g, 128)], own(384 * g + 128 * i, 128))
+    copy("cot", cot_in, cot)
+    copy("tokens", tokens_in, tokens)
+    copy("o", outw_t, own(3 * half, half))
+    parts["o"] = ["o"]
+    for i in range(n_ff):
+        copy(f"u{i}", upw_in.at[:, pl.ds(ft * i, ft)], own(4 * half + 2 * ft * i, ft))
+        copy(f"d{i}", downw_t.at[:, pl.ds(ft * i, ft)], own(4 * half + 2 * ft * i + ft, ft))
+        parts[f"m{i}"] = [f"u{i}", f"d{i}"]
+
+    def launch(name):
+        for key in parts[name]:
+            copies[key].wait()
+        flow[name].start(0)
+
     stage[...] = jnp.zeros_like(stage)
     stage[0:2, 0:share] = gains[...].astype(F32)
     stage[2:7, 0:share] = biases[...].astype(F32)
     stage[7:8, 0:share] = shift2[...].astype(F32)
-    picked = (steps[...] == lax.broadcasted_iota(jnp.int32, (steps.shape[0], table.shape[0]), 1)).astype(BF16)
-    stage[32 : 32 + steps.shape[0], 0:share] = nn(picked, table[...])
-    turned = stage[...].T
-    pack[y, z, x, c, 0:share, :] = turned[0:share]
+    n_steps, n_seq = table_t.shape[1], steps.shape[1]
+    wanted = jnp.concatenate([steps[...], jnp.full((1, 128 - n_seq), -1, jnp.int32)], axis=1)
+    picked = (wanted == lax.broadcasted_iota(jnp.int32, (n_steps, 128), 0)).astype(BF16)
+    pack[y, z, x, c] = fold(stage[...].T[0:share] + pltpu.roll(nn(table_t[...], picked), 8, 1))
     hshare = hidden.shape[1]
     lane = lax.broadcasted_iota(jnp.int32, (hshare, NC * NY * hshare), 0) + hshare * (c * NY + y)
     place = (lane == lax.broadcasted_iota(jnp.int32, (hshare, NC * NY * hshare), 1)).astype(BF16)
     spread = nn(jnp.broadcast_to(hidden[...], (8, hshare)), place)
-    for j in range(spread.shape[1] // 128):
-        pack[y, z, x, c, share + j : share + j + 1, :] = spread[0:1, 128 * j : 128 * j + 128]
-    flow["pack"].start(0)
-    flow["k"].start(0)
-    flow["v"].start(0)
-    full[y, z, x, c, :, col["o"]] = outw[...].T
-    flow["o"].start(0)
-    for i in range(n_ff):
-        full[y, z, x, c, :, pl.ds(4 * half + 2 * ft * i, ft)] = upw[:, ft * i : ft * i + ft]
-        full[y, z, x, c, :, pl.ds(4 * half + 2 * ft * i + ft, ft)] = downw[ft * i : ft * i + ft, :].T
-        flow[f"m{i}"].start(0)
-
-    flow["pack"].next(0)
-    flow["q"].next(0)
-    flow["pack"].next(1)
+    n_hid = NC * NY * hshare // 128
+    pieces = [spread[0:1, 128 * j : 128 * j + 128] for j in range(n_hid)]
+    lines[y, z, x, c] = jnp.concatenate([*pieces, jnp.zeros((8 - n_hid, 128), F32)], axis=0)
+
+    ready()
+    launch("pack")
+    launch("g0")
+    copies["cot"].wait()
 
     def turn_cot(i, total):
         rb = row_block(i, 256)
@@ -545,23 +678,22 @@
         return total + sum_rows_of(block)
 
     csum_out[...] = lax.fori_loop(0, rows // 256, turn_cot, jnp.zeros((1, width), F32))
-    flow["q"].next(1)
-    flow["pack"].next(2)
-    flow["k"].next(0)
-    flow["pack"].wait(3)
+    flow["pack"].next(0)
+    flow["g0"].next(0)
+    launch("g1")
+    flow["g0"].next(1)
+    flow["pack"].wait(1)
+    flow["g1"].next(0)
+    launch("g2")
+    launch("hid")
+    launch("o")
 
     for d, (by, bz, bx, bc) in blocks():
-        middle[d * share : d * share + share, 0:128] = pack[by, bz, bx, bc, 0:share, :]
+        middle[d * share : d * share + share, 0:128] = unfold(pack[by, bz, bx, bc])
     small_out[...] = middle[0:width, 0:128].T
-    for bz in range(NZ):
-        for bx in range(NX):
-            total = pack[0, bz, bx, 0, share : share + 8, :]
-            for bc, by in ((0, 1), (1, 0), (1, 1)):
-                total = total + pack[by, bz, bx, bc, share : share + 8, :]
-            for j in range(NC * NY * hshare // 128):
-                at = (bz * NX + bx) * NC * NY * hshare + 128 * j
-                hid[0:1, at : at + 128] = total[j : j + 1]
-    embed = small_out[pl.ds(32 + me, 1), :]
+    embed = small_out[pl.ds(8 + me, 1), :]
+    copies["tokens"].wait()
+    flow["g0"].next(2)
 
     def first_norm(i, _):
         rb = row_block(i, 128)
@@ -569,96 +701,103 @@
         normed[rb, :] = (xhat * small_out[0:1, :] + small_out[2:3, :]).astype(BF16)
         return 0
 
-    flow["q"].next(2)
     lax.fori_loop(0, rows // 128, first_norm, 0)
-
-    def whole(cols):
-        return jnp.concatenate([full[by, :, :, :, :, cols].reshape(width, half) for by in range(NY)], axis=1)
-
-    def project(name, bias, factor, out):
+    copy("normed", normed, normed_out)
+    flow["g1"].next(1)
+    flow["g2"].next(0)
+    launch("m0")
+
+    def whole(cols, size):
+        return jnp.concatenate([full[by, :, :, :, :, cols].reshape(width, size) for by in range(NY)], axis=1)
+
+    def project(group):
+        cols = pl.ds(pl.multiple_of(group * 384, 128), 384)
+
         def body(i, _):
             rb = row_block(i, 512)
-            value = nn(normed[rb, :], whole(col[name]))
-            if bias is not None:
-                value = value + small_out[bias : bias + 1, :]
-            value = value.astype(BF16)
-            out[rb, :] = value * jnp.asarray(factor, BF16) if factor != 1 else value
+            value = nn(normed[rb, :], whole(cols, 384))
+            for by in range(NY):
+                to = pl.ds(pl.multiple_of((by * n_groups + group) * 128, 128), 128)
+                piece = [value[:, by * 384 + 128 * j : by * 384 + 128 * j + 128] for j in range(3)]
+                queries[rb, to] = (piece[0] + small_out[3:4, to]).astype(BF16) * jnp.asarray(HEAD_DIM**-0.5, BF16)
+                keys_all[rb, to] = piece[1].astype(BF16)
+                values_all[rb, to] = (piece[2] + small_out[4:5, to]).astype(BF16)
             return 0
 
         lax.fori_loop(0, rows // 512, body, 0)
 
-    locals_ = []
-
-    def save(src, dst, index):
-        copy = pltpu.make_async_copy(src, dst, local.at[index])
-        copy.start()
-        locals_.append(copy)
-
-    flow["k"].next(1)
-    flow["v"].next(0)
-    flow["q"].wait(3)
-    project("q", 3, HEAD_DIM**-0.5, queries)
-    flow["k"].next(2)
-    flow["v"].next(1)
-    flow["o"].next(0)
-    flow["k"].wait(3)
-    project("k", None, 1, keys_all)
-    flow["v"].next(2)
-    flow["o"].next(1)
-    flow["m0"].next(0)
-    flow["v"].wait(3)
-    project("v", 4, 1, values_all)
-    save(normed, normed_out, 0)
-    save(queries, q_out, 1)
-    save(keys_all, k_out, 2)
-    save(values_all, v_out, 3)
-
-    def attend(p, _):
-        @pl.when(p == 0)
+    def then(name, step):
+        return lambda: flow[name].next(step)
+
+    def arrived(name):
+        return lambda: flow[name].wait(3)
+
+    def off(name):
+        return lambda: launch(name)
+
+    events = {
+        (0, 1): [then("o", 0), then("hid", 0)],
+        (0, 2): [then("g1", 2)],
+        (0, 3): [then("g2", 1), off("m1")],
+        (1, 2): [then("m0", 0)],
+        (1, 3): [then("o", 1)],
+        (2, 0): [then("g2", 2)],
+        (2, 2): [off("m2")],
+        (3, 0): [then("o", 2), then("m1", 0)],
+        (3, 2): [then("m0", 1)],
+        (5, 0): [then("m2", 0), then("m1", 1)],
+    }
+
+    def attend(s, _):
+        group, by = s // NY, lax.rem(s, NY)
+        p = by * n_groups + group
+
+        @pl.when(by == 0)
         def _():
-            flow["o"].next(2)
-            flow["m0"].next(1)
-
-        @pl.when(p == 1)
-        def _():
-            flow["m1"].next(0)
-
-        @pl.when(p == 3)
-        def _():
-            flow["m0"].next(2)
-            flow["m2"].next(0)
-
-        @pl.when(p == 4)
-        def _():
-            flow["m1"].next(1)
+            at_step(group, {g: [arrived(f"g{g}")] for g in range(n_groups)})
+            project(group)
 
         cols = pl.ds(pl.multiple_of(p * 128, 128), 128)
         low = lax.broadcasted_iota(jnp.int32, (QB, 128), 1) < HEAD_DIM
         for i in range(rows // QB):
+            at_step(s, {key[0]: names for key, names in events.items() if key[1] == i})
             n = (i + 1) * QB
             rb = slice(i * QB, n)
             key, value, query = keys_all[0:n, cols], values_all[0:n, cols], queries[rb, cols]
-            outs = []
+            outs, scales = [], []
             for h in range(2):
                 scores = nt(key, jnp.where(low == (h == 0), query, jnp.zeros_like(query)))
                 top = jnp.max(scores, axis=0, keepdims=True)
                 expo = jnp.exp(scores - top)
                 total = jnp.sum(expo, axis=0, keepdims=True)
                 lse_out[pl.ds(2 * p + h, 1), rb] = top + jnp.log(total)
-                outs.append(tn((expo * (1.0 / total)).astype(BF16), value))
-            mixed[rb, cols] = jnp.where(low, outs[0], outs[1]).astype(BF16)
+                scales.append(jnp.broadcast_to(1.0 / total, (HEAD_DIM, QB)))
+                outs.append(tn(expo.astype(BF16), value))
+            scale = jnp.concatenate(scales, axis=0).T
+            mixed[rb, cols] = (jnp.where(low, outs[0], outs[1]) * scale).astype(BF16)
         return 0
 
     lax.fori_loop(0, width // 128, attend, 0)
+    copy("queries", queries, q_out)
+    copy("keys", keys_all, k_out)
+    copy("values", values_all, v_out)
     flow["o"].wait(3)
-    save(mixed, mixed_out, 4)
+    flow["m0"].next(2)
+    flow["hid"].wait(1)
+    for bz in range(NZ):
+        for bx in range(NX):
+            total = lines[0, bz, bx, 0] + lines[0, bz, bx, 1] + lines[1, bz, bx, 0] + lines[1, bz, bx, 1]
+            for j in range(n_hid):
+                at = ((bz * NX + bx) * n_hid + j) * 128
+                hid[0:1, at : at + 128] = total[j : j + 1]
+    copy("mixed", mixed, mixed_out)
     for by in range(NY):
-        save(full.at[by, :, :, :, :, pl.ds(0, 4 * half)], weights_out.at[by], 5 + by)
+        copy(f"w{by}", full.at[by, :, :, :, :, pl.ds(0, 4 * half)], weights_out.at[by])
 
     def second_norm(i, _):
         rb = row_block(i, 256)
         start_h = tokens[rb, :].astype(F32) + embed
-        value = start_h + (nt(mixed[rb, :], whole(col["o"])) + small_out[5:6, :])
+        value = start_h + (nt(mixed[rb, :], whole(col["o"], half)) + small_out[5:6, :])
         middle[rb, :] = value
         xhat, _ = moments(value)
         block = (xhat * small_out[1:2, :] + small_out[7:8, :]).astype(BF16)
@@ -667,36 +806,39 @@
         return 0
 
     lax.fori_loop(0, rows // 256, second_norm, 0)
-    save(middle, middle_out, 7)
-    flow["m1"].next(2)
+    copy("middle", middle, middle_out)
     flow["m0"].wait(3)
+    at = len(copies)
 
     def tile_copy(t, slot):
         ty, tm = lax.rem(t, NY), t // NY
         return pltpu.make_async_copy(
-            gtile.at[slot], grads_out.at[ty, :, pl.ds(pl.multiple_of(tm * 2 * ft, 128), 2 * ft)], local.at[8 + slot]
+            gtile.at[slot],
+            grads_out.at[ty, :, :, :, :, pl.ds(pl.multiple_of(tm * 2 * ft, 128), 2 * ft)],
+            local.at[at + slot],
         )
+
+    part = Scatter(
+        grads_out.at[:, :, :, :, :, pl.ds(0, 2 * ft)],
+        scatter_bufs[0],
+        scatter_bufs[1:],
+        send.at[len(names)],
+        recv.at[len(names)],
+        pos,
+        True,
+    )
+    part_load = pltpu.make_async_copy(part.source.at[:, :, :, c], part.own, local.at[at + 2])
+    tiles = NY * n_ff
 
     def tile(t, _):
         ty, tm = lax.rem(t, NY), t // NY
         slot = lax.rem(t, 2)
 
-        @pl.when(t == 1)
-        def _():
-            flow["m2"].next(1)
-
-        @pl.when(t == 2)
-        def _():
-            flow["m1"].wait(3)
-
-        @pl.when(t == 3)
-        def _():
-            flow["m2"].next(2)
-
-        @pl.when(t == 4)
-        def _():
-            flow["m2"].wait(3)
-
+        def load_part():
+            part_load.wait()
+            part.next(0)
+
+        at_step(t, {2: [arrived("m1")], 3: [then("m2", 2), load_part], 4: [arrived("m2")]})
         up_at = pl.ds(pl.multiple_of(4 * half + tm * 2 * ft, 128), ft)
         down_at = pl.ds(pl.multiple_of(4 * half + tm * 2 * ft + ft, 128), ft)
         hid_at = pl.ds(pl.multiple_of(ty * ffh + tm * ft, 128), ft)
@@ -727,36 +869,65 @@
             result[...] += more
             gsec[...] += gmore
 
-        @pl.when(t >= 2)
+        @pl.when(t > 0)
         def _():
-            tile_copy(t - 2, slot).wait()
+            tile_copy(t - 1, 1 - slot).wait()
+
+        def start_part():
+            part_load.start()
+            part.start(0)
+
+        at_step(
+            t,
+            {
+                0: [then("m2", 1)],
+                1: [then("m1", 2)],
+                2: [start_part],
+                4: [lambda: part.next(1)],
+            },
+        )
 
         def weight_grad(i, _):
-            rb = row_block(i, 256)
-            gtile[slot, rb, 0:ft] = nn(second_t[rb, :], gpre[...]).astype(BF16)
-            gtile[slot, rb, ft : 2 * ft] = nn(cot_t[rb, :], act[...]).astype(BF16)
+            rb = row_block(i, 384)
+            gz = pl.ds(i * 2, 2)
+            gtile[slot, gz, :, :, :, 0:ft] = nn(second_t[rb, :], gpre[...]).astype(BF16).reshape(2, NX, NC, per, ft)
+            gtile[slot, gz, :, :, :, ft : 2 * ft] = nn(cot_t[rb, :], act[...]).astype(BF16).reshape(2, NX, NC, per, ft)
             return 0
 
-        lax.fori_loop(0, width // 256, weight_grad, 0)
+        @pl.when(t == tiles - 1)
+        def _():
+            def finish(i, _):
+                rb = row_block(i, 128)
+                normed[rb, :] = (middle[rb, :] + (result[rb, :] + small_out[6:7, :])).astype(BF16)
+                return 0
+
+            copies["normed"].wait()
+            lax.fori_loop(0, rows // 128, finish, 0)
+            last_copies[0].start()
+            last_copies[1].start()
+
+        lax.fori_loop(0, width // 384, weight_grad, 0)
         tile_copy(t, slot).start()
         return 0
 
-    tiles = NY * n_ff
+    last_copies = [
+        pltpu.make_async_copy(normed, layer_out, local.at[at + 3]),
+        pltpu.make_async_copy(gsec, gsec_out, local.at[at + 4]),
+    ]
     lax.fori_loop(0, tiles, tile, 0)
-    save(gsec, gsec_out, 10)
-
-    def finish(i, _):
-        rb = row_block(i, 256)
-        layer_out[rb, :] = (middle[rb, :] + (result[rb, :] + small_out[6:7, :])).astype(BF16)
-        return 0
-
-    lax.fori_loop(0, rows // 256, finish, 0)
-    tile_copy(tiles - 2, 0).wait()
-    tile_copy(tiles - 1, 1).wait()
-    for copy in locals_:
-        copy.wait()
+    part.wait(2)
+    part.add(2)
+    part_save = pltpu.make_async_copy(part.own.at[y, :, x], part_out, local.at[at + 5])
+    part_save.start()
+    tile_copy(tiles - 1, (tiles - 1) % 2).wait()
+    for key in ["queries", "keys", "values", "mixed", "middle"] + [f"w{by}" for by in range(NY)]:
+        copies[key].wait()
+    for last in last_copies:
+        last.wait()
     for name in names:
-        flow[name].drain()
+        flow[name].drain(4 if name in col else 2)
+    part.drain(3)
+    part_save.wait()
 
 
 class Scatter:
@@ -843,8 +1014,8 @@
             total = total + last[k].astype(F32)
         return total
 
-    def drain(self):
-        for step in range(4):
+    def drain(self, count, first=0):
+        for step in range(first, count):
             for sem, src, dst, peer in self.copies(step):
                 remote(src, dst, self.send, self.recv, sem, peer).wait_send()
 
@@ -863,12 +1034,12 @@
 
 def backward_kernel(
     dims,
-    tokens,
-    cot,
     small,
     lse,
     ghid,
     csum,
+    tokens_in,
+    cot_in,
     q_in,
     k_in,
     v_in,
@@ -878,12 +1049,17 @@
     gsec_in,
     weights_in,
     grads_in,
+    part_in,
     gup_out,
     gdown_out,
     gout_out,
     gqkv_out,
     gpack_out,
     gtok_out,
+    tokens,
+    cot,
+    part_own,
+    part_last,
     queries,
     keys_all,
     values_all,
@@ -896,10 +1072,10 @@
     gattn,
     gattn_t,
     gval,
-    acc_k,
-    acc_v,
+    gmixed,
+    acc,
+    inner,
     sums,
-    gpack,
     gout,
     gqkv,
     *rest,
@@ -911,44 +1087,68 @@
     share = width // (NZ * NX * NC * NY)
     n_ff = ffh // ft
     n_groups = half // 128
-    names = [f"m{i}" for i in range(n_ff)] + ["o"] + [f"q{i}" for i in range(n_groups)] + ["pack"]
+    names = [f"m{i}" for i in range(n_ff)] + ["o"] + [f"q{i}" for i in range(n_groups)] + ["pack", "hid"]
     send, recv, local = rest[-3:]
     flow = {}
     for i, name in enumerate(names):
-        own, first, *others = rest[7 * i : 7 * i + 7]
+        if name == "m0":
+            continue
+        if name in ("pack", "hid"):
+            at = -11 if name == "pack" else -7
+            flow[name] = SmallScatter(*rest[at : at + 4], send.at[i], recv.at[i], pos)
+            continue
+        own, first, *others = rest[7 * i - 7 : 7 * i]
         if name[0] == "m":
             source = grads_in.at[:, :, :, :, :, pl.ds(2 * ft * i, 2 * ft)]
         else:
-            source = {"o": gout, "p": gpack}.get(name[0], None)
-            if source is None:
-                source = gqkv.at[int(name[1:])]
+            source = gout if name == "o" else gqkv.at[int(name[1:])]
         flow[name] = Scatter(source, own, [first] + others, send.at[i], recv.at[i], pos, name[0] == "m")
 
     copies = {}
 
-    def load(name, src, dst, index):
-        copies[name] = pltpu.make_async_copy(src, dst, local.at[index])
+    def load(name, src, dst):
+        copies[name] = pltpu.make_async_copy(src, dst, local.at[len(copies)])
         copies[name].start()
 
-    load("middle", middle_in, middle, 0)
-    load("gsec", gsec_in, gsec, 1)
-    for i in range(n_ff):
-        name = f"m{i}"
-        load(name, flow[name].source.at[:, :, :, c], flow[name].own, 2 + i)
-    at = 2 + n_ff
-    load("w", weights_in, weights, at)
-    load("mixed", mixed_in, mixed, at + 1)
-    load("normed", normed_in, normed, at + 2)
-    load("q", q_in, queries, at + 3)
-    load("k", k_in, keys_all, at + 4)
-    load("v", v_in, values_all, at + 5)
-    greet(pos)
-    for i in range(n_ff):
-        flow[f"m{i}"].start(0)
-    copies["middle"].wait()
-    copies["gsec"].wait()
+    ready = greet(pos)
+    n_hid = ghid.shape[1] // (NZ * NX * 128)
+    for d, (by, bz, bx, bc) in blocks():
+        start = (bz * NX + bx) * n_hid
+        pieces = [ghid[:, 128 * (start + j) : 128 * (start + j + 1)] for j in range(n_hid)]
+        flow["hid"].source[by, bz, bx, bc] = jnp.concatenate([*pieces, jnp.zeros((8 - n_hid, 128), F32)], axis=0)
+    load("part", part_in, part_own)
+    for i in range(4):
+        rb = pl.ds(i * (rows // 4), rows // 4)
+        load(f"middle{i}", middle_in.at[rb], middle.at[rb])
+        load(f"gsec{i}", gsec_in.at[rb], gsec.at[rb])
+        load(f"cot{i}", cot_in.at[rb], cot.at[rb])
+    for i in range(1, n_ff):
+        load(f"m{i}", flow[f"m{i}"].source.at[:, :, :, c], flow[f"m{i}"].own)
+    load("mixed", mixed_in, mixed)
+    load("w", weights_in, weights)
+    load("normed", normed_in, normed)
+    load("q", q_in, queries)
+    load("k", k_in, keys_all)
+    load("v", v_in, values_all)
+    load("tokens", tokens_in, tokens)
+
+    def part_copies():
+        m0 = names.index("m0")
+        return [
+            remote(
+                part_own.at[lax.rem(z + k, NZ)],
+                part_last.at[k - 1],
+                send.at[m0],
+                recv.at[m0],
+                k,
+                device_at(y, lax.rem(z + k, NZ), x, c),
+            )
+            for k in range(1, NZ)
+        ]
 
     def second_back(i, totals):
+        arrive = [lambda i=i: [copies[f"{name}{i}"].wait() for name in ("middle", "gsec", "cot")] for i in range(4)]
+        at_step(i, {rows // 512 * k: [arrive[k]] for k in range(4)})
         rb = row_block(i, 128)
         xhat, scale = moments(middle[rb, :])
         grad = gsec[rb, :]
@@ -964,20 +1164,30 @@
         )
 
     zero = jnp.zeros((1, width), F32)
-    ggain2, gshift2, gattn_sum = lax.fori_loop(0, rows // 128, second_back, (zero, zero, zero))
+    totals = lax.fori_loop(0, rows // 256, second_back, (zero, zero, zero))
+    ready()
+    for i in range(1, n_ff):
+        flow[f"m{i}"].start(0)
+    copies["part"].wait()
+    for copy in part_copies():
+        copy.start()
+    flow["hid"].start(0)
+    ggain2, gshift2, gattn_sum = lax.fori_loop(rows // 256, rows // 128, second_back, totals)
     sums[...] = jnp.zeros_like(sums)
     sums[1:2, :] = ggain2
     sums[5:6, :] = gattn_sum
     sums[6:7, :] = csum[...]
     sums[7:8, :] = gshift2
-    copies["m0"].wait()
-    flow["m0"].next(0)
+    copies["m1"].wait()
+    flow["m1"].next(0)
     copies["w"].wait()
     copies["mixed"].wait()
 
     def whole(index):
-        cols = pl.ds(index * half, half)
-        return jnp.concatenate([weights[by, :, cols] for by in range(NY)], axis=1)
+        if index == 3:
+            return jnp.concatenate([weights[by, :, pl.ds(3 * half, half)] for by in range(NY)], axis=1)
+        picks = [weights[by, :, pl.ds(384 * g + 128 * index, 128)] for by in range(NY) for g in range(n_groups)]
+        return jnp.concatenate(picks, axis=1)
 
     for by in range(NY):
         def out_grad(i, _):
@@ -991,12 +1201,13 @@
 
     def mixed_grad(i, _):
         rb = row_block(i, 512)
-        mixed[rb, :] = nn(gattn[rb, :], whole(3)).astype(BF16)
+        gmixed[rb, :] = nn(gattn[rb, :], whole(3)).astype(BF16)
         return 0
 
     lax.fori_loop(0, rows // 512, mixed_grad, 0)
-    copies["m1"].wait()
-    flow["m1"].next(0)
+    copies["m2"].wait()
+    flow["m2"].next(0)
+    flow["o"].next(0)
     copies["normed"].wait()
 
     def turn_normed(i, _):
@@ -1010,66 +1221,55 @@
     copies["v"].wait()
     gq, gk, gv = gattn, normed, gval
 
+    def then(name, step):
+        return lambda: flow[name].next(step)
+
+    events = {
+        (2, 0): [then("m1", 1)],
+        (2, 1): [then("q0", 0)],
+        (2, 2): [then("m2", 1)],
+        (3, 0): [then("o", 1), flow["hid"].next],
+        (4, 0): [then("m1", 2)],
+        (4, 1): [then("q1", 0)],
+        (4, 2): [then("q0", 1)],
+        (5, 0): [then("m2", 2)],
+        (5, 1): [then("o", 2)],
+        (5, 2): [then("q0", 2)],
+    }
+
     def attend_back(s, _):
         group, by = s // NY, lax.rem(s, NY)
         p = by * n_groups + group
 
-        @pl.when(s == 1)
-        def _():
-            copies["m2"].wait()
-            flow["m2"].next(0)
-            flow["m0"].next(1)
-
-        @pl.when(s == 2)
-        def _():
-            flow["o"].next(0)
-
-        @pl.when(s == 3)
-        def _():
-            flow["m1"].next(1)
-            flow["m0"].next(2)
-            flow["q0"].next(0)
-
-        @pl.when(s == 4)
-        def _():
-            flow["m2"].next(1)
-            flow["o"].next(1)
-
-        @pl.when(s == 5)
-        def _():
-            flow["q1"].next(0)
-            flow["m1"].next(2)
-            flow["q0"].next(1)
-
         cols = pl.ds(pl.multiple_of(p * 128, 128), 128)
-        low = lax.broadcasted_iota(jnp.int32, (QB, 128), 1) < HEAD_DIM
-        for i in range(rows // QB):
-            n = (i + 1) * QB
-            rb = slice(i * QB, n)
-            key, value = keys_all[0:n, cols], values_all[0:n, cols]
-            query, grad = queries[rb, cols], mixed[rb, cols]
-            parts, dv, dk = [], None, None
-            for h in range(2):
-                sel = low == (h == 0)
-                query_h = jnp.where(sel, query, jnp.zeros_like(query))
-                grad_h = jnp.where(sel, grad, jnp.zeros_like(grad))
-                probs = jnp.exp(nt(key, query_h) - lse[pl.ds(2 * p + h, 1), rb])
-                gprobs = nt(value, grad_h)
-                inner = jnp.sum(probs * gprobs, axis=0, keepdims=True)
-                gscores = (probs * (gprobs - inner)).astype(BF16)
-                pv, pk = nn(probs.astype(BF16), grad_h), nn(gscores, query_h)
-                dv = pv if dv is None else dv + pv
-                dk = pk if dk is None else dk + pk
-                parts.append(tn(gscores, key))
-            last = n - QB
-            if last:
-                acc_k[0:last] += dk[:last]
-                acc_v[0:last] += dv[:last]
-            acc_k[last:n] = dk[last:]
-            acc_v[last:n] = dv[last:]
-            gq[rb, cols] = (jnp.where(low, parts[0], parts[1]) * HEAD_DIM**-0.5).astype(BF16)
-        gk[:, cols] = acc_k[...].astype(BF16)
-        gv[:, cols] = acc_v[...].astype(BF16)
+        dots = (gmixed[:, cols].astype(F32) * mixed[:, cols].astype(F32)).T
+        for h in range(2):
+            inner[h : h + 1, :] = jnp.sum(dots[HEAD_DIM * h : HEAD_DIM * (h + 1)], axis=0, keepdims=True)
+        for j in range(rows // QB):
+            at_step(s, {key[0]: names for key, names in events.items() if key[1] == j})
+            kb, first = slice(j * QB, (j + 1) * QB), j * QB
+            later = rows - first
+            key, value = keys_all[kb, cols], values_all[kb, cols]
+            low = lax.broadcasted_iota(jnp.int32, (later, 128), 1) < HEAD_DIM
+
+            def two(block):
+                none = jnp.zeros_like(block)
+                return jnp.concatenate([jnp.where(low, block, none), jnp.where(low, none, block)], axis=0)
+
+            query, grad = two(queries[first:rows, cols]), two(gmixed[first:rows, cols])
+            logs = jnp.concatenate([lse[pl.ds(2 * p + h, 1), first:rows] for h in range(2)], axis=1)
+            inners = jnp.concatenate([inner[h : h + 1, first:rows] for h in range(2)], axis=1)
+            probs = jnp.exp(nt(key, query) - logs)
+            gscores = (probs * (nt(value, grad) - inners)).astype(BF16)
+            gv[kb, cols] = nn(probs.astype(BF16), grad).astype(BF16)
+            gk[kb, cols] = nn(gscores, query).astype(BF16)
+            both = tn(gscores, key)
+            more = jnp.where(low, both[:later], both[later:])
+            if j == 0:
+                acc[...] = more
+            else:
+                acc[first:rows] += more
+        gq[:, cols] = (acc[...] * HEAD_DIM**-0.5).astype(BF16)
 
         @pl.when(by == NY - 1)
         def _():
@@ -1090,12 +1290,8 @@
         return 0
 
     lax.fori_loop(0, NY * n_groups, attend_back, 0)
-    flow["q0"].next(2)
-    flow["m2"].next(2)
-    flow["o"].next(2)
-    flow["q1"].next(1)
-    flow["q2"].next(0)
-    embed = small[pl.ds(32 + me, 1), :]
+    copies["tokens"].wait()
+    embed = small[pl.ds(8 + me, 1), :]
 
     def first_back(i, totals):
         rb = row_block(i, 256)
@@ -1105,11 +1301,10 @@
         result = gsec[rb, :] + norm_back(xhat, scale, grad * small[0:1, :])
         middle[rb, :] = result
 
-        @pl.when(i == 1)
-        def _():
-            flow["q1"].next(2)
-            flow["q2"].next(1)
-
+        at_step(
+            i,
+            {0: [then("q1", 1)], 1: [then("q2", 0)], 2: [then("q1", 2)], 3: [then("q2", 1)]},
+        )
         return (
             totals[0] + sum_rows_of(grad * xhat),
             totals[1] + sum_rows_of(grad),
@@ -1123,39 +1318,82 @@
     sums[2:3, :] = gshift1
     sums[3:4, :] = q_sum
     sums[4:5, :] = v_sum
-    sums[pl.ds(32 + me, 1), :] = seq_sum
-    gtok = pltpu.make_async_copy(middle, gtok_out, local.at[at + 6])
+    sums[pl.ds(8 + me, 1), :] = seq_sum
+    gtok = pltpu.make_async_copy(middle, gtok_out, local.at[len(copies)])
     gtok.start()
     turned = sums[...].T
-    hgroup = ghid.shape[1] // (NZ * NX)
     for d, (by, bz, bx, bc) in blocks():
-        gpack[by, bz, bx, bc, 0:share, :] = turned[d * share : d * share + share]
-        for j in range(hgroup // 128):
-            start = (bz * NX + bx) * hgroup + 128 * j
-            gpack[by, bz, bx, bc, share + j : share + j + 1, :] = ghid[:, start : start + 128]
-        gpack[by, bz, bx, bc, share + hgroup // 128 :, :] = jnp.zeros((PACK_ROWS - share - hgroup // 128, 128), F32)
+        flow["pack"].source[by, bz, bx, bc] = fold(turned[d * share : d * share + share])
     flow["pack"].start(0)
-    for i in range(n_ff):
+    flow["q2"].next(2)
+    total = part_own[z].astype(F32)
+    for k, copy in enumerate(part_copies()):
+        copy.wait_recv()
+        total = total + part_last[k].astype(F32)
+    gup_out[:, 0:ft] = total[:, 0:ft]
+    gdown_out[:, 0:ft] = total[:, ft:]
+    for i in range(1, n_ff):
         total = flow[f"m{i}"].final()
         gup_out[:, ft * i : ft * i + ft] = total[:, 0:ft]
         gdown_out[:, ft * i : ft * i + ft] = total[:, ft:]
-    flow["pack"].next(0)
-    flow["q2"].next(2)
-    flow["pack"].next(1)
+    flow["pack"].next()
     gout_out[...] = flow["o"].final()
-    for g in range(n_groups - 1):
+    gpack_out[8:16] = flow["hid"].final()
+
+    def qkv_final(g):
         total = flow[f"q{g}"].final()
         for piece in range(3):
             gqkv_out[piece, :, 128 * g : 128 * g + 128] = total[:, 128 * piece : 128 * piece + 128]
-    flow["pack"].next(2)
-    g = n_groups - 1
-    total = flow[f"q{g}"].final()
-    for piece in range(3):
-        gqkv_out[piece, :, 128 * g : 128 * g + 128] = total[:, 128 * piece : 128 * piece + 128]
-    gpack_out[...] = flow["pack"].final()
+
+    for g in range(n_groups):
+        qkv_final(g)
+    gpack_out[0:8] = flow["pack"].final()
     gtok.wait()
-    for name in names:
-        flow[name].drain()
+    for copy in part_copies():
+        copy.wait_send()
+    for name in names[1:]:
+        flow[name].drain(4)
+
+
+def finish_kernel(slots, count, steps, gpack, *refs):
+    large, (gains_out, biases_out, shift_out, hidden_out, table_out) = refs[:count], refs[count : count + 5]
+    outs, bufs, (load_sem, save_sem) = refs[count + 5 : 2 * count + 5], refs[2 * count + 5 : 3 * count + 5], refs[-2:]
+    pieces = []
+    for src, buf, out in zip(large, bufs, outs):
+        cut = 4 if src.shape[0] % 512 == 0 else 1
+        size = src.shape[0] // cut
+        for k in range(cut):
+            at, n = pl.ds(k * size, size), len(pieces)
+            pieces.append(
+                (
+                    pltpu.make_async_copy(src.at[at], buf.at[at], load_sem.at[n]),
+                    pltpu.make_async_copy(buf.at[at], out.at[at], save_sem.at[n]),
+                )
+            )
+    for load, _ in pieces:
+        load.start()
+    share, hshare = gains_out.shape[1], hidden_out.shape[1]
+    features = unfold(gpack[0:8, :])
+    turned = jnp.concatenate([features, jnp.zeros((128 - share, 128), F32)], axis=0).T
+    gains_out[...] = turned[0:2, 0:share]
+    biases_out[...] = turned[2:7, 0:share]
+    shift_out[...] = turned[7:8, 0:share]
+    slot = lax.rem(lax.axis_index("dp"), NC) * NY + lax.axis_index("tensor")
+    line = jnp.concatenate([gpack[8 + j : 9 + j, :] for j in range(slots * hshare // 128)], axis=1)
+    value = line[:, 0:hshare]
+    for k in range(1, slots):
+        value = jnp.where(slot == k, line[:, hshare * k : hshare * k + hshare], value)
+    hidden_out[...] = value
+    n_steps, n_seq = table_out.shape[1], steps.shape[1]
+    picked = (steps[...] == lax.broadcasted_iota(jnp.int32, (n_steps, n_seq), 0)).astype(F32)
+    table_out[...] = lax.dot_general(
+        features[:, 8 : 8 + n_seq], picked, (((1,), (1,)), ((), ())), precision=HIGH, preferred_element_type=F32
+    )
+    for load, save in pieces:
+        load.wait()
+        save.start()
+    for _, save in pieces:
+        save.wait()
 
 
 def fast_shards(
@@ -1184,11 +1422,12 @@
     low, wide = shape((rows, width), BF16), shape((rows, width), F32)
     vm = pltpu.VMEM
     hshare = hidden_bias.shape[0]
-    n_chunks = 5 + n_ff
+    n_chunks = 3 + n_groups + n_ff
+    steps = timesteps.reshape(1, -1)
     outs = pl.pallas_call(
         functools.partial(forward_kernel, dims),
-        in_specs=[vmem] * 12,
-        out_specs=[anywhere] * 7 + [vmem] * 5 + [anywhere] * 2,
+        in_specs=[vmem] * 6 + [anywhere] * 6,
+        out_specs=[anywhere] * 7 + [vmem] * 4 + [anywhere] * 4,
         out_shape=[
             low,
             low,
@@ -1203,12 +1442,16 @@
             shape((1, width), F32),
             low,
             shape((NY, NZ, NX, NC, per, 4 * half), BF16),
-            shape((NY, width, 2 * ffh), BF16),
+            shape((NY, NZ, NX, NC, per, 2 * ffh), BF16),
+            shape((NZ, per, 2 * ft), BF16),
         ],
         scratch_shapes=[
             vm((NY, NZ, NX, NC, per, total), BF16),
-            vm((NY, NZ, NX, NC, PACK_ROWS, 128), F32),
+            vm((NY, NZ, NX, NC, 8, 128), F32),
+            vm((NY, NZ, NX, NC, 8, 128), F32),
             vm((128, 128), F32),
+            vm((rows, width), BF16),
+            vm((rows, width), BF16),
             vm((rows, width), BF16),
             vm((rows, width), BF16),
             vm((rows, width), BF16),
@@ -1222,48 +1465,52 @@
             vm((rows, width), F32),
             vm((rows, ft), BF16),
             vm((rows, ft), BF16),
-            vm((2, width, 2 * ft), BF16),
+            vm((2, NZ, NX, NC, per, 2 * ft), BF16),
             vm((1, NY * ffh), F32),
-            pltpu.SemaphoreType.DMA((n_chunks, 8)),
-            pltpu.SemaphoreType.DMA((n_chunks, 8)),
-            pltpu.SemaphoreType.DMA((11,)),
+            *scatter_scratch(per, 2 * ft, BF16),
+            pltpu.SemaphoreType.DMA((n_chunks + 1, 10)),
+            pltpu.SemaphoreType.DMA((n_chunks + 1, 10)),
+            pltpu.SemaphoreType.DMA((18 + 3 * n_groups + 2 * n_ff,)),
         ],
         compiler_params=pltpu.CompilerParams(collective_id=0, has_side_effects=True, vmem_limit_bytes=VMEM_LIMIT),
         name="layer_forward",
     )(
-        tokens,
-        timesteps.reshape(-1, 1),
+        steps,
         norm_gains,
         biases,
         second_shift.reshape(1, -1),
         hidden_bias.reshape(1, -1),
-        step_table,
+        step_table.T,
+        tokens,
         qkv_weight,
-        out_weight,
+        out_weight.T,
         up_weight,
-        down_weight,
+        down_weight.T,
         cotangent,
     )
-    q, k, v, mixed, normed, middle, gsec, small, lse, ghid, csum, layer_out, weights, grads = outs
-    chunks = [2 * ft] * n_ff + [half] * (1 + n_groups)
+    q, k, v, mixed, normed, middle, gsec, small, lse, ghid, csum, layer, weights, grads, part = outs
+    chunks = [2 * ft] * (n_ff - 1) + [half] * (1 + n_groups)
     scratch = []
     for cols in chunks:
         scratch += scatter_scratch(per, cols, BF16)
-    scratch += scatter_scratch(PACK_ROWS, 128, F32)
-    n_local = 2 + n_ff + 7
+    scratch += small_scratch() + small_scratch()
     gup, gdown, gout, gqkv, gpack, gtok = pl.pallas_call(
         functools.partial(backward_kernel, dims),
-        in_specs=[vmem] * 6 + [anywhere] * 9,
+        in_specs=[vmem] * 4 + [anywhere] * 12,
         out_specs=[vmem] * 5 + [anywhere],
         out_shape=[
             shape((per, ffh), F32),
             shape((per, ffh), F32),
             shape((per, half), F32),
             shape((3, per, half), F32),
-            shape((PACK_ROWS, 128), F32),
+            shape((16, 128), F32),
             wide,
         ],
         scratch_shapes=[
+            vm((rows, width), BF16),
+            vm((rows, width), BF16),
+            vm((NZ, per, 2 * ft), BF16),
+            vm((NZ - 1, per, 2 * ft), BF16),
             vm((rows, width), BF16),
             vm((rows, width), BF16),
             vm((rows, width), BF16),
@@ -1276,26 +1523,26 @@
             vm((rows, width), BF16),
             vm((width, rows), BF16),
             vm((rows, width), BF16),
+            vm((rows, width), BF16),
             vm((rows, 128), F32),
-            vm((rows, 128), F32),
+            vm((8, rows), F32),
             vm((128, width), F32),
-            vm((NY, NZ, NX, NC, PACK_ROWS, 128), F32),
             vm((NY, NZ, NX, NC, per, half), BF16),
             vm((n_groups, NY, NZ, NX, NC, per, 3 * 128), BF16),
             *scratch,
-            pltpu.SemaphoreType.DMA((len(chunks) + 1, 8)),
-            pltpu.SemaphoreType.DMA((len(chunks) + 1, 8)),
-            pltpu.SemaphoreType.DMA((n_local,)),
+            pltpu.SemaphoreType.DMA((len(chunks) + 3, 10)),
+            pltpu.SemaphoreType.DMA((len(chunks) + 3, 10)),
+            pltpu.SemaphoreType.DMA((20 + n_ff,)),
         ],
         compiler_params=pltpu.CompilerParams(collective_id=1, has_side_effects=True, vmem_limit_bytes=VMEM_LIMIT),
         name="layer_backward",
     )(
-        tokens,
-        cotangent,
         small,
         lse,
         ghid,
         csum,
+        tokens,
+        cotangent,
         q,
         k,
         v,
@@ -1304,26 +1551,30 @@
         middle,
         gsec,
         weights.reshape(NY, width, 4 * half),
-        grads.reshape(NY, NZ, NX, NC, per, 2 * ffh),
-    )
-    share = norm_gains.shape[1]
-    rows_small = gpack[:share, :8].T
-    hid_rows = gpack[share : share + NC * NY * hshare // 128].reshape(-1)
-    slot = lax.rem(lax.axis_index("dp"), NC) * NY + lax.axis_index("tensor")
-    grad_hidden = lax.dynamic_slice_in_dim(hid_rows, slot * hshare, hshare, 0)
-    n_seq = timesteps.shape[0]
-    picker = (jnp.arange(step_table.shape[0])[:, None] == timesteps[None, :]).astype(F32)
-    grad_table = lax.dot_general(
-        picker, gpack[:share, 32 : 32 + n_seq], (((1,), (1,)), ((), ())), precision=HIGH, preferred_element_type=F32
-    )
+        grads,
+        part,
+    )
+    share, n_steps = norm_gains.shape[1], step_table.shape[0]
+    large = (gtok, layer, gqkv, gout, gup, gdown)
+    pieces = sum(4 if array.shape[0] % 512 == 0 else 1 for array in large)
+    small_shapes = [(2, share), (5, share), (1, share), (1, hshare), (share, n_steps)]
+    large_shapes = [shape(array.shape, array.dtype) for array in large]
+    grad_gains, grad_biases, grad_shift, grad_hidden, grad_table, gtok, layer, gqkv, gout, gup, gdown = pl.pallas_call(
+        functools.partial(finish_kernel, NC * NY, len(large)),
+        in_specs=[vmem] * 2 + [anywhere] * len(large),
+        out_specs=[vmem] * 5 + [anywhere] * len(large),
+        out_shape=[shape(dims, F32) for dims in small_shapes] + large_shapes,
+        scratch_shapes=[vm(array.shape, array.dtype) for array in large] + [pltpu.SemaphoreType.DMA((pieces,))] * 2,
+        name="finish",
+    )(steps, gpack, *large)
     return (
-        layer_out,
+        layer,
         gtok,
-        rows_small[0:2],
-        rows_small[2:7],
-        rows_small[7],
-        grad_hidden,
-        grad_table,
+        grad_gains,
+        grad_biases,
+        grad_shift.reshape(share),
+        grad_hidden.reshape(hshare),
+        grad_table.T,
         gqkv,
         gout.T,
         gup,

time: 229 us -> 189 us (0.83)
  Pallas kernels: 209 us -> 188 us
  local copies, waits for them, and re-layouts: 17.3 us -> 0 us
    pallas_call x1, Pallas kernels: 92.9 us -> 75.3 us  [fast_shards(): pl.pallas_call(functools.partial(backward_kernel, dims), in_specs=[vmem]...]
    unnamed x25 -> x0, local copies, waits for them, and re-layouts: 13.2 us -> none
    pallas_call x1, Pallas kernels: 116 us -> 106 us  [fast_shards(): pl.pallas_call(functools.partial(forward_kernel, dims), in_specs=[vmem] *...]
    pallas_call x0 -> x1, Pallas kernels: none -> 6.45 us  [fast_shards(): pl.pallas_call(functools.partial(finish_kernel, NC * NY, len(large)), in_...]
where the time goes in v2:
time: 189 us
  Pallas kernels  188 us (99%)
    pallas_call x1, Pallas kernels, fast_shards(): pl.pallas_call(functools.partial(forward_kernel, dims), in_specs=[vmem] *...  106 us
    pallas_call x1, Pallas kernels, fast_shards(): pl.pallas_call(functools.partial(backward_kernel, dims), in_specs=[vmem]...  75.3 us
    pallas_call x1, Pallas kernels, fast_shards(): pl.pallas_call(functools.partial(finish_kernel, NC * NY, len(large)), in_...  6.45 us

profile of v2, /device:TPU:0, one launch (start us, length us, event | category | flops | bytes accessed | tf_op | source)
XLA Modules:
  0.0 189.0 jit_solution(762469628733029272)
XLA Ops:
  0.6 106.4 %layer_forward.1 = (bf16[1024,768]{1,0:T(8,128)(2,1)}, bf16[1024,768]{1,0:T(8,128)(2,1)}, bf16[1024,768]{1,0:T(8,128)(2,1)}, bf16[1024,768]{1,0:T(8,128)(2,1)}, ...) custom-call(s32[1,32]{1,0:T(1,128)} %bitcast.16, ...), custom_call_target="tpu_custom_call" | custom-call | tf_op jit(solution)/shard_map/layer_forward/pallas_call | solution.py:1427
  107.0 75.3 %layer_backward.1 = (f32[48,1536]{1,0:T(8,128)}, f32[48,1536]{1,0:T(8,128)}, f32[48,384]{1,0:T(8,128)}, f32[3,48,384]{2,1,0:T(8,128)}, f32[16,128]{1,0:T(8,128)}, /*index=5*/f32[1024,768]{1,0:T(8,128)}) custom-call(f32[128,768]{1,0:T(8,128)} %get-tuple-element.43.small, f32[16,1024]{1,0:T(8,128)} %get-tuple-element.44.lse, ...), custom_call_target="tpu_custom_call" | custom-call | tf_op jit(solution)/shard_map/layer_backward/pallas_call | solution.py:1497
  182.4 6.4 %finish.1 = (f32[2,24]{1,0:T(2,128)}, f32[5,24]{1,0:T(8,128)}, f32[1,24]{1,0:T(1,128)}, f32[1,96]{1,0:T(1,128)}, f32[24,1000]{1,0:T(8,128)}, /*index=5*/f32[1024...) custom-call(s32[1,32]{1,0:T(1,128)} %bitcast.17, ...), custom_call_target="tpu_custom_call" | custom-call | tf_op jit(solution)/shard_map/finish/pallas_call | solution.py:1562

commit v3 on v0

--- a/solution.py
+++ b/solution.py
@@ -1,6 +1,10 @@
+import functools
+
 import jax
 import jax.numpy as jnp
 from jax import lax
+from jax.experimental import pallas as pl
+from jax.experimental.pallas import tpu as pltpu
 from jax.sharding import PartitionSpec as P
 
 HEAD_DIM = 64
@@ -13,6 +17,7 @@
 EPS = 1e-05
 NEGATIVE = -1e30
 HIGH = lax.Precision.HIGHEST
+VMEM_LIMIT = 62 * 1024 * 1024
 
 
 def layer_norm(hidden, gain, shift):
@@ -304,6 +309,1070 @@
     )
 
 
+MESH_ID = pl.DeviceIdType.MESH
+F32, BF16 = jnp.float32, jnp.bfloat16
+NZ, NX, NC, NY = 4, 2, 2, 2
+QB = 256
+LINE = 40
+GELU_A, GELU_B = 0.7978845608028654, 0.044715
+
+
+def nt(left, right):
+    return lax.dot_general(left, right, (((1,), (1,)), ((), ())), preferred_element_type=F32)
+
+
+def nn(left, right):
+    return lax.dot_general(left, right, (((1,), (0,)), ((), ())), preferred_element_type=F32)
+
+
+def tn(left, right):
+    return lax.dot_general(left, right, (((0,), (0,)), ((), ())), preferred_element_type=F32)
+
+
+def position():
+    dp = lax.axis_index("dp")
+    return (lax.axis_index("tensor"), dp // (NX * NC), lax.rem(dp // NC, NX), lax.rem(dp, NC))
+
+
+def device_at(y, z, x, c):
+    return (z * (NX * NC) + x * NC + c, y)
+
+
+def plane_peers(pos):
+    y, z, x, c = pos
+    for flip in range(1, NY * NX * NC):
+        to = (1 - y if flip & 4 else y, z, 1 - x if flip & 2 else x, 1 - c if flip & 1 else c)
+        yield flip - 1, to
+
+
+def greet(pos):
+    y, z, x, c = pos
+    peers = [device_at(y, lax.rem(z + k, NZ), x, c) for k in range(1, NZ)]
+    peers += [device_at(*to) for _, to in plane_peers(pos)]
+    barrier = pltpu.get_barrier_semaphore()
+    for peer in peers:
+        pl.semaphore_signal(barrier, inc=1, device_id=peer, device_id_type=MESH_ID)
+    return lambda: pl.semaphore_wait(barrier, len(peers))
+
+
+def at_step(index, events):
+    for step, names in events.items():
+
+        @pl.when(index == step)
+        def _():
+            for name in names:
+                name()
+
+
+def remote(src, dst, send, recv, index, peer):
+    return pltpu.make_async_remote_copy(
+        src_ref=src,
+        dst_ref=dst,
+        send_sem=send.at[index],
+        recv_sem=recv.at[index],
+        device_id=peer,
+        device_id_type=MESH_ID,
+    )
+
+
+class Gather:
+    def __init__(self, buf, cols, send, recv, pos):
+        self.buf, self.cols, self.send, self.recv, self.pos = buf, cols, send, recv, pos
+
+    def view(self, y, z, x, c):
+        return self.buf.at[y, z, x, c, :, self.cols]
+
+    def steps(self, step):
+        y, z, x, c = self.pos
+        lo, hi, both = pl.ds(0, 2), pl.ds(2, 2), pl.ds(0, 2)
+        if step == 0:
+            return [
+                (k - 1, (y, z, x, c), (y, lax.rem(z + NZ - k, NZ), x, c), device_at(y, lax.rem(z + k, NZ), x, c))
+                for k in range(1, NZ)
+            ]
+        x_peer, y_peer = device_at(y, z, 1 - x, c), device_at(1 - y, z, x, c)
+        if step == 1:
+            return [(3, (y, lo, x, c), (y, lo, 1 - x, c), x_peer), (4, (y, hi, x, c), (1 - y, hi, x, c), y_peer)]
+        if step == 2:
+            return [
+                (5, (y, lo, both, c), (1 - y, lo, both, c), y_peer),
+                (6, (both, hi, x, c), (both, hi, 1 - x, c), x_peer),
+            ]
+        return [(7, (both, pl.ds(0, NZ), both, c), (both, pl.ds(0, NZ), both, 1 - c), device_at(y, z, x, 1 - c))]
+
+    def start(self, step):
+        for sem, src, _, peer in self.steps(step):
+            remote(self.view(*src), self.view(*src), self.send, self.recv, sem, peer).start()
+
+    def wait(self, step):
+        for sem, _, dst, peer in self.steps(step):
+            remote(self.view(*dst), self.view(*dst), self.send, self.recv, sem, peer).wait_recv()
+
+    def next(self, step):
+        self.wait(step)
+        self.start(step + 1)
+
+    count = 4
+
+    def drain(self):
+        for step in range(self.count):
+            for sem, src, _, peer in self.steps(step):
+                remote(self.view(*src), self.view(*src), self.send, self.recv, sem, peer).wait_send()
+
+
+class SmallGather(Gather):
+    count = 2
+
+    def __init__(self, buf, send, recv, pos):
+        super().__init__(buf, None, send, recv, pos)
+
+    def view(self, y, z, x, c):
+        return self.buf.at[y, z, x, c]
+
+    def steps(self, step):
+        y, z, x, c = self.pos
+        if step == 0:
+            return super().steps(0)
+        every = pl.ds(0, NZ)
+        return [
+            (3 + flip, (y, every, x, c), (to[0], every, to[2], to[3]), device_at(*to)) for flip, to in plane_peers(self.pos)
+        ]
+
+
+class SmallScatter:
+    def __init__(self, source, acc, first, last, send, recv, pos):
+        self.source, self.acc, self.first, self.last = source, acc, first, last
+        self.send, self.recv, self.pos = send, recv, pos
+
+    def copies(self, step):
+        y, z, x, c = self.pos
+        every = pl.ds(0, NZ)
+        if step == 0:
+            return [
+                remote(
+                    self.source.at[to[0], every, to[2], to[3]],
+                    self.first.at[flip],
+                    self.send,
+                    self.recv,
+                    3 + flip,
+                    device_at(*to),
+                )
+                for flip, to in plane_peers(self.pos)
+            ]
+        return [
+            remote(
+                self.acc.at[lax.rem(z + k, NZ)],
+                self.last.at[k - 1],
+                self.send,
+                self.recv,
+                k - 1,
+                device_at(y, lax.rem(z + k, NZ), x, c),
+            )
+            for k in range(1, NZ)
+        ]
+
+    def start(self, step):
+        for copy in self.copies(step):
+            copy.start()
+
+    def next(self):
+        y, z, x, c = self.pos
+        total = self.source[y, :, x, c]
+        for flip, copy in enumerate(self.copies(0)):
+            copy.wait_recv()
+            total = total + self.first[flip]
+        self.acc[...] = total
+        self.start(1)
+
+    def final(self):
+        total = self.acc[self.pos[1]]
+        for k, copy in enumerate(self.copies(1)):
+            copy.wait_recv()
+            total = total + self.last[k]
+        return total
+
+    def drain(self):
+        for step in range(2):
+            for copy in self.copies(step):
+                copy.wait_send()
+
+
+def small_scratch():
+    tile = (8, 128)
+    return [
+        pltpu.VMEM((NY, NZ, NX, NC, *tile), F32),
+        pltpu.VMEM((NZ, *tile), F32),
+        pltpu.VMEM((NY * NX * NC - 1, NZ, *tile), F32),
+        pltpu.VMEM((NZ - 1, *tile), F32),
+    ]
+
+
+def fold(values):
+    return values[0:8] + pltpu.roll(values[8:16], LINE, 1) + pltpu.roll(values[16:24], 2 * LINE, 1)
+
+
+def unfold(tile):
+    return jnp.concatenate([tile, pltpu.roll(tile, 128 - LINE, 1), pltpu.roll(tile, 128 - 2 * LINE, 1)], axis=0)
+
+
+def gelu_parts(v):
+    square = v * v
+    half = 0.5 + 0.5 * jnp.tanh(v * (GELU_A + (GELU_A * GELU_B) * square))
+    act = v * half
+    slope = half + (2.0 * act) * (1.0 - half) * (GELU_A + (3 * GELU_A * GELU_B) * square)
+    return act, slope
+
+
+def moments(hidden):
+    average = jnp.mean(hidden, axis=-1, keepdims=True)
+    centered = hidden - average
+    variance = jnp.mean(centered * centered, axis=-1, keepdims=True)
+    scale = lax.rsqrt(variance + EPS)
+    return centered * scale, scale
+
+
+def norm_back(xhat, scale, grad):
+    return (grad - jnp.mean(grad, axis=-1, keepdims=True) - xhat * jnp.mean(grad * xhat, axis=-1, keepdims=True)) * scale
+
+
+def row_block(index, size):
+    return pl.ds(pl.multiple_of(index * size, size), size)
+
+
+def sum_rows_of(values):
+    return jnp.sum(values.astype(F32), axis=0, keepdims=True)
+
+
+def blocks():
+    for z in range(NZ):
+        for x in range(NX):
+            for c in range(NC):
+                for y in range(NY):
+                    yield (z * NX + x) * NC * NY + c * NY + y, (y, z, x, c)
+
+
+class Scatter:
+    def __init__(self, source, own, bufs, send, recv, pos, loaded):
+        self.source, self.own, self.bufs = source, own, bufs
+        self.send, self.recv, self.pos, self.loaded = send, recv, pos, loaded
+
+    def copies(self, step):
+        y, z, x, c = self.pos
+        first, second_x, second_y, third_y, third_x, last = self.bufs
+        own = self.own
+        lo, hi, both = pl.ds(0, 2), pl.ds(2, 2), pl.ds(0, 2)
+        x_peer, y_peer = device_at(y, z, 1 - x, c), device_at(1 - y, z, x, c)
+        if step == 0:
+            return [(0, self.source.at[both, pl.ds(0, NZ), both, 1 - c], first, device_at(y, z, x, 1 - c))]
+        if step == 1:
+            return [(1, own.at[both, lo, 1 - x], second_x, x_peer), (2, own.at[1 - y, hi, both], second_y, y_peer)]
+        if step == 2:
+            return [(3, own.at[1 - y, lo, x], third_y, y_peer), (4, own.at[y, hi, 1 - x], third_x, x_peer)]
+        return [
+            (4 + k, own.at[y, lax.rem(z + k, NZ), x], last.at[k - 1], device_at(y, lax.rem(z + k, NZ), x, c))
+            for k in range(1, NZ)
+        ]
+
+    def start(self, step):
+        for sem, src, dst, peer in self.copies(step):
+            remote(src, dst, self.send, self.recv, sem, peer).start()
+
+    def wait(self, step):
+        for sem, src, dst, peer in self.copies(step):
+            remote(src, dst, self.send, self.recv, sem, peer).wait_recv()
+
+    def add(self, step):
+        y, z, x, c = self.pos
+        own, source = self.own, self.source
+        first, second_x, second_y, third_y, third_x, last = self.bufs
+        kind = own.dtype
+
+        def plus(left, right):
+            return (left.astype(F32) + right.astype(F32)).astype(kind)
+
+        def each(count, body):
+            def run(i, _):
+                body(i)
+                return 0
+
+            lax.fori_loop(0, count, run, 0)
+
+        if step == 0:
+
+            def body(i):
+                iy, iz, ix = i // (NZ * NX), lax.rem(i // NX, NZ), lax.rem(i, NX)
+                mine = own[iy, iz, ix] if self.loaded else source[iy, iz, ix, c]
+                own[iy, iz, ix] = plus(mine, first[iy, iz, ix])
+
+            each(NY * NZ * NX, body)
+        elif step == 1:
+
+            def body(i):
+                a, b = i // 2, lax.rem(i, 2)
+                own[a, b, x] = plus(own[a, b, x], second_x[a, b])
+                own[y, 2 + a, b] = plus(own[y, 2 + a, b], second_y[a, b])
+
+            each(4, body)
+        else:
+
+            def body(i):
+                own[y, i, x] = plus(own[y, i, x], third_y[i])
+                own[y, 2 + i, x] = plus(own[y, 2 + i, x], third_x[i])
+
+            each(2, body)
+
+    def next(self, step):
+        self.wait(step)
+        self.add(step)
+        if step == 0:
+            self.sent(0)
+        self.start(step + 1)
+
+    def sent(self, step):
+        for sem, src, dst, peer in self.copies(step):
+            remote(src, dst, self.send, self.recv, sem, peer).wait_send()
+
+    def final(self):
+        y, z, x, c = self.pos
+        last = self.bufs[5]
+        self.wait(3)
+        total = self.own[y, z, x].astype(F32)
+        for k in range(NZ - 1):
+            total = total + last[k].astype(F32)
+        return total
+
+    def drain(self):
+        for step in range(1, 4):
+            self.sent(step)
+
+
+def scatter_scratch(per, width, kind):
+    return [
+        pltpu.VMEM((NY, NZ, NX, per, width), kind),
+        pltpu.VMEM((2, 2, per, width), kind),
+        pltpu.VMEM((2, 2, per, width), kind),
+        pltpu.VMEM((2, per, width), kind),
+        pltpu.VMEM((2, per, width), kind),
+        pltpu.VMEM((NZ - 1, per, width), kind),
+    ]
+
+
+def layer_kernel(
+    dims,
+    steps,
+    gains,
+    biases,
+    shift2,
+    hidden,
+    table_t,
+    tokens_in,
+    qkv_in,
+    outw_t,
+    upw_in,
+    downw_t,
+    cot_in,
+    gup_out,
+    gdown_out,
+    gout_out,
+    gqkv_out,
+    gpack_out,
+    gtok_out,
+    layer_out,
+    middle_hbm,
+    grads_hbm,
+    small_out,
+    lse_out,
+    ghid_out,
+    full,
+    pack,
+    lines,
+    stage,
+    tokens,
+    cot,
+    normed,
+    queries,
+    keys_all,
+    values_all,
+    mixed,
+    second,
+    second_t,
+    cot_t,
+    result,
+    gsec,
+    act,
+    gpre,
+    gtile,
+    hid,
+    acc,
+    inner,
+    sums,
+    *rest,
+):
+    rows, width, per, half, ffh, ft = dims
+    pos = position()
+    y, z, x, c = pos
+    me = device_at(y, z, x, c)[0] * NY + y
+    share = width // (NZ * NX * NC * NY)
+    n_ff = ffh // ft
+    send, recv, local = rest[-3:]
+
+    n_groups = half // 128
+    groups = [f"g{i}" for i in range(n_groups)]
+    names = ["pack", "hid", *groups, "o"] + [f"m{i}" for i in range(n_ff)]
+    col = {"o": pl.ds(3 * half, half)}
+    for i in range(n_groups):
+        col[f"g{i}"] = pl.ds(i * 384, 384)
+    for i in range(n_ff):
+        col[f"m{i}"] = pl.ds(4 * half + 2 * ft * i, 2 * ft)
+    flow = {}
+    for i, name in enumerate(names):
+        if name in col:
+            flow[name] = Gather(full, col[name], send.at[i], recv.at[i], pos)
+        else:
+            flow[name] = SmallGather({"pack": pack, "hid": lines}[name], send.at[i], recv.at[i], pos)
+    ready = greet(pos)
+    copies = {}
+
+    def copy(name, src, dst):
+        copies[name] = pltpu.make_async_copy(src, dst, local.at[len(copies)])
+        copies[name].start()
+
+    def own(start, size):
+        return full.at[y, z, x, c, :, pl.ds(start, size)]
+
+    parts = {"pack": [], "hid": []}
+    for g in range(n_groups):
+        parts[f"g{g}"] = [f"g{g}{i}" for i in range(3)]
+        for i in range(3):
+            copy(f"g{g}{i}", qkv_in.at[i, :, pl.ds(128 * g, 128)], own(384 * g + 128 * i, 128))
+    copy("cot", cot_in, cot)
+    copy("tokens", tokens_in, tokens)
+    copy("o", outw_t, own(3 * half, half))
+    parts["o"] = ["o"]
+    for i in range(n_ff):
+        copy(f"u{i}", upw_in.at[:, pl.ds(ft * i, ft)], own(4 * half + 2 * ft * i, ft))
+        copy(f"d{i}", downw_t.at[:, pl.ds(ft * i, ft)], own(4 * half + 2 * ft * i + ft, ft))
+        parts[f"m{i}"] = [f"u{i}", f"d{i}"]
+
+    def launch(name):
+        for key in parts[name]:
+            copies[key].wait()
+        flow[name].start(0)
+
+    stage[...] = jnp.zeros_like(stage)
+    stage[0:2, 0:share] = gains[...].astype(F32)
+    stage[2:7, 0:share] = biases[...].astype(F32)
+    stage[7:8, 0:share] = shift2[...].astype(F32)
+    n_steps, n_seq = table_t.shape[1], steps.shape[1]
+    wanted = jnp.concatenate([steps[...], jnp.full((1, 128 - n_seq), -1, jnp.int32)], axis=1)
+    picked = (wanted == lax.broadcasted_iota(jnp.int32, (n_steps, 128), 0)).astype(BF16)
+    pack[y, z, x, c] = fold(stage[...].T[0:share] + pltpu.roll(nn(table_t[...], picked), 8, 1))
+    hshare = hidden.shape[1]
+    lane = lax.broadcasted_iota(jnp.int32, (hshare, NC * NY * hshare), 0) + hshare * (c * NY + y)
+    place = (lane == lax.broadcasted_iota(jnp.int32, (hshare, NC * NY * hshare), 1)).astype(BF16)
+    spread = nn(jnp.broadcast_to(hidden[...], (8, hshare)), place)
+    n_hid = NC * NY * hshare // 128
+    pieces = [spread[0:1, 128 * j : 128 * j + 128] for j in range(n_hid)]
+    lines[y, z, x, c] = jnp.concatenate([*pieces, jnp.zeros((8 - n_hid, 128), F32)], axis=0)
+
+    ready()
+    launch("pack")
+    launch("g0")
+    copies["cot"].wait()
+
+    def turn_cot(i, total):
+        rb = row_block(i, 256)
+        block = cot[rb, :]
+        cot_t[:, rb] = block.T
+        return total + sum_rows_of(block)
+
+    csum = lax.fori_loop(0, rows // 256, turn_cot, jnp.zeros((1, width), F32))
+    sums[...] = jnp.zeros_like(sums)
+    sums[6:7, :] = csum
+    flow["pack"].next(0)
+    flow["g0"].next(0)
+    launch("g1")
+    flow["g0"].next(1)
+    flow["pack"].wait(1)
+    flow["g1"].next(0)
+    launch("g2")
+    launch("hid")
+    launch("o")
+
+    for d, (by, bz, bx, bc) in blocks():
+        result[d * share : d * share + share, 0:128] = unfold(pack[by, bz, bx, bc])
+    small_out[...] = result[0:width, 0:128].T
+    embed = small_out[pl.ds(8 + me, 1), :]
+    copies["tokens"].wait()
+
+    def first_norm(i, _):
+        rb = row_block(i, 128)
+        xhat, _ = moments(tokens[rb, :].astype(F32) + embed)
+        normed[rb, :] = (xhat * small_out[0:1, :] + small_out[2:3, :]).astype(BF16)
+        return 0
+
+    lax.fori_loop(0, rows // 128, first_norm, 0)
+    flow["g0"].next(2)
+    flow["g1"].next(1)
+    flow["g2"].next(0)
+    launch("m0")
+
+    def whole(cols, size):
+        return jnp.concatenate([full[by, :, :, :, :, cols].reshape(width, size) for by in range(NY)], axis=1)
+
+    def project(group):
+        cols = pl.ds(pl.multiple_of(group * 384, 128), 384)
+
+        def body(i, _):
+            rb = row_block(i, 512)
+            value = nn(normed[rb, :], whole(cols, 384))
+            for by in range(NY):
+                to = pl.ds(pl.multiple_of((by * n_groups + group) * 128, 128), 128)
+                piece = [value[:, by * 384 + 128 * j : by * 384 + 128 * j + 128] for j in range(3)]
+                queries[rb, to] = (piece[0] + small_out[3:4, to]).astype(BF16) * jnp.asarray(HEAD_DIM**-0.5, BF16)
+                keys_all[rb, to] = piece[1].astype(BF16)
+                values_all[rb, to] = (piece[2] + small_out[4:5, to]).astype(BF16)
+            return 0
+
+        lax.fori_loop(0, rows // 512, body, 0)
+
+    def then(name, step):
+        return lambda: flow[name].next(step)
+
+    def back(name, step):
+        return lambda: sums_of[name].next(step)
+
+    def arrived(name):
+        return lambda: flow[name].wait(3)
+
+    def off(name):
+        return lambda: launch(name)
+
+    events = {
+        1: [then("g1", 2), then("g2", 1), then("o", 0), then("hid", 0)],
+        3: [then("g2", 2), then("o", 1)],
+        4: [then("m0", 1)],
+        5: [then("o", 2), then("m1", 0), off("m2")],
+    }
+    between = {1: [then("m0", 0), off("m1")]}
+
+    def attend(s, _):
+        group, by = s // NY, lax.rem(s, NY)
+        p = by * n_groups + group
+
+        @pl.when(by == 0)
+        def _():
+            at_step(group, {g: [arrived(f"g{g}")] for g in range(n_groups)})
+            project(group)
+            at_step(group, between)
+
+        at_step(s, events)
+        cols = pl.ds(pl.multiple_of(p * 128, 128), 128)
+        low = lax.broadcasted_iota(jnp.int32, (QB, 128), 1) < HEAD_DIM
+        for i in range(rows // QB):
+            n = (i + 1) * QB
+            rb = slice(i * QB, n)
+            key, value, query = keys_all[0:n, cols], values_all[0:n, cols], queries[rb, cols]
+            outs, scales = [], []
+            for h in range(2):
+                scores = nt(key, jnp.where(low == (h == 0), query, jnp.zeros_like(query)))
+                top = jnp.max(scores, axis=0, keepdims=True)
+                expo = jnp.exp(scores - top)
+                total = jnp.sum(expo, axis=0, keepdims=True)
+                lse_out[pl.ds(2 * p + h, 1), rb] = top + jnp.log(total)
+                scales.append(jnp.broadcast_to(1.0 / total, (HEAD_DIM, QB)))
+                outs.append(tn(expo.astype(BF16), value))
+            scale = jnp.concatenate(scales, axis=0).T
+            mixed[rb, cols] = (jnp.where(low, outs[0], outs[1]) * scale).astype(BF16)
+        return 0
+
+    lax.fori_loop(0, width // 128, attend, 0)
+    flow["o"].wait(3)
+    flow["hid"].wait(1)
+    for bz in range(NZ):
+        for bx in range(NX):
+            total = lines[0, bz, bx, 0] + lines[0, bz, bx, 1] + lines[1, bz, bx, 0] + lines[1, bz, bx, 1]
+            for j in range(n_hid):
+                at = ((bz * NX + bx) * n_hid + j) * 128
+                hid[0:1, at : at + 128] = total[j : j + 1]
+
+    def second_norm(i, _):
+        at_step(i, {2: [then("m0", 2)]})
+        rb = row_block(i, 256)
+        start_h = tokens[rb, :].astype(F32) + embed
+        value = start_h + (nt(mixed[rb, :], whole(col["o"], half)) + small_out[5:6, :])
+        result[rb, :] = value
+        gsec[rb, :] = jnp.zeros_like(value)
+        xhat, _ = moments(value)
+        block = (xhat * small_out[1:2, :] + small_out[7:8, :]).astype(BF16)
+        second[rb, :] = block
+        second_t[:, rb] = block.T
+        return 0
+
+    lax.fori_loop(0, rows // 256, second_norm, 0)
+    copy("middle", result, middle_hbm)
+    flow["m1"].next(1)
+    flow["m0"].wait(3)
+    copies["middle"].wait()
+    at = len(copies)
+
+    free = 4 * half
+    half_f = 2 * ft
+    places = {"m0": (0, free, half_f), "m1": (1, free, half_f), "m2": (0, free + half_f, half_f), "o": (1, free + half_f, half)}
+    for g in range(n_groups):
+        places[f"q{g}"] = (g % 2, free + 2 * half_f + 384 * (g // 2), 384)
+    sums_of = {}
+    for i, name in enumerate([*places, "pack", "hid"]):
+        sems = (send.at[len(names) + i], recv.at[len(names) + i], pos)
+        if name in places:
+            core, start, size = places[name]
+            own_view = full.at[:, :, :, core, :, pl.ds(start, size)]
+            bufs = rest[6 * i : 6 * i + 6]
+            if name[0] == "m":
+                source = grads_hbm.at[:, :, :, :, :, pl.ds(half_f * i, half_f)]
+            else:
+                source = gtile.at[:, :, :, :, :, pl.ds(0 if name in ("o", "q1") else half, 384)]
+            sums_of[name] = Scatter(source, own_view, bufs, *sems, name[0] == "m")
+        else:
+            sums_of[name] = SmallScatter(*(rest[-11:-7] if name == "pack" else rest[-7:-3]), *sems)
+    loads = {
+        name: pltpu.make_async_copy(sums_of[name].source.at[:, :, :, c], sums_of[name].own, local.at[at + 2 + i])
+        for i, name in enumerate(["m0", "m1", "m2"])
+    }
+
+    def tile_copy(t, slot):
+        ty, tm = lax.rem(t, NY), t // NY
+        return pltpu.make_async_copy(
+            gtile.at[slot],
+            grads_hbm.at[ty, :, :, :, :, pl.ds(pl.multiple_of(tm * 2 * ft, 128), 2 * ft)],
+            local.at[at + slot],
+        )
+
+    tiles = NY * n_ff
+
+    def tile(t, _):
+        ty, tm = lax.rem(t, NY), t // NY
+        slot = lax.rem(t, 2)
+
+        def begin(name):
+            loads[name].start()
+            sums_of[name].start(0)
+
+        def first_sum(name):
+            loads[name].wait()
+            sums_of[name].next(0)
+
+        def reuse():
+            tile_copy(t - 2, slot).wait()
+
+        def reuse_both():
+            tile_copy(t - 2, slot).wait()
+            tile_copy(t - 1, 1 - slot).wait()
+
+        at_step(
+            t,
+            {
+                1: [then("m2", 0)],
+                2: [flow["m0"].drain, reuse_both, lambda: begin("m0"), then("m2", 1), arrived("m1")],
+                3: [lambda: first_sum("m0")],
+                4: [reuse_both, lambda: begin("m1"), arrived("m2")],
+                5: [back("m0", 1), lambda: first_sum("m1")],
+            },
+        )
+
+        up_at = pl.ds(pl.multiple_of(4 * half + tm * 2 * ft, 128), ft)
+        down_at = pl.ds(pl.multiple_of(4 * half + tm * 2 * ft + ft, 128), ft)
+        hid_at = pl.ds(pl.multiple_of(ty * ffh + tm * ft, 128), ft)
+
+        def up():
+            return full[ty, :, :, :, :, up_at].reshape(width, ft)
+
+        def down():
+            return full[ty, :, :, :, :, down_at].reshape(width, ft)
+
+        pre = nn(second[...], up()) + hid[:, hid_at]
+        gact = nn(cot[...], down())
+        value, slope = gelu_parts(pre)
+        act[...] = value.astype(BF16)
+        grad = (gact * slope).astype(BF16)
+        gpre[...] = grad
+        ghid_out[:, hid_at] = sum_rows_of(grad)
+        result[...] += nt(act[...], down())
+        gsec[...] += nt(gpre[...], up())
+
+        def results():
+            second[...] = (result[...] + small_out[6:7, :]).astype(BF16)
+            layer_save.start()
+            middle_load.start()
+
+        at_step(t, {1: [then("m1", 2)], 3: [then("m2", 2)], tiles - 1: [results]})
+
+        turn = (NZ, NX, NC, per, ft)
+        gtile[slot, :, :, :, :, 0:ft] = nn(second_t[...], gpre[...]).astype(BF16).reshape(turn)
+        gtile[slot, :, :, :, :, ft : 2 * ft] = nn(cot_t[...], act[...]).astype(BF16).reshape(turn)
+        tile_copy(t, slot).start()
+        return 0
+
+    layer_save = pltpu.make_async_copy(second, layer_out, local.at[at + 5])
+    middle_load = pltpu.make_async_copy(middle_hbm, result, local.at[at + 6])
+    lax.fori_loop(0, tiles, tile, 0)
+    flow["m1"].drain()
+    flow["m2"].drain()
+    tile_copy(tiles - 2, 0).wait()
+    tile_copy(tiles - 1, 1).wait()
+    loads["m2"].start()
+    sums_of["m2"].start(0)
+    reload = [
+        pltpu.make_async_copy(tokens_in.at[:, pl.ds(0, ft)], act, local.at[at + 7]),
+        pltpu.make_async_copy(tokens_in.at[:, pl.ds(ft, width - ft)], gpre.at[:, pl.ds(0, width - ft)], local.at[at + 8]),
+    ]
+    for load in reload:
+        load.start()
+    for d, (by, bz, bx, bc) in blocks():
+        start = (bz * NX + bx) * n_hid
+        pieces = [ghid_out[:, 128 * (start + j) : 128 * (start + j + 1)] for j in range(n_hid)]
+        sums_of["hid"].source[by, bz, bx, bc] = jnp.concatenate([*pieces, jnp.zeros((8 - n_hid, 128), F32)], axis=0)
+    sums_of["hid"].start(0)
+    layer_save.wait()
+    middle_load.wait()
+    gattn, gattn_t, normed_t, gmixed = second, cot_t, second_t, tokens
+    gq, gk, gv = second, normed, cot
+    def second_back(i, totals):
+        rb = row_block(i, 128)
+        xhat, scale = moments(result[rb, :])
+        grad = gsec[rb, :]
+        total = cot[rb, :].astype(F32) + norm_back(xhat, scale, grad * small_out[1:2, :])
+        gsec[rb, :] = total
+        low = total.astype(BF16)
+        gattn[rb, :] = low
+        gattn_t[:, rb] = low.T
+        return (
+            totals[0] + sum_rows_of(grad * xhat),
+            totals[1] + sum_rows_of(grad),
+            totals[2] + sum_rows_of(low),
+        )
+
+    zero = jnp.zeros((1, width), F32)
+    ggain2, gshift2, gattn_sum = lax.fori_loop(0, rows // 128, second_back, (zero, zero, zero))
+    sums[1:2, :] = ggain2
+    sums[5:6, :] = gattn_sum
+    sums[7:8, :] = gshift2
+
+    def weight(index):
+        picks = [
+            full[by, :, :, :, :, pl.ds(384 * g + 128 * index, 128)].reshape(width, 128)
+            for by in range(NY)
+            for g in range(n_groups)
+        ]
+        return jnp.concatenate(picks, axis=1)
+
+    for by in range(NY):
+        def out_grad(i, _):
+            rb = row_block(i, 384)
+            part = nn(gattn_t[rb, :], mixed[:, by * half : by * half + half]).astype(BF16)
+            gtile[by, pl.ds(i * 2, 2), :, :, :, 0:half] = part.reshape(2, NX, NC, per, half)
+            return 0
+
+        lax.fori_loop(0, width // 384, out_grad, 0)
+    sums_of["o"].start(0)
+    loads["m2"].wait()
+    sums_of["m2"].next(0)
+    sums_of["m0"].next(2)
+
+    def mixed_grad(i, _):
+        rb = row_block(i, 512)
+        gmixed[rb, :] = nn(gattn[rb, :], whole(col["o"], half)).astype(BF16)
+        return 0
+
+    lax.fori_loop(0, rows // 512, mixed_grad, 0)
+    sums_of["m1"].next(1)
+    sums_of["o"].next(0)
+
+    def turn_normed(i, _):
+        rb = row_block(i, 256)
+        normed_t[:, rb] = normed[rb, :].T
+        return 0
+
+    lax.fori_loop(0, rows // 256, turn_normed, 0)
+    events_back = {
+        2: [back("m1", 2)],
+        3: [back("q0", 0), back("m2", 1)],
+        4: [back("o", 1), back("m2", 2), sums_of["hid"].next],
+        5: [back("q1", 0), back("q0", 1)],
+    }
+
+    def attend_back(s, _):
+        group, by = s // NY, lax.rem(s, NY)
+        p = by * n_groups + group
+        at_step(s, events_back)
+        cols = pl.ds(pl.multiple_of(p * 128, 128), 128)
+        dots = (gmixed[:, cols].astype(F32) * mixed[:, cols].astype(F32)).T
+        for h in range(2):
+            inner[h : h + 1, :] = jnp.sum(dots[HEAD_DIM * h : HEAD_DIM * (h + 1)], axis=0, keepdims=True)
+        for j in range(rows // QB):
+            kb, first = slice(j * QB, (j + 1) * QB), j * QB
+            later = rows - first
+            key, value = keys_all[kb, cols], values_all[kb, cols]
+            low = lax.broadcasted_iota(jnp.int32, (later, 128), 1) < HEAD_DIM
+
+            def two(block):
+                none = jnp.zeros_like(block)
+                return jnp.concatenate([jnp.where(low, block, none), jnp.where(low, none, block)], axis=0)
+
+            query, grad = two(queries[first:rows, cols]), two(gmixed[first:rows, cols])
+            logs = jnp.concatenate([lse_out[pl.ds(2 * p + h, 1), first:rows] for h in range(2)], axis=1)
+            inners = jnp.concatenate([inner[h : h + 1, first:rows] for h in range(2)], axis=1)
+            probs = jnp.exp(nt(key, query) - logs)
+            gscores = (probs * (nt(value, grad) - inners)).astype(BF16)
+            gv[kb, cols] = nn(probs.astype(BF16), grad).astype(BF16)
+            gk[kb, cols] = nn(gscores, query).astype(BF16)
+            both = tn(gscores, key)
+            more = jnp.where(low, both[:later], both[later:])
+            if j == 0:
+                acc[...] = more
+            else:
+                acc[first:rows] += more
+        gq[:, cols] = (acc[...] * HEAD_DIM**-0.5).astype(BF16)
+
+        @pl.when(by == NY - 1)
+        def _():
+            offset = lax.rem(group + 1, 2) * half
+            for piece, source in enumerate((gq, gk, gv)):
+                pick = jnp.concatenate(
+                    [source[:, pl.ds(pl.multiple_of((b * n_groups + group) * 128, 128), 128)] for b in range(NY)], axis=1
+                )
+                part = nn(normed_t[...], pick).astype(BF16)
+                for b in range(NY):
+                    to = pl.ds(pl.multiple_of(offset + piece * 128, 128), 128)
+                    gtile[b, :, :, :, :, to] = part[:, b * 128 : b * 128 + 128].reshape(NZ, NX, NC, per, 128)
+            at_step(group, {g: [lambda g=g: sums_of[f"q{g}"].start(0)] for g in range(n_groups)})
+
+        return 0
+
+    lax.fori_loop(0, NY * n_groups, attend_back, 0)
+    sums_of["o"].next(2)
+    for load in reload:
+        load.wait()
+
+    def first_back(i, totals):
+        rb = row_block(i, 256)
+        block = jnp.concatenate([act[rb, :], gpre[rb, 0 : width - ft]], axis=1)
+        xhat, scale = moments(block.astype(F32) + embed)
+        q_rows, k_rows, v_rows = gq[rb, :], gk[rb, :], gv[rb, :]
+        grad = nt(q_rows, weight(0)) + nt(k_rows, weight(1)) + nt(v_rows, weight(2))
+        total = gsec[rb, :] + norm_back(xhat, scale, grad * small_out[0:1, :])
+        result[rb, :] = total
+
+        at_step(
+            i,
+            {0: [back("q0", 2)], 1: [back("q1", 1), back("q2", 0)], 2: [back("q1", 2)], 3: [back("q2", 1)]},
+        )
+        return (
+            totals[0] + sum_rows_of(grad * xhat),
+            totals[1] + sum_rows_of(grad),
+            totals[2] + sum_rows_of(q_rows),
+            totals[3] + sum_rows_of(v_rows),
+            totals[4] + sum_rows_of(total),
+        )
+
+    ggain1, gshift1, q_sum, v_sum, seq_sum = lax.fori_loop(0, rows // 256, first_back, (zero,) * 5)
+    sums[0:1, :] = ggain1
+    sums[2:3, :] = gshift1
+    sums[3:4, :] = q_sum
+    sums[4:5, :] = v_sum
+    sums[pl.ds(8 + me, 1), :] = seq_sum
+    gtok = pltpu.make_async_copy(result, gtok_out, local.at[at + 9])
+    gtok.start()
+    turned = sums[...].T
+    for d, (by, bz, bx, bc) in blocks():
+        sums_of["pack"].source[by, bz, bx, bc] = fold(turned[d * share : d * share + share])
+    sums_of["pack"].start(0)
+    sums_of["q2"].next(2)
+    for i in range(n_ff):
+        total = sums_of[f"m{i}"].final()
+        gup_out[:, ft * i : ft * i + ft] = total[:, 0:ft]
+        gdown_out[:, ft * i : ft * i + ft] = total[:, ft:]
+    sums_of["pack"].next()
+    gout_out[...] = sums_of["o"].final()
+    gpack_out[8:16] = sums_of["hid"].final()
+    for g in range(n_groups):
+        total = sums_of[f"q{g}"].final()
+        for piece in range(3):
+            gqkv_out[piece, :, 128 * g : 128 * g + 128] = total[:, 128 * piece : 128 * piece + 128]
+    gpack_out[0:8] = sums_of["pack"].final()
+    gtok.wait()
+    for name in ["pack", "hid", *groups, "o"]:
+        flow[name].drain()
+    for each in sums_of.values():
+        each.drain()
+
+
+def finish_kernel(slots, count, steps, gpack, *refs):
+    large, (gains_out, biases_out, shift_out, hidden_out, table_out) = refs[:count], refs[count : count + 5]
+    outs, bufs, (load_sem, save_sem) = refs[count + 5 : 2 * count + 5], refs[2 * count + 5 : 3 * count + 5], refs[-2:]
+    pieces = []
+    for src, buf, out in zip(large, bufs, outs):
+        cut = 4 if src.shape[0] % 512 == 0 else 1
+        size = src.shape[0] // cut
+        for k in range(cut):
+            at, n = pl.ds(k * size, size), len(pieces)
+            pieces.append(
+                (
+                    pltpu.make_async_copy(src.at[at], buf.at[at], load_sem.at[n]),
+                    pltpu.make_async_copy(buf.at[at], out.at[at], save_sem.at[n]),
+                )
+            )
+    for load, _ in pieces:
+        load.start()
+    share, hshare = gains_out.shape[1], hidden_out.shape[1]
+    features = unfold(gpack[0:8, :])
+    turned = jnp.concatenate([features, jnp.zeros((128 - share, 128), F32)], axis=0).T
+    gains_out[...] = turned[0:2, 0:share]
+    biases_out[...] = turned[2:7, 0:share]
+    shift_out[...] = turned[7:8, 0:share]
+    slot = lax.rem(lax.axis_index("dp"), NC) * NY + lax.axis_index("tensor")
+    line = jnp.concatenate([gpack[8 + j : 9 + j, :] for j in range(slots * hshare // 128)], axis=1)
+    value = line[:, 0:hshare]
+    for k in range(1, slots):
+        value = jnp.where(slot == k, line[:, hshare * k : hshare * k + hshare], value)
+    hidden_out[...] = value
+    n_steps, n_seq = table_out.shape[1], steps.shape[1]
+    picked = (steps[...] == lax.broadcasted_iota(jnp.int32, (n_steps, n_seq), 0)).astype(F32)
+    table_out[...] = lax.dot_general(
+        features[:, 8 : 8 + n_seq], picked, (((1,), (1,)), ((), ())), precision=HIGH, preferred_element_type=F32
+    )
+    for load, save in pieces:
+        load.wait()
+        save.start()
+    for _, save in pieces:
+        save.wait()
+
+
+def fast_shards(
+    tokens,
+    timesteps,
+    norm_gains,
+    biases,
+    second_shift,
+    hidden_bias,
+    step_table,
+    qkv_weight,
+    out_weight,
+    up_weight,
+    down_weight,
+    cotangent,
+):
+    rows, width = tokens.shape
+    _, per, half = qkv_weight.shape
+    ffh = up_weight.shape[1]
+    ft = 512
+    dims = (rows, width, per, half, ffh, ft)
+    n_ff, n_groups = ffh // ft, half // 128
+    total = 4 * half + 2 * ffh
+    vmem, anywhere = pl.BlockSpec(memory_space=pltpu.VMEM), pl.BlockSpec(memory_space=pl.ANY)
+    shape = jax.ShapeDtypeStruct
+    low, wide = shape((rows, width), BF16), shape((rows, width), F32)
+    vm = pltpu.VMEM
+    hshare = hidden_bias.shape[0]
+    steps = timesteps.reshape(1, -1)
+    chunks = [2 * ft] * n_ff + [half] * (1 + n_groups)
+    scratch = []
+    for cols in chunks:
+        scratch += scatter_scratch(per, cols, BF16)
+    n_flows = 3 + n_groups + n_ff + len(chunks) + 2
+    gup, gdown, gout, gqkv, gpack, gtok, layer, _, _ = pl.pallas_call(
+        functools.partial(layer_kernel, dims),
+        in_specs=[vmem] * 6 + [anywhere] * 6,
+        out_specs=[vmem] * 5 + [anywhere] * 4,
+        out_shape=[
+            shape((per, ffh), F32),
+            shape((per, ffh), F32),
+            shape((per, half), F32),
+            shape((3, per, half), F32),
+            shape((16, 128), F32),
+            wide,
+            low,
+            wide,
+            shape((NY, NZ, NX, NC, per, 2 * ffh), BF16),
+        ],
+        scratch_shapes=[
+            vm((128, width), F32),
+            vm((16, rows), F32),
+            vm((1, NY * ffh), F32),
+            vm((NY, NZ, NX, NC, per, total), BF16),
+            vm((NY, NZ, NX, NC, 8, 128), F32),
+            vm((NY, NZ, NX, NC, 8, 128), F32),
+            vm((128, 128), F32),
+            vm((rows, width), BF16),
+            vm((rows, width), BF16),
+            vm((rows, width), BF16),
+            vm((rows, width), BF16),
+            vm((rows, width), BF16),
+            vm((rows, width), BF16),
+            vm((rows, width), BF16),
+            vm((rows, width), BF16),
+            vm((width, rows), BF16),
+            vm((width, rows), BF16),
+            vm((rows, width), F32),
+            vm((rows, width), F32),
+            vm((rows, ft), BF16),
+            vm((rows, ft), BF16),
+            vm((2, NZ, NX, NC, per, 2 * ft), BF16),
+            vm((1, NY * ffh), F32),
+            vm((rows, 128), F32),
+            vm((8, rows), F32),
+            vm((128, width), F32),
+            *scratch,
+            *small_scratch(),
+            *small_scratch(),
+            pltpu.SemaphoreType.DMA((n_flows, 10)),
+            pltpu.SemaphoreType.DMA((n_flows, 10)),
+            pltpu.SemaphoreType.DMA((14 + 3 * n_groups + 2 * n_ff,)),
+        ],
+        compiler_params=pltpu.CompilerParams(collective_id=0, has_side_effects=True, vmem_limit_bytes=VMEM_LIMIT),
+        name="layer",
+    )(
+        steps,
+        norm_gains,
+        biases,
+        second_shift.reshape(1, -1),
+        hidden_bias.reshape(1, -1),
+        step_table.T,
+        tokens,
+        qkv_weight,
+        out_weight.T,
+        up_weight,
+        down_weight.T,
+        cotangent,
+    )
+    share, n_steps = norm_gains.shape[1], step_table.shape[0]
+    large = (gtok, layer, gqkv, gout, gup, gdown)
+    pieces = sum(4 if array.shape[0] % 512 == 0 else 1 for array in large)
+    small_shapes = [(2, share), (5, share), (1, share), (1, hshare), (share, n_steps)]
+    large_shapes = [shape(array.shape, array.dtype) for array in large]
+    grad_gains, grad_biases, grad_shift, grad_hidden, grad_table, gtok, layer, gqkv, gout, gup, gdown = pl.pallas_call(
+        functools.partial(finish_kernel, NC * NY, len(large)),
+        in_specs=[vmem] * 2 + [anywhere] * len(large),
+        out_specs=[vmem] * 5 + [anywhere] * len(large),
+        out_shape=[shape(dims, F32) for dims in small_shapes] + large_shapes,
+        scratch_shapes=[vm(array.shape, array.dtype) for array in large] + [pltpu.SemaphoreType.DMA((pieces,))] * 2,
+        name="finish",
+    )(steps, gpack, *large)
+    return (
+        layer,
+        gtok,
+        grad_gains,
+        grad_biases,
+        grad_shift.reshape(share),
+        grad_hidden.reshape(hshare),
+        grad_table.T,
+        gqkv,
+        gout.T,
+        gup,
+        gdown.T,
+    )
+
+
 def solution(mesh):
     in_specs = (
         P(("dp", "tensor"), None),
@@ -332,4 +1401,5 @@
         P("dp", "tensor"),
         P("tensor", "dp"),
     )
-    return jax.shard_map(shards, mesh=mesh, in_specs=in_specs, out_specs=out_specs, check_vma=False)
+    fast = mesh.shape["dp"] == NZ * NX * NC and mesh.shape["tensor"] == NY
+    return jax.shard_map(fast_shards if fast else shards, mesh=mesh, in_specs=in_specs, out_specs=out_specs, check_vma=False)

time: 1440 us -> 172 us (0.12)
  waiting for transfers between devices: 696 us -> 0 us
  blocking collectives: 235 us -> 0 us
  matrix products: 210 us -> 0 us
  Pallas kernels: 0 us -> 171 us
  local copies, waits for them, and re-layouts: 156 us -> 0 us
  other arithmetic: 94.2 us -> 0 us
  loops' own time: 22.2 us -> 0 us
  between operations: 15.5 us -> 0.82 us
    reduce_scatter x8 -> x0, waiting for transfers between devices: 361 us -> none  [the longest x1 106 us: shards(): lax.psum_scatter(table_terms, ('dp', 'tensor'), scatter_dimension=1, tile...]
    all_gather x8 -> x0, waiting for transfers between devices: 228 us -> none  [the longest x4 146 us: gather_rows(): return lax.all_gather(values, 'tensor', axis=0, tiled=True)]
    dot_general x41 -> x0, matrix products: 210 us -> none  [the longest x4 46.5 us: attention_advance(): jnp.einsum('qhd,khd->hqk', grad_heads, split_heads(value_seq), preferred_...]
    pallas_call x0 -> x2, Pallas kernels: none -> 171 us  [the longest x1 164 us: fast_shards(): pl.pallas_call(functools.partial(layer_kernel, dims), in_specs=[vmem] * 6...]
    all_gather x3 -> x0, blocking collectives: 154 us -> none  [the longest x1 69.5 us: shards(): lax.all_gather(norm_gains, ('dp', 'tensor'), axis=1, tiled=True)]
    unnamed x18 -> x0, waiting for transfers between devices: 108 us -> none
    unnamed x2 -> x0, blocking collectives: 80.8 us -> none
    dynamic_slice x54 -> x0, local copies, waits for them, and re-layouts: 66.9 us -> none  [the longest x8 18.1 us: attention_advance(): old_values = lax.dynamic_slice_in_dim(grad_values, seq_start, LEN, 0)]
  transfers between devices with their start and end apart: 17 -> 0, of which waited for: 14 -> 0; matrix products, arithmetic and copies ran while one was open for 7% -> 0% of each run, Pallas kernels for 0% -> 0%
where the time goes in v3:
time: 172 us
  Pallas kernels  171 us (99%)
    pallas_call x1, Pallas kernels, fast_shards(): pl.pallas_call(functools.partial(layer_kernel, dims), in_specs=[vmem] * 6...  164 us
    pallas_call x1, Pallas kernels, fast_shards(): pl.pallas_call(functools.partial(finish_kernel, NC * NY, len(large)), in_...  6.45 us

profile of v3, /device:TPU:0, one launch (start us, length us, event | category | flops | bytes accessed | tf_op | source)
XLA Modules:
  0.0 171.6 jit_solution(2681471739447188674)
XLA Ops:
  0.6 164.3 %layer.1 = (f32[48,1536]{1,0:T(8,128)}, f32[48,1536]{1,0:T(8,128)}, f32[48,384]{1,0:T(8,128)}, f32[3,48,384]{2,1,0:T(8,128)}, f32[16,128]{1,0:T(8,128)}, /*index...) custom-call(s32[1,32]{1,0:T(1,128)} %bitcast.14, ...), custom_call_target="tpu_custom_call" | custom-call | tf_op jit(solution)/shard_map/layer/pallas_call | solution.py:1283
  165.0 6.4 %finish.1 = (f32[2,24]{1,0:T(2,128)}, f32[5,24]{1,0:T(8,128)}, f32[1,24]{1,0:T(1,128)}, f32[1,96]{1,0:T(1,128)}, f32[24,1000]{1,0:T(8,128)}, /*index=5*/f32[1024...) custom-call(s32[1,32]{1,0:T(1,128)} %bitcast.15, ...), custom_call_target="tpu_custom_call" | custom-call | tf_op jit(solution)/shard_map/finish/pallas_call | solution.py:1353

commit v4 on v3

--- a/solution.py
+++ b/solution.py
@@ -413,11 +413,42 @@
         self.start(step + 1)
 
     count = 4
+    order = (7, 3, 4, 5, 6, 0, 1, 2)
 
     def drain(self):
         for step in range(self.count):
             for sem, src, _, peer in self.steps(step):
                 remote(self.view(*src), self.view(*src), self.send, self.recv, sem, peer).wait_send()
+
+
+class PlaneGather(Gather):
+    order = (10, 0, 1, 8, 9, 2, 4, 6)
+
+    def view(self, y, z, x, c, part=2):
+        start, size = self.cols
+        if part < 2:
+            start, size = start + part * (size // 2), size // 2
+        return self.buf.at[y, z, x, c, :, pl.ds(start, size)]
+
+    def steps(self, step):
+        y, z, x, c = self.pos
+        both, every = pl.ds(0, 2), pl.ds(0, NZ)
+        x_peer, y_peer = device_at(y, z, 1 - x, c), device_at(1 - y, z, x, c)
+        if step == 0:
+            return [(0, (y, z, x, c, 0), (y, z, 1 - x, c, 0), x_peer), (1, (y, z, x, c, 1), (1 - y, z, x, c, 1), y_peer)]
+        if step == 1:
+            found = []
+            for k in range(1, NZ):
+                peer, other = device_at(y, lax.rem(z + k, NZ), x, c), lax.rem(z + NZ - k, NZ)
+                found.append((2 * k, (y, z, both, c, 0), (y, other, both, c, 0), peer))
+                found.append((2 * k + 1, (both, z, x, c, 1), (both, other, x, c, 1), peer))
+            return found
+        if step == 2:
+            return [
+                (8, (y, every, both, c, 0), (1 - y, every, both, c, 0), y_peer),
+                (9, (both, every, x, c, 1), (both, every, 1 - x, c, 1), x_peer),
+            ]
+        return [(10, (both, every, both, c), (both, every, both, 1 - c), device_at(y, z, x, 1 - c))]
 
 
 class SmallGather(Gather):
@@ -552,9 +583,9 @@
 
 
 class Scatter:
-    def __init__(self, source, own, bufs, send, recv, pos, loaded):
+    def __init__(self, source, own, bufs, send, recv, pos, order):
         self.source, self.own, self.bufs = source, own, bufs
-        self.send, self.recv, self.pos, self.loaded = send, recv, pos, loaded
+        self.send, self.recv, self.pos, self.order = send, recv, pos, order
 
     def copies(self, step):
         y, z, x, c = self.pos
@@ -562,14 +593,18 @@
         own = self.own
         lo, hi, both = pl.ds(0, 2), pl.ds(2, 2), pl.ds(0, 2)
         x_peer, y_peer = device_at(y, z, 1 - x, c), device_at(1 - y, z, x, c)
+        sem = self.order
         if step == 0:
-            return [(0, self.source.at[both, pl.ds(0, NZ), both, 1 - c], first, device_at(y, z, x, 1 - c))]
+            return [(sem[0], self.source.at[both, pl.ds(0, NZ), both, 1 - c], first, device_at(y, z, x, 1 - c))]
         if step == 1:
-            return [(1, own.at[both, lo, 1 - x], second_x, x_peer), (2, own.at[1 - y, hi, both], second_y, y_peer)]
+            return [
+                (sem[1], own.at[both, lo, 1 - x], second_x, x_peer),
+                (sem[2], own.at[1 - y, hi, both], second_y, y_peer),
+            ]
         if step == 2:
-            return [(3, own.at[1 - y, lo, x], third_y, y_peer), (4, own.at[y, hi, 1 - x], third_x, x_peer)]
+            return [(sem[3], own.at[1 - y, lo, x], third_y, y_peer), (sem[4], own.at[y, hi, 1 - x], third_x, x_peer)]
         return [
-            (4 + k, own.at[y, lax.rem(z + k, NZ), x], last.at[k - 1], device_at(y, lax.rem(z + k, NZ), x, c))
+            (sem[4 + k], own.at[y, lax.rem(z + k, NZ), x], last.at[k - 1], device_at(y, lax.rem(z + k, NZ), x, c))
             for k in range(1, NZ)
         ]
 
@@ -601,8 +636,7 @@
 
             def body(i):
                 iy, iz, ix = i // (NZ * NX), lax.rem(i // NX, NZ), lax.rem(i, NX)
-                mine = own[iy, iz, ix] if self.loaded else source[iy, iz, ix, c]
-                own[iy, iz, ix] = plus(mine, first[iy, iz, ix])
+                own[iy, iz, ix] = plus(source[iy, iz, ix, c], first[iy, iz, ix])
 
             each(NY * NZ * NX, body)
         elif step == 1:
@@ -621,11 +655,17 @@
 
             each(2, body)
 
+    def first_sum(self):
+        self.wait(0)
+        self.add(0)
+        self.sent(0)
+
     def next(self, step):
-        self.wait(step)
-        self.add(step)
         if step == 0:
-            self.sent(0)
+            self.first_sum()
+        else:
+            self.wait(step)
+            self.add(step)
         self.start(step + 1)
 
     def sent(self, step):
@@ -671,15 +711,14 @@
     upw_in,
     downw_t,
     cot_in,
+    gpack_out,
     gup_out,
     gdown_out,
     gout_out,
     gqkv_out,
-    gpack_out,
     gtok_out,
     layer_out,
     middle_hbm,
-    grads_hbm,
     small_out,
     lse_out,
     ghid_out,
@@ -706,6 +745,10 @@
     acc,
     inner,
     sums,
+    gup,
+    gdown,
+    gout,
+    gqkv,
     *rest,
 ):
     rows, width, per, half, ffh, ft = dims
@@ -724,12 +767,17 @@
         col[f"g{i}"] = pl.ds(i * 384, 384)
     for i in range(n_ff):
         col[f"m{i}"] = pl.ds(4 * half + 2 * ft * i, 2 * ft)
-    flow = {}
-    for i, name in enumerate(names):
-        if name in col:
-            flow[name] = Gather(full, col[name], send.at[i], recv.at[i], pos)
+    flow, used = {}, 0
+    for name in names:
+        count = {"pack": 10, "hid": 10, "m1": 11}.get(name, 8)
+        sems = (send.at[pl.ds(used, count)], recv.at[pl.ds(used, count)], pos)
+        used += count
+        if name == "m1":
+            flow[name] = PlaneGather(full, (4 * half + 2 * ft, 2 * ft), *sems)
+        elif name in col:
+            flow[name] = Gather(full, col[name], *sems)
         else:
-            flow[name] = SmallGather({"pack": pack, "hid": lines}[name], send.at[i], recv.at[i], pos)
+            flow[name] = SmallGather({"pack": pack, "hid": lines}[name], *sems)
     ready = greet(pos)
     copies = {}
 
@@ -816,6 +864,7 @@
     flow["g1"].next(1)
     flow["g2"].next(0)
     launch("m0")
+    launch("m1")
 
     def whole(cols, size):
         return jnp.concatenate([full[by, :, :, :, :, cols].reshape(width, size) for by in range(NY)], axis=1)
@@ -852,9 +901,9 @@
         1: [then("g1", 2), then("g2", 1), then("o", 0), then("hid", 0)],
         3: [then("g2", 2), then("o", 1)],
         4: [then("m0", 1)],
-        5: [then("o", 2), then("m1", 0), off("m2")],
+        5: [then("o", 2)],
     }
-    between = {1: [then("m0", 0), off("m1")]}
+    between = {1: [then("m0", 0), then("m1", 0)]}
 
     def attend(s, _):
         group, by = s // NY, lax.rem(s, NY)
@@ -888,6 +937,7 @@
 
     lax.fori_loop(0, width // 128, attend, 0)
     flow["o"].wait(3)
+    launch("m2")
     flow["hid"].wait(1)
     for bz in range(NZ):
         for bx in range(NX):
@@ -896,12 +946,19 @@
                 at = ((bz * NX + bx) * n_hid + j) * 128
                 hid[0:1, at : at + 128] = total[j : j + 1]
 
+    at = len(copies)
+
+    def middle_save(i):
+        rb = row_block(i, 256)
+        return pltpu.make_async_copy(result.at[rb], middle_hbm.at[rb], local.at[at + 10 + i])
+
     def second_norm(i, _):
         at_step(i, {2: [then("m0", 2)]})
         rb = row_block(i, 256)
         start_h = tokens[rb, :].astype(F32) + embed
         value = start_h + (nt(mixed[rb, :], whole(col["o"], half)) + small_out[5:6, :])
         result[rb, :] = value
+        middle_save(i).start()
         gsec[rb, :] = jnp.zeros_like(value)
         xhat, _ = moments(value)
         block = (xhat * small_out[1:2, :] + small_out[7:8, :]).astype(BF16)
@@ -910,11 +967,10 @@
         return 0
 
     lax.fori_loop(0, rows // 256, second_norm, 0)
-    copy("middle", result, middle_hbm)
     flow["m1"].next(1)
     flow["m0"].wait(3)
-    copies["middle"].wait()
-    at = len(copies)
+    for i in range(rows // 256):
+        middle_save(i).wait()
 
     free = 4 * half
     half_f = 2 * ft
@@ -922,32 +978,21 @@
     for g in range(n_groups):
         places[f"q{g}"] = (g % 2, free + 2 * half_f + 384 * (g // 2), 384)
     sums_of = {}
+    before = {"m0": "g0", "m1": "g1", "m2": "g2", "o": "o", "q0": "m0", "q1": "m2", "q2": "m1", "pack": "pack", "hid": "hid"}
     for i, name in enumerate([*places, "pack", "hid"]):
-        sems = (send.at[len(names) + i], recv.at[len(names) + i], pos)
+        gather = flow[before[name]]
+        sems = (gather.send, gather.recv, pos)
         if name in places:
             core, start, size = places[name]
             own_view = full.at[:, :, :, core, :, pl.ds(start, size)]
             bufs = rest[6 * i : 6 * i + 6]
             if name[0] == "m":
-                source = grads_hbm.at[:, :, :, :, :, pl.ds(half_f * i, half_f)]
+                source = gtile
             else:
                 source = gtile.at[:, :, :, :, :, pl.ds(0 if name in ("o", "q1") else half, 384)]
-            sums_of[name] = Scatter(source, own_view, bufs, *sems, name[0] == "m")
+            sums_of[name] = Scatter(source, own_view, bufs, *sems, gather.order)
         else:
             sums_of[name] = SmallScatter(*(rest[-11:-7] if name == "pack" else rest[-7:-3]), *sems)
-    loads = {
-        name: pltpu.make_async_copy(sums_of[name].source.at[:, :, :, c], sums_of[name].own, local.at[at + 2 + i])
-        for i, name in enumerate(["m0", "m1", "m2"])
-    }
-
-    def tile_copy(t, slot):
-        ty, tm = lax.rem(t, NY), t // NY
-        return pltpu.make_async_copy(
-            gtile.at[slot],
-            grads_hbm.at[ty, :, :, :, :, pl.ds(pl.multiple_of(tm * 2 * ft, 128), 2 * ft)],
-            local.at[at + slot],
-        )
-
     tiles = NY * n_ff
 
     def tile(t, _):
@@ -955,28 +1000,20 @@
         slot = lax.rem(t, 2)
 
         def begin(name):
-            loads[name].start()
-            sums_of[name].start(0)
+            return lambda: sums_of[name].start(0)
 
         def first_sum(name):
-            loads[name].wait()
-            sums_of[name].next(0)
-
-        def reuse():
-            tile_copy(t - 2, slot).wait()
-
-        def reuse_both():
-            tile_copy(t - 2, slot).wait()
-            tile_copy(t - 1, 1 - slot).wait()
+            return lambda: sums_of[name].first_sum()
+
+        def second_step(name):
+            return lambda: sums_of[name].start(1)
 
         at_step(
             t,
             {
                 1: [then("m2", 0)],
-                2: [flow["m0"].drain, reuse_both, lambda: begin("m0"), then("m2", 1), arrived("m1")],
-                3: [lambda: first_sum("m0")],
-                4: [reuse_both, lambda: begin("m1"), arrived("m2")],
-                5: [back("m0", 1), lambda: first_sum("m1")],
+                2: [flow["g0"].drain, begin("m0"), flow["m0"].drain, then("m2", 1), arrived("m1")],
+                4: [flow["g1"].drain, begin("m1"), arrived("m2")],
             },
         )
 
@@ -1005,22 +1042,27 @@
             layer_save.start()
             middle_load.start()
 
-        at_step(t, {1: [then("m1", 2)], 3: [then("m2", 2)], tiles - 1: [results]})
+        at_step(
+            t,
+            {
+                1: [then("m1", 2)],
+                2: [first_sum("m0")],
+                3: [then("m2", 2), second_step("m0")],
+                4: [first_sum("m1"), second_step("m1")],
+                tiles - 1: [results, back("m0", 1)],
+            },
+        )
 
         turn = (NZ, NX, NC, per, ft)
         gtile[slot, :, :, :, :, 0:ft] = nn(second_t[...], gpre[...]).astype(BF16).reshape(turn)
         gtile[slot, :, :, :, :, ft : 2 * ft] = nn(cot_t[...], act[...]).astype(BF16).reshape(turn)
-        tile_copy(t, slot).start()
         return 0
 
     layer_save = pltpu.make_async_copy(second, layer_out, local.at[at + 5])
     middle_load = pltpu.make_async_copy(middle_hbm, result, local.at[at + 6])
     lax.fori_loop(0, tiles, tile, 0)
-    flow["m1"].drain()
-    flow["m2"].drain()
-    tile_copy(tiles - 2, 0).wait()
-    tile_copy(tiles - 1, 1).wait()
-    loads["m2"].start()
+    for name in ("g2", "m1", "m2", "hid"):
+        flow[name].drain()
     sums_of["m2"].start(0)
     reload = [
         pltpu.make_async_copy(tokens_in.at[:, pl.ds(0, ft)], act, local.at[at + 7]),
@@ -1066,17 +1108,20 @@
         ]
         return jnp.concatenate(picks, axis=1)
 
-    for by in range(NY):
-        def out_grad(i, _):
-            rb = row_block(i, 384)
-            part = nn(gattn_t[rb, :], mixed[:, by * half : by * half + half]).astype(BF16)
-            gtile[by, pl.ds(i * 2, 2), :, :, :, 0:half] = part.reshape(2, NX, NC, per, half)
-            return 0
-
-        lax.fori_loop(0, width // 384, out_grad, 0)
+    flow["pack"].drain()
+    flow["o"].drain()
+    sums_of["m1"].next(1)
+    sums_of["m2"].next(0)
+
+    def out_grad(i, _):
+        part = nn(gattn_t[row_block(i, 384), :], mixed[...]).astype(BF16)
+        for by in range(NY):
+            to = part[:, by * half : by * half + half].reshape(2, NX, NC, per, half)
+            gtile[by, pl.ds(i * 2, 2), :, :, :, 0:half] = to
+        return 0
+
+    lax.fori_loop(0, width // 384, out_grad, 0)
     sums_of["o"].start(0)
-    loads["m2"].wait()
-    sums_of["m2"].next(0)
     sums_of["m0"].next(2)
 
     def mixed_grad(i, _):
@@ -1085,7 +1130,6 @@
         return 0
 
     lax.fori_loop(0, rows // 512, mixed_grad, 0)
-    sums_of["m1"].next(1)
     sums_of["o"].next(0)
 
     def turn_normed(i, _):
@@ -1095,10 +1139,11 @@
 
     lax.fori_loop(0, rows // 256, turn_normed, 0)
     events_back = {
-        2: [back("m1", 2)],
-        3: [back("q0", 0), back("m2", 1)],
-        4: [back("o", 1), back("m2", 2), sums_of["hid"].next],
-        5: [back("q1", 0), back("q0", 1)],
+        1: [back("m1", 2)],
+        2: [back("m2", 1)],
+        3: [back("q0", 0), back("o", 1), sums_of["hid"].next],
+        4: [back("m2", 2), back("q0", 1)],
+        5: [back("o", 2), back("q0", 2), back("q1", 0)],
     }
 
     def attend_back(s, _):
@@ -1146,13 +1191,25 @@
                     to = pl.ds(pl.multiple_of(offset + piece * 128, 128), 128)
                     gtile[b, :, :, :, :, to] = part[:, b * 128 : b * 128 + 128].reshape(NZ, NX, NC, per, 128)
             at_step(group, {g: [lambda g=g: sums_of[f"q{g}"].start(0)] for g in range(n_groups)})
+            at_step(group, {n_groups - 1: [back("q1", 1)]})
 
         return 0
 
     lax.fori_loop(0, NY * n_groups, attend_back, 0)
-    sums_of["o"].next(2)
     for load in reload:
         load.wait()
+
+    def m_final(i):
+        def run():
+            total = sums_of[f"m{i}"].final()
+            gup[:, ft * i : ft * i + ft] = total[:, 0:ft]
+            gdown[:, ft * i : ft * i + ft] = total[:, ft:]
+
+        return run
+
+    owners = {}
+    for i, (name, src, dst) in enumerate([("gup", gup, gup_out), ("gdown", gdown, gdown_out), ("gout", gout, gout_out), ("gqkv", gqkv, gqkv_out)]):
+        owners[name] = pltpu.make_async_copy(src, dst, local.at[at + 14 + i])
 
     def first_back(i, totals):
         rb = row_block(i, 256)
@@ -1165,7 +1222,7 @@
 
         at_step(
             i,
-            {0: [back("q0", 2)], 1: [back("q1", 1), back("q2", 0)], 2: [back("q1", 2)], 3: [back("q2", 1)]},
+            {0: [back("q2", 0)], 1: [m_final(0), back("q1", 2)], 2: [back("q2", 1), m_final(1)]},
         )
         return (
             totals[0] + sum_rows_of(grad * xhat),
@@ -1187,24 +1244,35 @@
     for d, (by, bz, bx, bc) in blocks():
         sums_of["pack"].source[by, bz, bx, bc] = fold(turned[d * share : d * share + share])
     sums_of["pack"].start(0)
-    sums_of["q2"].next(2)
-    for i in range(n_ff):
-        total = sums_of[f"m{i}"].final()
-        gup_out[:, ft * i : ft * i + ft] = total[:, 0:ft]
-        gdown_out[:, ft * i : ft * i + ft] = total[:, ft:]
+    last = f"q{n_groups - 1}"
+    sums_of[last].next(2)
+    for i in range(2, n_ff):
+        m_final(i)()
+    owners["gup"].start()
+    owners["gdown"].start()
     sums_of["pack"].next()
-    gout_out[...] = sums_of["o"].final()
+    gout[...] = sums_of["o"].final()
+    owners["gout"].start()
     gpack_out[8:16] = sums_of["hid"].final()
-    for g in range(n_groups):
+
+    def qkv_final(g):
         total = sums_of[f"q{g}"].final()
         for piece in range(3):
-            gqkv_out[piece, :, 128 * g : 128 * g + 128] = total[:, 128 * piece : 128 * piece + 128]
+            gqkv[piece, :, 128 * g : 128 * g + 128] = total[:, 128 * piece : 128 * piece + 128]
+
+    for g in range(n_groups - 1):
+        qkv_final(g)
+    for name, each in sums_of.items():
+        if name not in ("pack", last):
+            each.drain()
+    qkv_final(n_groups - 1)
+    owners["gqkv"].start()
     gpack_out[0:8] = sums_of["pack"].final()
     gtok.wait()
-    for name in ["pack", "hid", *groups, "o"]:
-        flow[name].drain()
-    for each in sums_of.values():
-        each.drain()
+    sums_of[last].drain()
+    sums_of["pack"].drain()
+    for each in owners.values():
+        each.wait()
 
 
 def finish_kernel(slots, count, steps, gpack, *refs):
@@ -1236,14 +1304,14 @@
     for k in range(1, slots):
         value = jnp.where(slot == k, line[:, hshare * k : hshare * k + hshare], value)
     hidden_out[...] = value
+    for load, save in pieces:
+        load.wait()
+        save.start()
     n_steps, n_seq = table_out.shape[1], steps.shape[1]
     picked = (steps[...] == lax.broadcasted_iota(jnp.int32, (n_steps, n_seq), 0)).astype(F32)
     table_out[...] = lax.dot_general(
         features[:, 8 : 8 + n_seq], picked, (((1,), (1,)), ((), ())), precision=HIGH, preferred_element_type=F32
     )
-    for load, save in pieces:
-        load.wait()
-        save.start()
     for _, save in pieces:
         save.wait()
 
@@ -1279,21 +1347,18 @@
     scratch = []
     for cols in chunks:
         scratch += scatter_scratch(per, cols, BF16)
-    n_flows = 3 + n_groups + n_ff + len(chunks) + 2
-    gup, gdown, gout, gqkv, gpack, gtok, layer, _, _ = pl.pallas_call(
+    n_sems = 2 * 10 + 8 * (n_groups + n_ff) + 11
+    owned = [shape((per, ffh), F32), shape((per, ffh), F32), shape((per, half), F32), shape((3, per, half), F32)]
+    gpack, gup, gdown, gout, gqkv, gtok, layer, _ = pl.pallas_call(
         functools.partial(layer_kernel, dims),
         in_specs=[vmem] * 6 + [anywhere] * 6,
-        out_specs=[vmem] * 5 + [anywhere] * 4,
+        out_specs=[vmem] + [anywhere] * 7,
         out_shape=[
-            shape((per, ffh), F32),
-            shape((per, ffh), F32),
-            shape((per, half), F32),
-            shape((3, per, half), F32),
             shape((16, 128), F32),
+            *owned,
             wide,
             low,
             wide,
-            shape((NY, NZ, NX, NC, per, 2 * ffh), BF16),
         ],
         scratch_shapes=[
             vm((128, width), F32),
@@ -1322,12 +1387,13 @@
             vm((rows, 128), F32),
             vm((8, rows), F32),
             vm((128, width), F32),
+            *[vm(each.shape, F32) for each in owned],
             *scratch,
             *small_scratch(),
             *small_scratch(),
-            pltpu.SemaphoreType.DMA((n_flows, 10)),
-            pltpu.SemaphoreType.DMA((n_flows, 10)),
-            pltpu.SemaphoreType.DMA((14 + 3 * n_groups + 2 * n_ff,)),
+            pltpu.SemaphoreType.DMA((n_sems,)),
+            pltpu.SemaphoreType.DMA((n_sems,)),
+            pltpu.SemaphoreType.DMA((24 + 3 * n_groups + 2 * n_ff,)),
         ],
         compiler_params=pltpu.CompilerParams(collective_id=0, has_side_effects=True, vmem_limit_bytes=VMEM_LIMIT),
         name="layer",

time: 172 us -> 165 us (0.959)
  Pallas kernels: 171 us -> 164 us
    pallas_call x1, Pallas kernels: 164 us -> 158 us  [fast_shards(): pl.pallas_call(functools.partial(layer_kernel, dims), in_specs=[vmem] * 6...]
where the time goes in v4:
time: 165 us
  Pallas kernels  164 us (99%)
    pallas_call x1, Pallas kernels, fast_shards(): pl.pallas_call(functools.partial(layer_kernel, dims), in_specs=[vmem] * 6...  158 us
    pallas_call x1, Pallas kernels, fast_shards(): pl.pallas_call(functools.partial(finish_kernel, NC * NY, len(large)), in_...  6.22 us

profile of v4, /device:TPU:0, one launch (start us, length us, event | category | flops | bytes accessed | tf_op | source)
XLA Modules:
  0.0 165.1 jit_solution(13099859281574127401)
XLA Ops:
  0.6 158.0 %layer.1 = (f32[16,128]{1,0:T(8,128)}, f32[48,1536]{1,0:T(8,128)}, f32[48,1536]{1,0:T(8,128)}, f32[48,384]{1,0:T(8,128)}, f32[3,48,384]{2,1,0:T(8,128)}, /*index...) custom-call(s32[1,32]{1,0:T(1,128)} %bitcast.14, bf16[2,24]{1,0:T(2,128)(2,1)} %gains.1, ...), custom_call_target="tpu_custom_call" | custom-call | tf_op jit(solution)/shard_map/layer/pallas_call | solution.py:1352
  158.7 6.2 %finish.1 = (f32[2,24]{1,0:T(2,128)}, f32[5,24]{1,0:T(8,128)}, f32[1,24]{1,0:T(1,128)}, f32[1,96]{1,0:T(1,128)}, f32[24,1000]{1,0:T(8,128)}, /*index=5*/f32[1024...) custom-call(s32[1,32]{1,0:T(1,128)} %bitcast.15, ...), custom_call_target="tpu_custom_call" | custom-call | tf_op jit(solution)/shard_map/finish/pallas_call | solution.py:1419

commit v5 on v4

--- a/solution.py
+++ b/solution.py
@@ -338,6 +338,13 @@
     return (z * (NX * NC) + x * NC + c, y)
 
 
+def across(z, k):
+    return {1: z + 1 - 2 * lax.rem(z, 2), 2: lax.rem(z + 2, NZ), 3: NZ - 1 - z}[k]
+
+
+FAR_FIRST = (3, 2, 1)
+
+
 def plane_peers(pos):
     y, z, x, c = pos
     for flip in range(1, NY * NX * NC):
@@ -347,7 +354,7 @@
 
 def greet(pos):
     y, z, x, c = pos
-    peers = [device_at(y, lax.rem(z + k, NZ), x, c) for k in range(1, NZ)]
+    peers = [device_at(y, across(z, k), x, c) for k in FAR_FIRST]
     peers += [device_at(*to) for _, to in plane_peers(pos)]
     barrier = pltpu.get_barrier_semaphore()
     for peer in peers:
@@ -387,8 +394,7 @@
         lo, hi, both = pl.ds(0, 2), pl.ds(2, 2), pl.ds(0, 2)
         if step == 0:
             return [
-                (k - 1, (y, z, x, c), (y, lax.rem(z + NZ - k, NZ), x, c), device_at(y, lax.rem(z + k, NZ), x, c))
-                for k in range(1, NZ)
+                (k - 1, (y, z, x, c), (y, across(z, k), x, c), device_at(y, across(z, k), x, c)) for k in FAR_FIRST
             ]
         x_peer, y_peer = device_at(y, z, 1 - x, c), device_at(1 - y, z, x, c)
         if step == 1:
@@ -438,8 +444,8 @@
             return [(0, (y, z, x, c, 0), (y, z, 1 - x, c, 0), x_peer), (1, (y, z, x, c, 1), (1 - y, z, x, c, 1), y_peer)]
         if step == 1:
             found = []
-            for k in range(1, NZ):
-                peer, other = device_at(y, lax.rem(z + k, NZ), x, c), lax.rem(z + NZ - k, NZ)
+            for k in FAR_FIRST:
+                peer, other = device_at(y, across(z, k), x, c), across(z, k)
                 found.append((2 * k, (y, z, both, c, 0), (y, other, both, c, 0), peer))
                 found.append((2 * k + 1, (both, z, x, c, 1), (both, other, x, c, 1), peer))
             return found
@@ -492,14 +498,14 @@
             ]
         return [
             remote(
-                self.acc.at[lax.rem(z + k, NZ)],
+                self.acc.at[across(z, k)],
                 self.last.at[k - 1],
                 self.send,
                 self.recv,
                 k - 1,
-                device_at(y, lax.rem(z + k, NZ), x, c),
+                device_at(y, across(z, k), x, c),
             )
-            for k in range(1, NZ)
+            for k in FAR_FIRST
         ]
 
     def start(self, step):
@@ -517,8 +523,9 @@
 
     def final(self):
         total = self.acc[self.pos[1]]
-        for k, copy in enumerate(self.copies(1)):
+        for copy in self.copies(1):
             copy.wait_recv()
+        for k in range(NZ - 1):
             total = total + self.last[k]
         return total
 
@@ -604,8 +611,8 @@
         if step == 2:
             return [(sem[3], own.at[1 - y, lo, x], third_y, y_peer), (sem[4], own.at[y, hi, 1 - x], third_x, x_peer)]
         return [
-            (sem[4 + k], own.at[y, lax.rem(z + k, NZ), x], last.at[k - 1], device_at(y, lax.rem(z + k, NZ), x, c))
-            for k in range(1, NZ)
+            (sem[4 + k], own.at[y, across(z, k), x], last.at[k - 1], device_at(y, across(z, k), x, c))
+            for k in FAR_FIRST
         ]
 
     def start(self, step):
@@ -903,7 +910,7 @@
         4: [then("m0", 1)],
         5: [then("o", 2)],
     }
-    between = {1: [then("m0", 0), then("m1", 0)]}
+    between = {1: [then("m0", 0)]}
 
     def attend(s, _):
         group, by = s // NY, lax.rem(s, NY)
@@ -911,6 +918,7 @@
 
         @pl.when(by == 0)
         def _():
+            at_step(group, {1: [then("m1", 0)]})
             at_step(group, {g: [arrived(f"g{g}")] for g in range(n_groups)})
             project(group)
             at_step(group, between)
@@ -1218,7 +1226,7 @@
         q_rows, k_rows, v_rows = gq[rb, :], gk[rb, :], gv[rb, :]
         grad = nt(q_rows, weight(0)) + nt(k_rows, weight(1)) + nt(v_rows, weight(2))
         total = gsec[rb, :] + norm_back(xhat, scale, grad * small_out[0:1, :])
-        result[rb, :] = total
+        mixed[rb, :] = total.astype(BF16)
 
         at_step(
             i,
@@ -1238,7 +1246,7 @@
     sums[3:4, :] = q_sum
     sums[4:5, :] = v_sum
     sums[pl.ds(8 + me, 1), :] = seq_sum
-    gtok = pltpu.make_async_copy(result, gtok_out, local.at[at + 9])
+    gtok = pltpu.make_async_copy(mixed, gtok_out, local.at[at + 9])
     gtok.start()
     turned = sums[...].T
     for d, (by, bz, bx, bc) in blocks():
@@ -1277,20 +1285,18 @@
 
 def finish_kernel(slots, count, steps, gpack, *refs):
     large, (gains_out, biases_out, shift_out, hidden_out, table_out) = refs[:count], refs[count : count + 5]
-    outs, bufs, (load_sem, save_sem) = refs[count + 5 : 2 * count + 5], refs[2 * count + 5 : 3 * count + 5], refs[-2:]
+    outs, rest = refs[count + 5 : 2 * count + 5], refs[2 * count + 5 :]
+    bufs, wide, (load_sem, save_sem) = rest[:count], rest[count], rest[-2:]
     pieces = []
     for src, buf, out in zip(large, bufs, outs):
         cut = 4 if src.shape[0] % 512 == 0 else 1
         size = src.shape[0] // cut
         for k in range(cut):
             at, n = pl.ds(k * size, size), len(pieces)
-            pieces.append(
-                (
-                    pltpu.make_async_copy(src.at[at], buf.at[at], load_sem.at[n]),
-                    pltpu.make_async_copy(buf.at[at], out.at[at], save_sem.at[n]),
-                )
-            )
-    for load, _ in pieces:
+            held = buf if src.dtype == out.dtype else wide
+            load = pltpu.make_async_copy(src.at[at], buf.at[at], load_sem.at[n])
+            pieces.append((load, pltpu.make_async_copy(held.at[at], out.at[at], save_sem.at[n]), held is wide and at))
+    for load, _, _ in pieces:
         load.start()
     share, hshare = gains_out.shape[1], hidden_out.shape[1]
     features = unfold(gpack[0:8, :])
@@ -1304,15 +1310,17 @@
     for k in range(1, slots):
         value = jnp.where(slot == k, line[:, hshare * k : hshare * k + hshare], value)
     hidden_out[...] = value
-    for load, save in pieces:
+    for load, save, at in pieces:
         load.wait()
+        if at:
+            wide[at, :] = bufs[0][at, :].astype(F32)
         save.start()
     n_steps, n_seq = table_out.shape[1], steps.shape[1]
     picked = (steps[...] == lax.broadcasted_iota(jnp.int32, (n_steps, n_seq), 0)).astype(F32)
     table_out[...] = lax.dot_general(
         features[:, 8 : 8 + n_seq], picked, (((1,), (1,)), ((), ())), precision=HIGH, preferred_element_type=F32
     )
-    for _, save in pieces:
+    for _, save, _ in pieces:
         save.wait()
 
 
@@ -1356,7 +1364,7 @@
         out_shape=[
             shape((16, 128), F32),
             *owned,
-            wide,
+            low,
             low,
             wide,
         ],
@@ -1415,13 +1423,15 @@
     large = (gtok, layer, gqkv, gout, gup, gdown)
     pieces = sum(4 if array.shape[0] % 512 == 0 else 1 for array in large)
     small_shapes = [(2, share), (5, share), (1, share), (1, hshare), (share, n_steps)]
-    large_shapes = [shape(array.shape, array.dtype) for array in large]
+    large_shapes = [wide, *[shape(array.shape, array.dtype) for array in large[1:]]]
     grad_gains, grad_biases, grad_shift, grad_hidden, grad_table, gtok, layer, gqkv, gout, gup, gdown = pl.pallas_call(
         functools.partial(finish_kernel, NC * NY, len(large)),
         in_specs=[vmem] * 2 + [anywhere] * len(large),
         out_specs=[vmem] * 5 + [anywhere] * len(large),
         out_shape=[shape(dims, F32) for dims in small_shapes] + large_shapes,
-        scratch_shapes=[vm(array.shape, array.dtype) for array in large] + [pltpu.SemaphoreType.DMA((pieces,))] * 2,
+        scratch_shapes=[vm(array.shape, array.dtype) for array in large]
+        + [vm(wide.shape, F32)]
+        + [pltpu.SemaphoreType.DMA((pieces,))] * 2,
         name="finish",
     )(steps, gpack, *large)
     return (

time: 165 us -> 161 us (0.976)
  Pallas kernels: 164 us -> 160 us
    pallas_call x1, Pallas kernels: 158 us -> 155 us  [fast_shards(): pl.pallas_call(functools.partial(layer_kernel, dims), in_specs=[vmem] * 6...]
where the time goes in v5:
time: 161 us; the launch traced here: 160 us
  Pallas kernels  160 us (99%)
    pallas_call x1, Pallas kernels, fast_shards(): pl.pallas_call(functools.partial(layer_kernel, dims), in_specs=[vmem] * 6...  155 us
    pallas_call x1, Pallas kernels, fast_shards(): pl.pallas_call(functools.partial(finish_kernel, NC * NY, len(large)), in_...  5.07 us

profile of v5, /device:TPU:0, one launch (start us, length us, event | category | flops | bytes accessed | tf_op | source)
XLA Modules:
  0.0 160.5 jit_solution(5515103340304176290)
XLA Ops:
  0.6 154.6 %layer.1 = (f32[16,128]{1,0:T(8,128)}, f32[48,1536]{1,0:T(8,128)}, f32[48,1536]{1,0:T(8,128)}, f32[48,384]{1,0:T(8,128)}, f32[3,48,384]{2,1,0:T(8,128)}, /*index...) custom-call(s32[1,32]{1,0:T(1,128)} %bitcast.14, bf16[2,24]{1,0:T(2,128)(2,1)} %gains.1, ...), custom_call_target="tpu_custom_call" | custom-call | tf_op jit(solution)/shard_map/layer/pallas_call | solution.py:1360
  155.3 5.1 %finish.1 = (f32[2,24]{1,0:T(2,128)}, f32[5,24]{1,0:T(8,128)}, f32[1,24]{1,0:T(1,128)}, f32[1,96]{1,0:T(1,128)}, f32[24,1000]{1,0:T(8,128)}, /*index=5*/f32[1024...) custom-call(s32[1,32]{1,0:T(1,128)} %bitcast.15, ...), custom_call_target="tpu_custom_call" | custom-call | tf_op jit(solution)/shard_map/finish/pallas_call | solution.py:1427

commit v6 on v5

--- a/solution.py
+++ b/solution.py
@@ -1148,10 +1148,9 @@
     lax.fori_loop(0, rows // 256, turn_normed, 0)
     events_back = {
         1: [back("m1", 2)],
-        2: [back("m2", 1)],
-        3: [back("q0", 0), back("o", 1), sums_of["hid"].next],
-        4: [back("m2", 2), back("q0", 1)],
-        5: [back("o", 2), back("q0", 2), back("q1", 0)],
+        3: [back("m2", 1), back("q0", 0), back("o", 1), sums_of["hid"].next],
+        4: [back("m2", 2)],
+        5: [back("q0", 1), back("o", 2), back("q1", 0)],
     }
 
     def attend_back(s, _):
@@ -1199,7 +1198,7 @@
                     to = pl.ds(pl.multiple_of(offset + piece * 128, 128), 128)
                     gtile[b, :, :, :, :, to] = part[:, b * 128 : b * 128 + 128].reshape(NZ, NX, NC, per, 128)
             at_step(group, {g: [lambda g=g: sums_of[f"q{g}"].start(0)] for g in range(n_groups)})
-            at_step(group, {n_groups - 1: [back("q1", 1)]})
+            at_step(group, {n_groups - 1: [back("q0", 2), back("q1", 1)]})
 
         return 0
 

time: 161 us -> 159 us (0.988)
  Pallas kernels: 160 us -> 158 us
where the time goes in v6:
time: 159 us
  Pallas kernels  158 us (99%)
    pallas_call x1, Pallas kernels, fast_shards(): pl.pallas_call(functools.partial(layer_kernel, dims), in_specs=[vmem] * 6...  153 us
    pallas_call x1, Pallas kernels, fast_shards(): pl.pallas_call(functools.partial(finish_kernel, NC * NY, len(large)), in_...  5.07 us

profile of v6, /device:TPU:0, one launch (start us, length us, event | category | flops | bytes accessed | tf_op | source)
XLA Modules:
  0.0 158.9 jit_solution(7548088418490816634)
XLA Ops:
  0.6 153.0 %layer.1 = (f32[16,128]{1,0:T(8,128)}, f32[48,1536]{1,0:T(8,128)}, f32[48,1536]{1,0:T(8,128)}, f32[48,384]{1,0:T(8,128)}, f32[3,48,384]{2,1,0:T(8,128)}, /*index...) custom-call(s32[1,32]{1,0:T(1,128)} %bitcast.14, bf16[2,24]{1,0:T(2,128)(2,1)} %gains.1, ...), custom_call_target="tpu_custom_call" | custom-call | tf_op jit(solution)/shard_map/layer/pallas_call | solution.py:1359
  153.7 5.1 %finish.1 = (f32[2,24]{1,0:T(2,128)}, f32[5,24]{1,0:T(8,128)}, f32[1,24]{1,0:T(1,128)}, f32[1,96]{1,0:T(1,128)}, f32[24,1000]{1,0:T(8,128)}, /*index=5*/f32[1024...) custom-call(s32[1,32]{1,0:T(1,128)} %bitcast.15, ...), custom_call_target="tpu_custom_call" | custom-call | tf_op jit(solution)/shard_map/finish/pallas_call | solution.py:1426
